TPU v7x, 256 devices: a whole 4x4x8 slice. The times are simulated.
256 devices in a mesh: term: 8 (over x, z_lo), sector: 32 (over z_hi, y, core).
Axes of the slice: x: 4, y: 4, z: 8 (z_hi: 4, z_lo: 2; z = z_hi * 2 + z_lo), core: 2. Of those that a mesh axis runs over, the one named last changes fastest.
Arguments:
- psi_start: bfloat16 [256, 256, 256], P('sector'), may hold values from -6 to 6
- left_env: bfloat16 [24, 256, 256, 256], P('term', 'sector')
- right_env: bfloat16 [24, 256, 256, 256], P('term', 'sector')
- connect: int32 [24, 256], P('term', 'sector'), may hold values from 0 to 255, as said below
- sector_dims: int32 [2, 256], P(None, 'sector'), may hold values from 64 to 256
- precond: bfloat16 [256, 256, 256], P('sector'), may hold values from 0.5 to 4
Outputs:
- projected: float32 [3, 3], replicated
- last_vector: float32 [256, 256, 256], P('sector', 'term')
- new_env: bfloat16 [24, 256, 256, 256], P('term', 'sector')
Inputs may be any that keep to these rules, and one draw needn't show every extreme that they name: connect[t, s] differs from s by at most 8.
All inputs are finite; a program needn't handle non-finite values.
Results may differ from a plain program's by a relative error of at most 0.012.
Values may be sent and summed in bfloat16 or wider, within the bound.
No kernel may reach another device: no remote copies, remote signals or barrier semaphores. Data moves between devices by JAX's collectives and lax.ppermute only.
A program may use at most 128 MiB of HBM per device.

v0:
```python
import jax
import jax.numpy as jnp
from jax import lax
from jax.sharding import PartitionSpec as P

epsilon = 1e-06


def from_everyone(x, axis):
    devices = lax.axis_size(axis)
    return lax.all_to_all(jnp.broadcast_to(x[None], (devices, *x.shape)), axis, 0, 0, tiled=True)


def over_copies(x, axis):
    return from_everyone(x, axis).sum(axis=0)


def with_halo(block, sides, width):
    for axis, dim in sides:
        count = lax.axis_size(axis)
        forward = [(i, i + 1) for i in range(count - 1)]
        backward = [(target, source) for source, target in forward]
        low = lax.ppermute(
            lax.slice_in_dim(block, block.shape[dim] - width, None, axis=dim), axis, forward
        )
        high = lax.ppermute(lax.slice_in_dim(block, 0, width, axis=dim), axis, backward)
        block = jnp.concatenate([low, block, high], axis=dim)
    return block


def on_device(psi_start, left_env, right_env, connect, sector_dims, precond):
    blocks = psi_start.shape[0]
    width = psi_start.shape[1]
    devices = lax.axis_size("sector")
    pieces = lax.axis_size("term")
    terms_here = left_env.shape[0]
    entries = float(blocks * devices * width * width)
    local_source = connect - (lax.axis_index("sector") * blocks - blocks)
    share = width // pieces
    share_start = lax.axis_index("term") * share
    row_ids = lax.broadcasted_iota(jnp.int32, (blocks, width, width), 1)
    col_ids = lax.broadcasted_iota(jnp.int32, (blocks, width, width), 2)
    keep = (row_ids < sector_dims[0][:, None, None]) & (col_ids < sector_dims[1][:, None, None])
    mask = keep.astype(jnp.float32)
    start_rows = psi_start.astype(jnp.float32) * mask
    divisor = precond.astype(jnp.float32)

    def totals(values):
        stacked = jnp.stack(values)
        summed = over_copies(stacked, "sector")
        return summed / entries

    norm_start = totals([jnp.sum(start_rows * start_rows)])[0]
    basis = [start_rows / jnp.sqrt(norm_start + epsilon)]
    sigmas = []
    env_list = []
    for which in range(3):
        vector_b = basis[which].astype(jnp.bfloat16)
        extended = with_halo(vector_b, (("sector", 0),), blocks)
        with_env = which == 2
        total = jnp.zeros((blocks, width, width), jnp.float32)
        own_blocks = extended[blocks : 2 * blocks]
        envs = []
        for apply_which in range(terms_here):
            source = jnp.take(extended, local_source[apply_which], axis=0)
            half = jnp.einsum(
                "sij,sjk->sik", left_env[apply_which], source, preferred_element_type=jnp.float32
            ).astype(jnp.bfloat16)
            total = total + jnp.einsum(
                "sik,slk->sil", half, right_env[apply_which], preferred_element_type=jnp.float32
            )
            if with_env:
                env_one = jnp.einsum(
                    "sji,sjk->sik", own_blocks, half, preferred_element_type=jnp.float32
                ) * width ** (-0.5)
                envs.append(env_one.astype(jnp.bfloat16))
        sigma = lax.psum(total, "term")
        sigma, env_list = (sigma * mask, envs)
        sigmas.append(sigma)
        if which < 2:
            theta = totals([jnp.sum(basis[which] * sigma)])[0]
            corr = (sigma - theta * basis[which]) / divisor
            correlations = totals([jnp.sum(member * corr) for member in basis])
            for position in range(len(basis)):
                corr = corr - correlations[position] * basis[position]
            length = totals([jnp.sum(corr * corr)])[0]
            basis.append(corr / jnp.sqrt(length + epsilon))
    products = totals([jnp.sum(basis[row] * sigmas[col]) for row in range(3) for col in range(3)])
    projected = products.reshape(3, 3)
    last_vector = lax.dynamic_slice_in_dim(basis[2], share_start, share, 1)
    return (projected, last_vector, jnp.stack(env_list))


def solution(mesh):
    placed = (
        P("sector", None, None),
        P("term", "sector", None, None),
        P("term", "sector", None, None),
        P("term", "sector"),
        P(None, "sector"),
        P("sector", None, None),
    )
    return jax.shard_map(
        on_device,
        mesh=mesh,
        in_specs=placed,
        out_specs=(P(), P("sector", "term", None), P("term", "sector", None, None)),
        check_vma=False,
    )
```

profile of v0, /device:TPU:1, one launch (start us, length us, event | category | flops | bytes accessed | tf_op | source)
XLA Modules:
  0.0 686.7 jit_solution(12341208729224850788)
XLA Ops:
  11.1 21.9 %all_to_all.48 = f32[32,1,1]{2,1,0:T(1,128)S(1)} all-to-all(f32[32,1,1]{2,1,0:T(1,128)S(1)} %broadcast_in_dim.25), channel_id=1, replica_groups=mesh['term'=8,'sector'=32] {'sector'}, dimensions={0} | all-to-all | bytes 256 | tf_op jit(solution)/shard_map/all_to_all | solution.py:11
  40.9 9.7 %collective-permute-done = bf16[8,256,256]{2,1,0:T(8,128)(2,1)S(1)} collective-permute-done((bf16[8,256,256]{2,1,0:T(8,128)(2,1)S(1)}, bf16[8,256,256]{2,1,0:T(8,128)(2,1)S(1)}, u32[]{:S(2)}, u32[]{:S(2)}) %collective-permute-start) | collective-permute-done | bytes 1048608 | tf_op jit(solution)/shard_map/ppermute | solution.py:23
  50.6 4.4 collective-permute-done.1
  56.8 3.5 gather_fusion.1
  69.1 4.0 fusion.2
  73.1 4.4 add_add_fusion.2
  77.6 121.0 %all-reduce.4.cloned.1.call-done = f32[8,256,256]{2,1,0:T(8,128)} async-done(((f32[8,256,256]{2,1,0:T(8,128)}), f32[8,256,256]{2,1,0:T(8,128)}) %all-reduce.4.cloned.1.call-update) | async-done | bytes 2097168 | tf_op jit(solution)/shard_map/psum | solution.py:77
  202.2 18.8 %all_to_all.49 = f32[32,1,1]{2,1,0:T(1,128)S(1)} all-to-all(f32[32,1,1]{2,1,0:T(1,128)S(1)} %broadcast_in_dim.26), channel_id=1, replica_groups=mesh['term'=8,'sector'=32] {'sector'}, dimensions={0} | all-to-all | bytes 256 | tf_op jit(solution)/shard_map/all_to_all | solution.py:11
  225.8 12.7 %all_to_all.50 = f32[32,1,1]{2,1,0:T(1,128)S(1)} all-to-all(f32[32,1,1]{2,1,0:T(1,128)S(1)} %broadcast_in_dim.27), channel_id=1, replica_groups=mesh['term'=8,'sector'=32] {'sector'}, dimensions={0} | all-to-all | bytes 256 | tf_op jit(solution)/shard_map/all_to_all | solution.py:11
  239.8 3.6 multiply_reduce_fusion.11
  244.1 12.8 %all_to_all.51 = f32[32,1,1]{2,1,0:T(1,128)S(1)} all-to-all(f32[32,1,1]{2,1,0:T(1,128)S(1)} %broadcast_in_dim.28), channel_id=1, replica_groups=mesh['term'=8,'sector'=32] {'sector'}, dimensions={0} | all-to-all | bytes 256 | tf_op jit(solution)/shard_map/all_to_all | solution.py:11
  263.2 9.6 %collective-permute-done.2 = bf16[8,256,256]{2,1,0:T(8,128)(2,1)S(1)} collective-permute-done((bf16[8,256,256]{2,1,0:T(8,128)(2,1)S(1)}, bf16[8,256,256]{2,1,0:T(8,128)(2,1)S(1)}, u32[]{:S(2)}, u32[]{:S(2)}) %collective-permute-start.2) | collective-permute-done | bytes 1048608 | tf_op jit(solution)/shard_map/ppermute | solution.py:23
  272.8 4.4 collective-permute-done.3
  279.1 3.5 gather_fusion.4
  286.1 3.5 gather_fusion.5
  289.6 4.0 fusion.5
  293.6 4.0 fusion.4
  297.6 5.4 add_add_fusion.1
  303.0 119.3 %all-reduce.6.cloned.1.call-done = f32[8,256,256]{2,1,0:T(8,128)} async-done(((f32[8,256,256]{2,1,0:T(8,128)}), f32[8,256,256]{2,1,0:T(8,128)}) %all-reduce.6.cloned.1.call-update) | async-done | bytes 2097168 | tf_op jit(solution)/shard_map/psum | solution.py:77
  425.8 18.8 %all_to_all.52 = f32[32,1,1]{2,1,0:T(1,128)S(1)} all-to-all(f32[32,1,1]{2,1,0:T(1,128)S(1)} %broadcast_in_dim.29), channel_id=1, replica_groups=mesh['term'=8,'sector'=32] {'sector'}, dimensions={0} | all-to-all | bytes 256 | tf_op jit(solution)/shard_map/all_to_all | solution.py:11
  445.8 3.8 multiply_reduce_fusion.8
  451.0 12.7 %all_to_all.53 = f32[32,1,2]{2,1,0:T(1,128)S(1)} all-to-all(f32[32,1,2]{2,1,0:T(1,128)S(1)} %broadcast_in_dim.30), channel_id=1, replica_groups=mesh['term'=8,'sector'=32] {'sector'}, dimensions={0} | all-to-all | bytes 512 | tf_op jit(solution)/shard_map/all_to_all | solution.py:11
  464.4 6.4 multiply_reduce_fusion.6
  471.5 12.8 %all_to_all.54 = f32[32,1,1]{2,1,0:T(1,128)S(1)} all-to-all(f32[32,1,1]{2,1,0:T(1,128)S(1)} %broadcast_in_dim.31), channel_id=1, replica_groups=mesh['term'=8,'sector'=32] {'sector'}, dimensions={0} | all-to-all | bytes 256 | tf_op jit(solution)/shard_map/all_to_all | solution.py:11
  493.6 9.6 %collective-permute-done.4 = bf16[8,256,256]{2,1,0:T(8,128)(2,1)S(1)} collective-permute-done((bf16[8,256,256]{2,1,0:T(8,128)(2,1)S(1)}, bf16[8,256,256]{2,1,0:T(8,128)(2,1)S(1)}, u32[]{:S(2)}, u32[]{:S(2)}) %collective-permute-start.4) | collective-permute-done | bytes 1048608 | tf_op jit(solution)/shard_map/ppermute | solution.py:23
  503.2 4.4 collective-permute-done.5
  537.8 111.4 %all-reduce.8.cloned.1.call-done = f32[8,256,256]{2,1,0:T(8,128)} async-done(((f32[8,256,256]{2,1,0:T(8,128)}), f32[8,256,256]{2,1,0:T(8,128)}) %all-reduce.8.cloned.1.call-update) | async-done | bytes 2097168 | tf_op jit(solution)/shard_map/psum | solution.py:77
  649.3 4.9 multiply_reduce_fusion
  654.1 5.7 stack.63
  660.4 9.6 %all-to-all-start.7 = ((f32[32,1,9]{2,1,0:T(1,128)}), f32[32,1,9]{2,1,0:T(1,128)S(1)}, u32[]{:S(2)}, u32[]{:S(2)}) async-start(f32[32,1,9]{2,1,0:T(1,128)} %broadcast_in_dim.58), calls=%async_computation.7 | async-start | bytes 32768 | tf_op jit(solution)/shard_map/all_to_all | solution.py:11
  670.0 3.9 pad_maximum_fusion.3
  673.9 5.5 all-to-all-done.7
  (91 shorter events, 88.5 us)
Async XLA Ops:
  7.2 33.6 %copy-start.12 = (s32[3,8]{1,0:T(4,128)S(1)}, s32[3,8]{1,0:T(4,128)}, u32[]{:S(2)}) copy-start(s32[3,8]{1,0:T(4,128)} %param.11) | copy-start | bytes 292
  7.2 191.4 %all-reduce.4.cloned.1.call-start = ((), (), s32[]{:S(2)}) async-start(), calls=%async_computation.8 | async-start | bytes 4194304 | tf_op jit(solution)/shard_map/psum | solution.py:77
  36.2 14.4 %collective-permute-start = (bf16[8,256,256]{2,1,0:T(8,128)(2,1)S(1)}, bf16[8,256,256]{2,1,0:T(8,128)(2,1)S(1)}, u32[]{:S(2)}, u32[]{:S(2)}) collective-permute-start(bf16[8,256,256]{2,1,0:T(8,128)(2,1)S(1)} %fusion.119), channel_id=1, source_target_pairs={{0,1},{1,2},{2,3},{3,4},{4,5},{5,6},{6,7},{7,8},{8,9},{9,10},{10,1... | collective-permute-start | bytes 3145736 | tf_op jit(solution)/shard_map/ppermute | solution.py:23
  38.9 16.1 %collective-permute-start.1 = (bf16[8,256,256]{2,1,0:T(8,128)(2,1)S(1)}, bf16[8,256,256]{2,1,0:T(8,128)(2,1)S(1)}, u32[]{:S(2)}, u32[]{:S(2)}) collective-permute-start(bf16[8,256,256]{2,1,0:T(8,128)(2,1)S(1)} %fusion.119), channel_id=1, source_target_pairs={{1,0},{2,1},{3,2},{4,3},{5,4},{6,5},{7,6},{8,7},{9,8},{10,9},{11,1... | collective-permute-start | bytes 3145736 | tf_op jit(solution)/shard_map/ppermute | solution.py:26
  77.5 121.1 %copy-start = (bf16[8,256,256]{2,1,0:T(8,128)(2,1)S(1)}, bf16[8,256,256]{2,1,0:T(8,128)(2,1)}, u32[]{:S(2)}) copy-start(bf16[8,256,256]{2,1,0:T(8,128)(2,1)} %param.8) | copy-start | bytes 3145732
  77.5 344.8 %all-reduce.6.cloned.1.call-start = ((), (), s32[]{:S(2)}) async-start(), calls=%async_computation.9 | async-start | bytes 4194304 | tf_op jit(solution)/shard_map/psum | solution.py:77
  198.6 23.8 %copy-start.1 = (f32[8,256,256]{2,1,0:T(8,128)S(1)}, f32[8,256,256]{2,1,0:T(8,128)}, u32[]{:S(2)}) copy-start(f32[8,256,256]{2,1,0:T(8,128)} %all-reduce.4.cloned.1.call-done) | copy-start | bytes 6291460
  258.4 14.5 %collective-permute-start.2 = (bf16[8,256,256]{2,1,0:T(8,128)(2,1)S(1)}, bf16[8,256,256]{2,1,0:T(8,128)(2,1)S(1)}, u32[]{:S(2)}, u32[]{:S(2)}) collective-permute-start(bf16[8,256,256]{2,1,0:T(8,128)(2,1)S(1)} %fusion.120), channel_id=1, source_target_pairs={{0,1},{1,2},{2,3},{3,4},{4,5},{5,6},{6,7},{7,8},{8,9},{9,10},{10,1... | collective-permute-start | bytes 3145736 | tf_op jit(solution)/shard_map/ppermute | solution.py:23
  261.1 16.1 %collective-permute-start.3 = (bf16[8,256,256]{2,1,0:T(8,128)(2,1)S(1)}, bf16[8,256,256]{2,1,0:T(8,128)(2,1)S(1)}, u32[]{:S(2)}, u32[]{:S(2)}) collective-permute-start(bf16[8,256,256]{2,1,0:T(8,128)(2,1)S(1)} %fusion.120), channel_id=1, source_target_pairs={{1,0},{2,1},{3,2},{4,3},{5,4},{6,5},{7,6},{8,7},{9,8},{10,9},{11,1... | collective-permute-start | bytes 3145736 | tf_op jit(solution)/shard_map/ppermute | solution.py:26
  303.0 346.3 %all-reduce.8.cloned.1.call-start = ((), (), s32[]{:S(2)}) async-start(), calls=%async_computation.10 | async-start | bytes 4194304 | tf_op jit(solution)/shard_map/psum | solution.py:77
  488.8 18.9 %copy-start.2 = (bf16[8,256,256]{2,1,0:T(8,128)(2,1)}, bf16[8,256,256]{2,1,0:T(8,128)(2,1)S(1)}, u32[]{:S(2)}) copy-start(bf16[8,256,256]{2,1,0:T(8,128)(2,1)S(1)} %get-tuple-element.13) | copy-start | bytes 3145732
  488.8 14.5 %collective-permute-start.4 = (bf16[8,256,256]{2,1,0:T(8,128)(2,1)S(1)}, bf16[8,256,256]{2,1,0:T(8,128)(2,1)S(1)}, u32[]{:S(2)}, u32[]{:S(2)}) collective-permute-start(bf16[8,256,256]{2,1,0:T(8,128)(2,1)S(1)} %get-tuple-element.13), channel_id=1, source_target_pairs={{0,1},{1,2},{2,3},{3,4},{4,5},{5,6},{6,7},{7,8},{8,9},{9,10},{10,1... | collective-permute-start | bytes 3145736 | tf_op jit(solution)/shard_map/ppermute | solution.py:23
  491.5 16.1 %collective-permute-start.5 = (bf16[8,256,256]{2,1,0:T(8,128)(2,1)S(1)}, bf16[8,256,256]{2,1,0:T(8,128)(2,1)S(1)}, u32[]{:S(2)}, u32[]{:S(2)}) collective-permute-start(bf16[8,256,256]{2,1,0:T(8,128)(2,1)S(1)} %get-tuple-element.13), channel_id=1, source_target_pairs={{1,0},{2,1},{3,2},{4,3},{5,4},{6,5},{7,6},{8,7},{9,8},{10,9},{11,1... | collective-permute-start | bytes 3145736 | tf_op jit(solution)/shard_map/ppermute | solution.py:26
  519.9 2.5 copy-start.10
  522.4 5.0 copy-start.5
  522.4 2.2 copy-start.11
  524.7 2.8 copy-start.6
  524.7 2.3 copy-start.4
  527.0 1.0 copy-start.8
  529.9 5.0 copy-start.3
  529.9 4.9 copy-start.7
  534.9 1.5 copy-start.9
  660.4 19.0 %all-to-all-start.7 = ((f32[32,1,9]{2,1,0:T(1,128)}), f32[32,1,9]{2,1,0:T(1,128)S(1)}, u32[]{:S(2)}, u32[]{:S(2)}) async-start(f32[32,1,9]{2,1,0:T(1,128)} %broadcast_in_dim.58), calls=%async_computation.7 | async-start | bytes 32768 | tf_op jit(solution)/shard_map/all_to_all | solution.py:11
Sparse Core Ops, SparseCore 0:
  77.6 120.8 all-reduce.3
  303.1 119.2 all-reduce.5
  530.0 119.2 all-reduce.7
where the time goes:
time: 688 us; the launch traced here: 687 us
  waiting for transfers between devices  399 us (58%)
  blocking collectives  111 us (16%)
  other arithmetic  49.7 us (7%)
  local copies, waits for them, and re-layouts  46.4 us (7%)
  matrix products  38.5 us (6%)
  starting transfers between devices  24.1 us (4%)
  between operations  18.1 us (3%)
    psum x3, waiting for transfers between devices, on_device(): sigma = lax.psum(total, 'term')  352 us
    all_to_all x7, blocking collectives, from_everyone(): lax.all_to_all(jnp.broadcast_to(x[None], (devices, *x.shape)), axis, 0, 0...  111 us
    gather x9, local copies, waits for them, and re-layouts, on_device(): source = jnp.take(extended, local_source[apply_which], axis=0)  30.5 us
    ppermute x3, waiting for transfers between devices, with_halo(): lax.ppermute(lax.slice_in_dim(block, block.shape[dim] - width, None, axis...  28.9 us
    dot_general x9, matrix products, on_device(): jnp.einsum('sik,slk->sil', half, right_env[apply_which], preferred_elemen...  27.4 us
  transfers between devices with their start and end apart: 10, of which 10 were waited for; matrix products, arithmetic and copies ran while one was open for 2% of the time, Pallas kernels for 0%

commit v1 on v0

v1 whole, which is shorter than its diff:
```python
import jax
import jax.numpy as jnp
from jax import lax
from jax.experimental import pallas as pl
from jax.experimental.pallas import tpu as pltpu
from jax.sharding import PartitionSpec as P

epsilon = 1e-06
f32 = jnp.float32
bf16 = jnp.bfloat16


def to_everyone(x, axis):
    devices = lax.axis_size(axis)
    return lax.all_to_all(jnp.broadcast_to(x[None], (devices, *x.shape)), axis, 0, 0, tiled=True)


def neighbours(block):
    count = lax.axis_size("sector")
    forward = [(i, i + 1) for i in range(count - 1)]
    backward = [(i + 1, i) for i in range(count - 1)]
    return lax.ppermute(block, "sector", forward), lax.ppermute(block, "sector", backward)


def row_of(total_ref, entries):
    return jnp.sum(total_ref[...], axis=0, keepdims=True) * (1.0 / entries)


def one(row, k):
    return row[:, k : k + 1]


def first_scale(row0):
    return 1.0 / jnp.sqrt(one(row0, 0) + epsilon)


def second_weights(row0, row1):
    inv = first_scale(row0)
    theta = inv * one(row1, 0)
    a = inv * one(row1, 1)
    b = inv * inv * one(row1, 2)
    aa = one(row1, 3)
    ab = inv * one(row1, 4)
    bb = inv * inv * one(row1, 5)
    vv = inv * inv * one(row0, 0)
    o = a - theta * b
    length = aa + theta * theta * bb + o * o * vv - 2.0 * theta * ab - 2.0 * o * a + 2.0 * theta * o * b
    r = 1.0 / jnp.sqrt(jnp.maximum(length, 0.0) + epsilon)
    return r, -r * theta * inv, -r * o * inv


def third_weights(row0, row2):
    inv = first_scale(row0)
    theta = one(row2, 0)
    v1a = inv * one(row2, 1)
    v1b = inv * one(row2, 2)
    v2a = one(row2, 3)
    v2b = one(row2, 4)
    aa = one(row2, 5)
    ab = one(row2, 6)
    bb = one(row2, 7)
    v1v2 = inv * one(row2, 8)
    v2v2 = one(row2, 9)
    v1v1 = inv * inv * one(row0, 0)
    o1 = v1a - theta * v1b
    o2 = v2a - theta * v2b
    length = (
        aa
        - 2.0 * theta * ab
        + theta * theta * bb
        - 2.0 * o1 * o1
        - 2.0 * o2 * o2
        + o1 * o1 * v1v1
        + 2.0 * o1 * o2 * v1v2
        + o2 * o2 * v2v2
    )
    r = 1.0 / jnp.sqrt(jnp.maximum(length, 0.0) + epsilon)
    return r, -r * theta, -r * o1 * inv, -r * o2


def whole(ref, s):
    block = ref[:, s]
    return block.reshape(block.shape[0] * block.shape[1], block.shape[2]).astype(f32)


def fold(x):
    return jnp.sum(x.reshape(x.shape[0] // 8, 8, x.shape[1]), axis=0)


def row_from(sums):
    lane = lax.broadcasted_iota(jnp.int32, (1, 128), 1)
    row = jnp.zeros((1, 128), f32)
    for k, total in enumerate(sums):
        row = row + jnp.where(lane == k, jnp.sum(total), 0.0)
    return row


def keep_of(dims_ref, s, width):
    rows = lax.broadcasted_iota(jnp.int32, (width, width), 0)
    cols = lax.broadcasted_iota(jnp.int32, (width, width), 1)
    return (rows < dims_ref[0, s]) & (cols < dims_ref[1, s])


def start_kernel(dims_ref, psi_ref, out_ref, row_ref):
    blocks, width = psi_ref.shape[0], psi_ref.shape[1]

    def body(s, acc):
        x = jnp.where(keep_of(dims_ref, s, width), psi_ref[s].astype(f32), 0.0)
        out_ref[s] = x.astype(bf16)
        return acc + fold(x * x)

    acc = lax.fori_loop(0, blocks, body, jnp.zeros((8, width), f32))
    row_ref[...] = row_from([acc])


def gram1_kernel(sig_ref, psi_ref, d_ref, row_ref):
    blocks, width = psi_ref.shape[0], psi_ref.shape[1]

    def body(s, acc):
        sig = whole(sig_ref, s)
        psi = psi_ref[s].astype(f32)
        rd = 1.0 / d_ref[s].astype(f32)
        a, b = sig * rd, psi * rd
        terms = (psi * sig, psi * a, psi * b, a * a, a * b, b * b)
        return tuple(t + fold(x) for t, x in zip(acc, terms))

    acc = lax.fori_loop(0, blocks, body, (jnp.zeros((8, width), f32),) * 6)
    row_ref[...] = row_from(acc)


def gram2_kernel(entries, tot0, tot1, sig2_ref, sig1_ref, psi_ref, d_ref, row_ref):
    blocks, width = psi_ref.shape[0], psi_ref.shape[1]
    p, q, w = second_weights(row_of(tot0, entries), row_of(tot1, entries))

    def body(s, acc):
        sig2, sig1 = whole(sig2_ref, s), whole(sig1_ref, s)
        psi = psi_ref[s].astype(f32)
        rd = 1.0 / d_ref[s].astype(f32)
        v2 = (p * sig1 + q * psi) * rd + w * psi
        a, b = sig2 * rd, v2 * rd
        terms = (
            v2 * sig2,
            psi * a,
            psi * b,
            v2 * a,
            v2 * b,
            a * a,
            a * b,
            b * b,
            psi * v2,
            v2 * v2,
            psi * sig2,
            v2 * sig1,
        )
        return tuple(t + fold(x) for t, x in zip(acc, terms))

    acc = lax.fori_loop(0, blocks, body, (jnp.zeros((8, width), f32),) * 12)
    row_ref[...] = row_from(acc)


def dot(a, b, ca, cb):
    return lax.dot_general(a, b, (((ca,), (cb,)), ((), ())), preferred_element_type=f32)


def product_kernel(stage, entries, *refs):
    conn_ref, dims_ref = refs[:2]
    refs = refs[2:]
    tots, refs = refs[:stage], refs[stage:]
    psi, refs = refs[:3], refs[3:]
    d = sig1 = sig2 = (None, None, None)
    if stage > 1:
        d, sig1, refs = refs[:3], refs[3:6], refs[6:]
    if stage > 2:
        sig2, refs = refs[:3], refs[3:]
    left_ref, right_ref = refs[:2]
    if stage < 3:
        out_ref, vb_ref = refs[2:]
    else:
        env_ref, last_ref, row_ref, vb_ref, acc_ref = refs[2:]
    step = pl.program_id(0)
    blocks, width = psi[0].shape[0], psi[0].shape[1]
    rows = [row_of(t, entries) for t in tots]

    def vectors(seg, s):
        x = psi[seg][s].astype(f32)
        inv = first_scale(rows[0])
        if stage == 1:
            return [x * inv], [], x
        p, q, w = second_weights(rows[0], rows[1])
        rd = 1.0 / d[seg][s].astype(f32)
        s1 = whole(sig1[seg], s)
        v2 = (p * s1 + q * x) * rd + w * x
        if stage == 2:
            return [x * inv, v2], [s1], x
        p, q, w, y = third_weights(rows[0], rows[2])
        s2 = whole(sig2[seg], s)
        v3 = (p * s2 + q * v2) * rd + w * x + y * v2
        return [x * inv, v2, v3], [s1, s2], x

    @pl.when(step == 0)
    def _():
        for seg in range(3):

            def body(s, carry, seg=seg):
                vb_ref[seg * blocks + s] = vectors(seg, s)[0][-1].astype(bf16)
                return carry

            lax.fori_loop(0, blocks, body, 0)
        if stage == 3:
            acc_ref[...] = jnp.zeros_like(acc_ref)

    total = jnp.zeros((width, width), f32)
    if stage == 3:
        own = vb_ref[blocks + step]
        own_t = own.T
    for t in range(left_ref.shape[0]):
        half = dot(left_ref[t, 0], vb_ref[conn_ref[t, step]], 1, 0).astype(bf16)
        total = total + dot(half, right_ref[t, 0], 1, 1)
        if stage == 3:
            env_ref[t, 0] = (dot(own_t, half, 1, 0) * width ** (-0.5)).astype(bf16)
    if stage < 3:
        total = jnp.where(keep_of(dims_ref, step, width), total, 0.0).astype(bf16)
        out_ref[:, 0] = total.reshape(out_ref.shape[0], out_ref.shape[2], width)
    else:
        vs, sigs, _ = vectors(1, step)
        pieces = sig1[1].shape[0]
        share = width // pieces
        last_ref[0] = vs[2].reshape(pieces, share, width)
        terms = (vs[0] * total, vs[1] * total, vs[2] * total, vs[2] * sigs[0], vs[2] * sigs[1])
        for k, x in enumerate(terms):
            acc_ref[k] += fold(x)

        @pl.when(step == blocks - 1)
        def _():
            row_ref[...] = row_from([acc_ref[k] for k in range(5)])


def product(stage, entries, pieces, conn, dims, tots, vectors, left, right):
    terms, blocks, width = left.shape[:3]
    share = width // pieces
    smem = pl.BlockSpec(memory_space=pltpu.SMEM)
    vmem = pl.BlockSpec(memory_space=pltpu.VMEM)
    env_spec = pl.BlockSpec((terms, 1, width, width), lambda s: (0, s, 0, 0))
    scratch = [pltpu.VMEM((3 * blocks, width, width), bf16)]
    if stage < 3:
        out_shape = jax.ShapeDtypeStruct((pieces, blocks, share, width), bf16)
        out_specs = pl.BlockSpec((pieces, 1, share, width), lambda s: (0, s, 0, 0))
    else:
        out_shape = (
            jax.ShapeDtypeStruct(left.shape, bf16),
            jax.ShapeDtypeStruct((blocks, pieces, share, width), f32),
            jax.ShapeDtypeStruct((1, 128), f32),
        )
        out_specs = (
            env_spec,
            pl.BlockSpec((1, pieces, share, width), lambda s: (s, 0, 0, 0)),
            pl.BlockSpec((1, 128), lambda s: (0, 0)),
        )
        scratch.append(pltpu.VMEM((5, 8, width), f32))
    return pl.pallas_call(
        lambda *refs: product_kernel(stage, entries, *refs),
        grid=(blocks,),
        in_specs=[smem, smem] + [vmem] * (len(tots) + len(vectors)) + [env_spec, env_spec],
        out_specs=out_specs,
        out_shape=out_shape,
        scratch_shapes=scratch,
        name=f"product_{stage}",
        compiler_params=pltpu.CompilerParams(vmem_limit_bytes=48 << 20),
    )(conn, dims, *tots, *vectors, left, right)


def call_small(kernel, dims, arrays, out_shape, name):
    smem = pl.BlockSpec(memory_space=pltpu.SMEM)
    vmem = pl.BlockSpec(memory_space=pltpu.VMEM)
    return pl.pallas_call(
        kernel,
        in_specs=[smem] * len(dims) + [vmem] * len(arrays),
        out_specs=jax.tree.map(lambda _: vmem, out_shape),
        out_shape=out_shape,
        name=name,
        compiler_params=pltpu.CompilerParams(vmem_limit_bytes=32 << 20),
    )(*dims, *arrays)


def on_device(psi_start, left_env, right_env, connect, sector_dims, precond):
    blocks, width = psi_start.shape[:2]
    devices = lax.axis_size("sector")
    pieces = lax.axis_size("term")
    share = width // pieces
    entries = float(blocks * devices * width * width)
    conn = connect - (lax.axis_index("sector") * blocks - blocks)
    row = jax.ShapeDtypeStruct((1, 128), f32)

    def totals(values):
        return to_everyone(values[0], "sector")

    def gathered(partial):
        arrived = lax.all_to_all(partial, "term", 0, 0, tiled=True)
        mine = arrived.astype(f32).sum(axis=0).astype(bf16)
        return to_everyone(mine, "term")

    psi, row0 = call_small(
        start_kernel, [sector_dims], [psi_start], (jax.ShapeDtypeStruct(psi_start.shape, bf16), row), "start"
    )
    psi_low, psi_high = neighbours(psi)
    tot0 = totals(row0)
    d_low, d_high = neighbours(precond)
    psis = (psi_low, psi, psi_high)
    ds = (d_low, precond, d_high)
    args = (left_env, right_env)

    part1 = product(1, entries, pieces, conn, sector_dims, (tot0,), psis, *args)
    sig1 = gathered(part1)
    low, high = neighbours(sig1)
    row1 = call_small(gram1_kernel, [], [sig1, psi, precond], row, "gram_1")
    tot1 = totals(row1)
    sig1s = (low, sig1, high)

    part2 = product(2, entries, pieces, conn, sector_dims, (tot0, tot1), (*psis, *ds, *sig1s), *args)
    sig2 = gathered(part2)
    low, high = neighbours(sig2)
    row2 = call_small(
        lambda *refs: gram2_kernel(entries, *refs), [], [tot0, tot1, sig2, sig1, psi, precond], row, "gram_2"
    )
    tot2 = totals(row2)
    sig2s = (low, sig2, high)

    env, last, row3 = product(
        3, entries, pieces, conn, sector_dims, (tot0, tot1, tot2), (*psis, *ds, *sig1s, *sig2s), *args
    )
    lane = lax.broadcasted_iota(jnp.int32, (1, 128), 1)
    row3 = jnp.where(lane < 3, row3, row3 / pieces)
    by_term = to_everyone(row3[0], "term").sum(axis=0)
    last_row = to_everyone(by_term, "sector").sum(axis=0) / entries
    inv = 1.0 / jnp.sqrt(tot0[:, 0].sum() / entries + epsilon)
    r1 = tot1.sum(axis=0) / entries
    r2 = tot2.sum(axis=0) / entries
    projected = jnp.stack(
        [inv * r1[0], inv * r2[10], last_row[0], r2[11], r2[0], last_row[1], last_row[3], last_row[4], last_row[2]]
    ).reshape(3, 3)
    mine = lax.dynamic_slice_in_dim(last, lax.axis_index("term"), 1, 1)
    last_vector = mine.reshape(blocks, share, width)
    return (projected, last_vector, env)


def solution(mesh):
    placed = (
        P("sector", None, None),
        P("term", "sector", None, None),
        P("term", "sector", None, None),
        P("term", "sector"),
        P(None, "sector"),
        P("sector", None, None),
    )
    return jax.shard_map(
        on_device,
        mesh=mesh,
        in_specs=placed,
        out_specs=(P(), P("sector", "term", None), P("term", "sector", None, None)),
        check_vma=False,
    )
```

time: 688 us -> 304 us (0.44)
  waiting for transfers between devices: 399 us -> 68.8 us
  Pallas kernels: 0 us -> 63.5 us
  starting transfers between devices: 24.1 us -> 84.5 us
  blocking collectives: 111 us -> 59.9 us
  other arithmetic: 49.7 us -> 4.26 us
  matrix products: 38.5 us -> 0 us
  local copies, waits for them, and re-layouts: 46.4 us -> 19 us
  between operations: 18.1 us -> 2.38 us
    psum x3 -> x0, waiting for transfers between devices: 352 us -> none  [on_device(): sigma = lax.psum(total, 'term')]
    pallas_call x0 -> x6, Pallas kernels: none -> 63.5 us  [the longest x3 56.1 us: product(): pl.pallas_call(lambda *refs: product_kernel(stage, entries, *refs), grid=...]
    all_to_all x1 -> x6, waiting for transfers between devices: 5.52 us -> 68.8 us  [to_everyone(): lax.all_to_all(jnp.broadcast_to(x[None], (devices, *x.shape)), axis, 0, 0...]
    all_to_all x7 -> x3, blocking collectives: 111 us -> 59.9 us  [the longest x2 42.9 us: gathered(): arrived = lax.all_to_all(partial, 'term', 0, 0, tiled=True)]
    all_to_all x1 -> x6, starting transfers between devices: 9.61 us -> 53.6 us  [to_everyone(): lax.all_to_all(jnp.broadcast_to(x[None], (devices, *x.shape)), axis, 0, 0...]
    ppermute x6 -> x8, waiting for transfers between devices: 42.1 us -> 0.02 us  [the longest x4 0.01 us: neighbours(): lax.ppermute(block, 'sector', backward)]
    dot_general x15 -> x0, matrix products: 38.5 us -> none  [the longest x9 27.4 us: on_device(): jnp.einsum('sik,slk->sil', half, right_env[apply_which], preferred_elemen...]
    gather x9 -> x0, local copies, waits for them, and re-layouts: 30.5 us -> none  [on_device(): source = jnp.take(extended, local_source[apply_which], axis=0)]
  transfers between devices with their start and end apart: 10 -> 14, of which waited for: 10 -> 6; matrix products, arithmetic and copies ran while one was open for 2% -> 2% of each run, Pallas kernels for 0% -> 2%
where the time goes in v1:
time: 304 us; the launch traced here: 302 us
  starting transfers between devices  84.5 us (28%)
  waiting for transfers between devices  68.8 us (23%)
  Pallas kernels  63.5 us (21%)
  blocking collectives  59.9 us (20%)
  local copies, waits for them, and re-layouts  19 us (6%)
  other arithmetic  4.26 us (1%)
    all_to_all x6, waiting for transfers between devices, to_everyone(): lax.all_to_all(jnp.broadcast_to(x[None], (devices, *x.shape)), axis, 0, 0...  68.8 us
    pallas_call x3, Pallas kernels, product(): pl.pallas_call(lambda *refs: product_kernel(stage, entries, *refs), grid=...  56.1 us
    all_to_all x6, starting transfers between devices, to_everyone(): lax.all_to_all(jnp.broadcast_to(x[None], (devices, *x.shape)), axis, 0, 0...  53.6 us
    all_to_all x2, blocking collectives, gathered(): arrived = lax.all_to_all(partial, 'term', 0, 0, tiled=True)  42.9 us
    ppermute x4, starting transfers between devices, neighbours(): lax.ppermute(block, 'sector', forward)  20.4 us
    all_to_all x1, blocking collectives, to_everyone(): lax.all_to_all(jnp.broadcast_to(x[None], (devices, *x.shape)), axis, 0, 0...  17 us
    ppermute x4, starting transfers between devices, neighbours(): lax.ppermute(block, 'sector', backward)  10.5 us
    unnamed x28, local copies, waits for them, and re-layouts  8.49 us
  transfers between devices with their start and end apart: 14, of which 6 were waited for; matrix products, arithmetic and copies ran while one was open for 2% of the time, Pallas kernels for 2%

profile of v1, /device:TPU:1, one launch (start us, length us, event | category | flops | bytes accessed | tf_op | source)
XLA Modules:
  0.0 302.4 jit_solution(9273862463657513897)
XLA Ops:
  3.7 4.6 %collective-permute-start = (bf16[8,256,256]{2,1,0:T(8,128)(2,1)S(1)}, bf16[8,256,256]{2,1,0:T(8,128)(2,1)S(1)}, u32[]{:S(2)}, u32[]{:S(2)}) collective-permute-start(bf16[8,256,256]{2,1,0:T(8,128)(2,1)S(1)} %get-tuple-element.9.refs_4_.psi_ref.refs_5_.refs_6_), channel_id=1, source_target_pairs={{0,1},{1,2},{2,3},{3,4},{4,5},{5,6},{6,7},{7,8},{8,9},{9,10},{10,1... | collective-permute-start | bytes 3145736 | tf_op jit(solution)/shard_map/ppermute | solution.py:22
  8.3 1.9 collective-permute-start.1
  10.8 13.4 %all-to-all-start = ((f32[32,1,128]{2,1,0:T(1,128)}), f32[32,1,128]{2,1,0:T(1,128)S(1)}, u32[]{:S(2)}, u32[]{:S(2)}) async-start(f32[32,1,128]{2,1,0:T(1,128)} %broadcast_in_dim.14), calls=%async_computation | async-start | bytes 32768 | tf_op jit(solution)/shard_map/all_to_all | solution.py:15
  24.9 16.0 %all-to-all-done = f32[32,1,128]{2,1,0:T(1,128)S(1)} async-done(((f32[32,1,128]{2,1,0:T(1,128)}), f32[32,1,128]{2,1,0:T(1,128)S(1)}, u32[]{:S(2)}, u32[]{:S(2)}) %all-to-all-start) | async-done | bytes 16416 | tf_op jit(solution)/shard_map/all_to_all | solution.py:15
  41.6 10.1 %product_1.1 = bf16[8,8,32,256]{3,2,1,0:T(8,128)(2,1)S(1)} custom-call(s32[3,8]{1,0:T(4,128)S(1)} %broadcast_subtract_fusion.refs_0_, s32[2,8]{1,0:T(2,128)S(1)} %copy-done.12, f32[32,128]{1,0:T(8,128)S(1)} %bitcast.17, bf16[8,256,256]{2,1,0:T(8,128)(2,1)S(1)} %collective-permute-done.refs_3_.refs_4_.refs_5_, ...), custom_call_target="tpu_custom_call" | custom-call | tf_op jit(solution)/shard_map/product_1/pallas_call | solution.py:260
  52.7 23.7 %all_to_all.56 = bf16[8,8,32,256]{3,2,1,0:T(8,128)(2,1)} all-to-all(bf16[8,8,32,256]{3,2,1,0:T(8,128)(2,1)S(1)} %product_1.1), channel_id=1, replica_groups=mesh['term'=8,'sector'=32] {'term'}, dimensions={0} | all-to-all | bytes 2097152 | tf_op jit(solution)/shard_map/all_to_all | solution.py:298
  76.4 1.4 reduce_sum.70
  78.9 3.6 %all-to-all-start.2 = ((bf16[8,8,32,256]{3,2,1,0:T(8,128)(2,1)}), bf16[8,8,32,256]{3,2,1,0:T(8,128)(2,1)S(1)}, u32[]{:S(2)}, u32[]{:S(2)}) async-start(bf16[8,8,32,256]{3,2,1,0:T(8,128)(2,1)} %broadcast_in_dim.15), calls=%async_computation.2 | async-start | bytes 2097152 | tf_op jit(solution)/shard_map/all_to_all | solution.py:15
  82.5 4.9 %collective-permute-start.2 = (bf16[8,256,256]{2,1,0:T(8,128)(2,1)S(1)}, bf16[8,256,256]{2,1,0:T(8,128)(2,1)}, u32[]{:S(2)}, u32[]{:S(2)}) collective-permute-start(bf16[8,256,256]{2,1,0:T(8,128)(2,1)S(1)} %copy-done.2), channel_id=1, source_target_pairs={{0,1},{1,2},{2,3},{3,4},{4,5},{5,6},{6,7},{7,8},{8,9},{9,10},{10,1... | collective-permute-start | bytes 3145736 | tf_op jit(solution)/shard_map/ppermute | solution.py:22
  87.4 1.9 collective-permute-start.3
  89.4 6.9 %all-to-all-done.2.sig_ref.refs_11_.refs_3_.refs_12_ = bf16[8,8,32,256]{3,2,1,0:T(8,128)(2,1)S(1)} async-done(((bf16[8,8,32,256]{3,2,1,0:T(8,128)(2,1)}), bf16[8,8,32,256]{3,2,1,0:T(8,128)(2,1)S(1)}, u32[]{:S(2)}, u32[]{:S(2)}) %all-to-all-start.2) | async-done | bytes 1048608 | tf_op jit(solution)/shard_map/all_to_all | solution.py:15
  96.3 5.8 %collective-permute-start.4 = (bf16[8,8,32,256]{3,2,1,0:T(8,128)(2,1)S(1)}, bf16[8,8,32,256]{3,2,1,0:T(8,128)(2,1)}, u32[]{:S(2)}, u32[]{:S(2)}) collective-permute-start(bf16[8,8,32,256]{3,2,1,0:T(8,128)(2,1)S(1)} %all-to-all-done.2.sig_ref.refs_11_.refs_3_.refs_12_), channel_id=1, source_target_pairs={{0,1},{1,2},{2,3},{3,4},{4,5},{5,6},{6,7},{7,8},{8,9},{9,10},{10,1... | collective-permute-start | bytes 3145736 | tf_op jit(solution)/shard_map/ppermute | solution.py:22
  102.1 4.8 %collective-permute-start.5 = (bf16[8,8,32,256]{3,2,1,0:T(8,128)(2,1)S(1)}, bf16[8,8,32,256]{3,2,1,0:T(8,128)(2,1)}, u32[]{:S(2)}, u32[]{:S(2)}) collective-permute-start(bf16[8,8,32,256]{3,2,1,0:T(8,128)(2,1)S(1)} %all-to-all-done.2.sig_ref.refs_11_.refs_3_.refs_12_), channel_id=1, source_target_pairs={{1,0},{2,1},{3,2},{4,3},{5,4},{6,5},{7,6},{8,7},{9,8},{10,9},{11,1... | collective-permute-start | bytes 3145736 | tf_op jit(solution)/shard_map/ppermute | solution.py:22
  106.9 1.4 gram_1.1
  108.9 11.5 %all-to-all-start.3 = ((f32[32,1,128]{2,1,0:T(1,128)}), f32[32,1,128]{2,1,0:T(1,128)S(1)}, u32[]{:S(2)}, u32[]{:S(2)}) async-start(f32[32,1,128]{2,1,0:T(1,128)} %broadcast_in_dim.16), calls=%async_computation.3 | async-start | bytes 32768 | tf_op jit(solution)/shard_map/all_to_all | solution.py:15
  120.4 22.1 %all-to-all-done.3 = f32[32,1,128]{2,1,0:T(1,128)S(1)} async-done(((f32[32,1,128]{2,1,0:T(1,128)}), f32[32,1,128]{2,1,0:T(1,128)S(1)}, u32[]{:S(2)}, u32[]{:S(2)}) %all-to-all-start.3) | async-done | bytes 16416 | tf_op jit(solution)/shard_map/all_to_all | solution.py:15
  145.0 18.7 %product_2.1 = bf16[8,8,32,256]{3,2,1,0:T(8,128)(2,1)S(1)} custom-call(s32[3,8]{1,0:T(4,128)S(1)} %broadcast_subtract_fusion.refs_0_, s32[2,8]{1,0:T(2,128)S(1)} %copy-done.13, f32[32,128]{1,0:T(8,128)S(1)} %bitcast.18, f32[32,128]{1,0:T(8,128)S(1)} %bitcast.22, bf16[8,256,256]{2,1,0:T(8,128)(2,1)S(1)} %copy-done.5, ...), custom_call_target="tpu_custom_call" | custom-call | tf_op jit(solution)/shard_map/product_2/pallas_call | solution.py:260
  163.7 19.2 %all_to_all.57 = bf16[8,8,32,256]{3,2,1,0:T(8,128)(2,1)} all-to-all(bf16[8,8,32,256]{3,2,1,0:T(8,128)(2,1)S(1)} %product_2.1), channel_id=1, replica_groups=mesh['term'=8,'sector'=32] {'term'}, dimensions={0} | all-to-all | bytes 2097152 | tf_op jit(solution)/shard_map/all_to_all | solution.py:298
  183.0 1.4 reduce_sum.72
  184.5 17.0 %all_to_all.58.refs_2_.refs_15_ = bf16[8,8,32,256]{3,2,1,0:T(8,128)(2,1)} all-to-all(bf16[8,8,32,256]{3,2,1,0:T(8,128)(2,1)S(1)} %broadcast_in_dim.17), channel_id=1, replica_groups=mesh['term'=8,'sector'=32] {'term'}, dimensions={0} | all-to-all | bytes 2097152 | tf_op jit(solution)/shard_map/all_to_all | solution.py:15
  201.5 5.1 %collective-permute-start.6 = (bf16[8,8,32,256]{3,2,1,0:T(8,128)(2,1)}, bf16[8,8,32,256]{3,2,1,0:T(8,128)(2,1)}, u32[]{:S(2)}, u32[]{:S(2)}) collective-permute-start(bf16[8,8,32,256]{3,2,1,0:T(8,128)(2,1)} %all_to_all.58.refs_2_.refs_15_), channel_id=1, source_target_pairs={{0,1},{1,2},{2,3},{3,4},{4,5},{5,6},{6,7},{7,8},{8,9},{9,10},{10,1... | collective-permute-start | bytes 3145736 | tf_op jit(solution)/shard_map/ppermute | solution.py:22
  206.6 1.9 collective-permute-start.7
  209.9 4.9 %gram_2.1 = f32[1,128]{1,0:T(1,128)S(1)} custom-call(f32[32,128]{1,0:T(8,128)S(1)} %bitcast.20, f32[32,128]{1,0:T(8,128)S(1)} %bitcast.23, bf16[8,8,32,256]{3,2,1,0:T(8,128)(2,1)} %all_to_all.58.refs_2_.refs_15_, bf16[8,8,32,256]{3,2,1,0:T(8,128)(2,1)S(1)} %copy-done.1, bf16[8,256,256]{2,1,0:T(8,128)(2,1)S(1)} %get-tuple-element.9.refs_4_.psi_ref.refs_5_.refs_6_, ...), custom_call_target="tpu_custom_call" | custom-call | tf_op jit(solution)/shard_map/gram_2/pallas_call | solution.py:275
  215.4 11.0 %all-to-all-start.6 = ((f32[32,1,128]{2,1,0:T(1,128)}), f32[32,1,128]{2,1,0:T(1,128)S(1)}, u32[]{:S(2)}, u32[]{:S(2)}) async-start(f32[32,1,128]{2,1,0:T(1,128)} %broadcast_in_dim.18), calls=%async_computation.6 | async-start | bytes 32768 | tf_op jit(solution)/shard_map/all_to_all | solution.py:15
  226.5 11.1 %all-to-all-done.6 = f32[32,1,128]{2,1,0:T(1,128)S(1)} async-done(((f32[32,1,128]{2,1,0:T(1,128)}), f32[32,1,128]{2,1,0:T(1,128)S(1)}, u32[]{:S(2)}, u32[]{:S(2)}) %all-to-all-start.6) | async-done | bytes 16416 | tf_op jit(solution)/shard_map/all_to_all | solution.py:15
  240.1 27.3 %product_3.1 = (bf16[3,8,256,256]{3,2,1,0:T(8,128)(2,1)}, f32[8,8,32,256]{3,2,1,0:T(8,128)}, f32[1,128]{1,0:T(1,128)S(1)}) custom-call(s32[3,8]{1,0:T(4,128)S(1)} %broadcast_subtract_fusion.refs_0_, s32[2,8]{1,0:T(2,128)S(1)} %copy-done.13, f32[32,128]{1,0:T(8,128)S(1)} %bitcast.21, f32[32,128]{1,0:T(8,128)S(1)} %bitcast.24, f32[32,128]{1,0:T(8,128)S(1)} %bitcast.25, ...), custom_call_target="tpu_custom_call" | custom-call | tf_op jit(solution)/shard_map/product_3/pallas_call | solution.py:260
  268.1 4.2 %all-to-all-start.7 = ((f32[8,1,128]{2,1,0:T(1,128)}), f32[8,1,128]{2,1,0:T(1,128)S(1)}, u32[]{:S(2)}, u32[]{:S(2)}) async-start(f32[8,1,128]{2,1,0:T(1,128)} %broadcast_in_dim.19), calls=%async_computation.7 | async-start | bytes 8192 | tf_op jit(solution)/shard_map/all_to_all | solution.py:15
  272.3 4.9 %all-to-all-done.7 = f32[8,1,128]{2,1,0:T(1,128)S(1)} async-done(((f32[8,1,128]{2,1,0:T(1,128)}), f32[8,1,128]{2,1,0:T(1,128)S(1)}, u32[]{:S(2)}, u32[]{:S(2)}) %all-to-all-start.7) | async-done | bytes 4128 | tf_op jit(solution)/shard_map/all_to_all | solution.py:15
  277.8 10.0 %all-to-all-start.8 = ((f32[32,1,128]{2,1,0:T(1,128)}), f32[32,1,128]{2,1,0:T(1,128)S(1)}, u32[]{:S(2)}, u32[]{:S(2)}) async-start(f32[32,1,128]{2,1,0:T(1,128)} %broadcast_in_dim.20), calls=%async_computation.8 | async-start | bytes 32768 | tf_op jit(solution)/shard_map/all_to_all | solution.py:15
  287.8 1.7 dynamic-slice_bitcast_fusion
  289.5 7.7 %all-to-all-done.8 = f32[32,1,128]{2,1,0:T(1,128)S(1)} async-done(((f32[32,1,128]{2,1,0:T(1,128)}), f32[32,1,128]{2,1,0:T(1,128)S(1)}, u32[]{:S(2)}, u32[]{:S(2)}) %all-to-all-start.8) | async-done | bytes 16416 | tf_op jit(solution)/shard_map/all_to_all | solution.py:15
  298.6 3.1 %stack.12 = f32[9]{0:T(128)S(1)} concatenate(f32[1]{0:T(128)} %bitcast.4, f32[1]{0:T(128)} %bitcast.8, f32[1]{0:T(128)} %get-tuple-element.15, f32[1]{0:T(128)} %get-tuple-element.20, f32[1]{0:T(128)} %get-tuple-element.21, f32[1]{0:T(128)} %get-tuple-element.14, f32[2]{0:T(128)S(1)} %slice.36, f32[1]{0:T(128)} %get-tuple-element.13), dimensions={0} | concatenate | bytes 72 | tf_op jit(solution)/shard_map/stack | solution.py:338
  (57 shorter events, 16.8 us)
Async XLA Ops:
  0.6 1.2 copy-start.10
  1.9 0.7 copy-start.11
  3.7 37.2 %collective-permute-start = (bf16[8,256,256]{2,1,0:T(8,128)(2,1)S(1)}, bf16[8,256,256]{2,1,0:T(8,128)(2,1)S(1)}, u32[]{:S(2)}, u32[]{:S(2)}) collective-permute-start(bf16[8,256,256]{2,1,0:T(8,128)(2,1)S(1)} %get-tuple-element.9.refs_4_.psi_ref.refs_5_.refs_6_), channel_id=1, source_target_pairs={{0,1},{1,2},{2,3},{3,4},{4,5},{5,6},{6,7},{7,8},{8,9},{9,10},{10,1... | collective-permute-start | bytes 3145736 | tf_op jit(solution)/shard_map/ppermute | solution.py:22
  8.3 32.6 %collective-permute-start.1 = (bf16[8,256,256]{2,1,0:T(8,128)(2,1)S(1)}, bf16[8,256,256]{2,1,0:T(8,128)(2,1)S(1)}, u32[]{:S(2)}, u32[]{:S(2)}) collective-permute-start(bf16[8,256,256]{2,1,0:T(8,128)(2,1)S(1)} %get-tuple-element.9.refs_4_.psi_ref.refs_5_.refs_6_), channel_id=1, source_target_pairs={{1,0},{2,1},{3,2},{4,3},{5,4},{6,5},{7,6},{8,7},{9,8},{10,9},{11,1... | collective-permute-start | bytes 3145736 | tf_op jit(solution)/shard_map/ppermute | solution.py:22
  10.8 30.1 %all-to-all-start = ((f32[32,1,128]{2,1,0:T(1,128)}), f32[32,1,128]{2,1,0:T(1,128)S(1)}, u32[]{:S(2)}, u32[]{:S(2)}) async-start(f32[32,1,128]{2,1,0:T(1,128)} %broadcast_in_dim.14), calls=%async_computation | async-start | bytes 32768 | tf_op jit(solution)/shard_map/all_to_all | solution.py:15
  40.9 10.8 %copy-start.4 = (bf16[8,256,256]{2,1,0:T(8,128)(2,1)}, bf16[8,256,256]{2,1,0:T(8,128)(2,1)S(1)}, u32[]{:S(2)}) copy-start(bf16[8,256,256]{2,1,0:T(8,128)(2,1)S(1)} %collective-permute-done.refs_3_.refs_4_.refs_5_) | copy-start | bytes 3145732
  40.9 0.7 copy-start.12
  51.7 1.0 copy-start.7
  52.7 29.8 %copy-start.2 = (bf16[8,256,256]{2,1,0:T(8,128)(2,1)S(1)}, bf16[8,256,256]{2,1,0:T(8,128)(2,1)}, u32[]{:S(2)}) copy-start(bf16[8,256,256]{2,1,0:T(8,128)(2,1)} %refs_9_.1) | copy-start | bytes 3145732
  77.8 64.7 %copy-start.13 = (s32[2,8]{1,0:T(2,128)S(1)}, s32[2,8]{1,0:T(2,128)}, u32[]{:S(2)}) copy-start(s32[2,8]{1,0:T(2,128)} %refs_1_.5) | copy-start | bytes 196
  78.9 17.4 %all-to-all-start.2 = ((bf16[8,8,32,256]{3,2,1,0:T(8,128)(2,1)}), bf16[8,8,32,256]{3,2,1,0:T(8,128)(2,1)S(1)}, u32[]{:S(2)}, u32[]{:S(2)}) async-start(bf16[8,8,32,256]{3,2,1,0:T(8,128)(2,1)} %broadcast_in_dim.15), calls=%async_computation.2 | async-start | bytes 2097152 | tf_op jit(solution)/shard_map/all_to_all | solution.py:15
  82.5 37.8 %collective-permute-start.2 = (bf16[8,256,256]{2,1,0:T(8,128)(2,1)S(1)}, bf16[8,256,256]{2,1,0:T(8,128)(2,1)}, u32[]{:S(2)}, u32[]{:S(2)}) collective-permute-start(bf16[8,256,256]{2,1,0:T(8,128)(2,1)S(1)} %copy-done.2), channel_id=1, source_target_pairs={{0,1},{1,2},{2,3},{3,4},{4,5},{5,6},{6,7},{7,8},{8,9},{9,10},{10,1... | collective-permute-start | bytes 3145736 | tf_op jit(solution)/shard_map/ppermute | solution.py:22
  87.4 32.9 %collective-permute-start.3 = (bf16[8,256,256]{2,1,0:T(8,128)(2,1)S(1)}, bf16[8,256,256]{2,1,0:T(8,128)(2,1)}, u32[]{:S(2)}, u32[]{:S(2)}) collective-permute-start(bf16[8,256,256]{2,1,0:T(8,128)(2,1)S(1)} %copy-done.2), channel_id=1, source_target_pairs={{1,0},{2,1},{3,2},{4,3},{5,4},{6,5},{7,6},{8,7},{9,8},{10,9},{11,1... | collective-permute-start | bytes 3145736 | tf_op jit(solution)/shard_map/ppermute | solution.py:22
  96.3 46.2 %copy-start = (bf16[8,8,32,256]{3,2,1,0:T(8,128)(2,1)}, bf16[8,8,32,256]{3,2,1,0:T(8,128)(2,1)S(1)}, u32[]{:S(2)}) copy-start(bf16[8,8,32,256]{3,2,1,0:T(8,128)(2,1)S(1)} %all-to-all-done.2.sig_ref.refs_11_.refs_3_.refs_12_) | copy-start | bytes 3145732
  96.3 46.2 %collective-permute-start.4 = (bf16[8,8,32,256]{3,2,1,0:T(8,128)(2,1)S(1)}, bf16[8,8,32,256]{3,2,1,0:T(8,128)(2,1)}, u32[]{:S(2)}, u32[]{:S(2)}) collective-permute-start(bf16[8,8,32,256]{3,2,1,0:T(8,128)(2,1)S(1)} %all-to-all-done.2.sig_ref.refs_11_.refs_3_.refs_12_), channel_id=1, source_target_pairs={{0,1},{1,2},{2,3},{3,4},{4,5},{5,6},{6,7},{7,8},{8,9},{9,10},{10,1... | collective-permute-start | bytes 3145736 | tf_op jit(solution)/shard_map/ppermute | solution.py:22
  102.1 40.4 %collective-permute-start.5 = (bf16[8,8,32,256]{3,2,1,0:T(8,128)(2,1)S(1)}, bf16[8,8,32,256]{3,2,1,0:T(8,128)(2,1)}, u32[]{:S(2)}, u32[]{:S(2)}) collective-permute-start(bf16[8,8,32,256]{3,2,1,0:T(8,128)(2,1)S(1)} %all-to-all-done.2.sig_ref.refs_11_.refs_3_.refs_12_), channel_id=1, source_target_pairs={{1,0},{2,1},{3,2},{4,3},{5,4},{6,5},{7,6},{8,7},{9,8},{10,9},{11,1... | collective-permute-start | bytes 3145736 | tf_op jit(solution)/shard_map/ppermute | solution.py:22
  108.9 33.6 %all-to-all-start.3 = ((f32[32,1,128]{2,1,0:T(1,128)}), f32[32,1,128]{2,1,0:T(1,128)S(1)}, u32[]{:S(2)}, u32[]{:S(2)}) async-start(f32[32,1,128]{2,1,0:T(1,128)} %broadcast_in_dim.16), calls=%async_computation.3 | async-start | bytes 32768 | tf_op jit(solution)/shard_map/all_to_all | solution.py:15
  142.5 1.2 copy-start.5
  143.8 1.2 copy-start.8
  163.7 46.2 %copy-start.1 = (bf16[8,8,32,256]{3,2,1,0:T(8,128)(2,1)S(1)}, bf16[8,8,32,256]{3,2,1,0:T(8,128)(2,1)}, u32[]{:S(2)}) copy-start(bf16[8,8,32,256]{3,2,1,0:T(8,128)(2,1)} %copy-done) | copy-start | bytes 3145732
  163.7 46.2 %copy-start.3 = (bf16[8,256,256]{2,1,0:T(8,128)(2,1)S(1)}, bf16[8,256,256]{2,1,0:T(8,128)(2,1)}, u32[]{:S(2)}) copy-start(bf16[8,256,256]{2,1,0:T(8,128)(2,1)} %refs_9_.1) | copy-start | bytes 3145732
  201.5 36.2 %collective-permute-start.6 = (bf16[8,8,32,256]{3,2,1,0:T(8,128)(2,1)}, bf16[8,8,32,256]{3,2,1,0:T(8,128)(2,1)}, u32[]{:S(2)}, u32[]{:S(2)}) collective-permute-start(bf16[8,8,32,256]{3,2,1,0:T(8,128)(2,1)} %all_to_all.58.refs_2_.refs_15_), channel_id=1, source_target_pairs={{0,1},{1,2},{2,3},{3,4},{4,5},{5,6},{6,7},{7,8},{8,9},{9,10},{10,1... | collective-permute-start | bytes 3145736 | tf_op jit(solution)/shard_map/ppermute | solution.py:22
  206.6 31.1 %collective-permute-start.7 = (bf16[8,8,32,256]{3,2,1,0:T(8,128)(2,1)}, bf16[8,8,32,256]{3,2,1,0:T(8,128)(2,1)}, u32[]{:S(2)}, u32[]{:S(2)}) collective-permute-start(bf16[8,8,32,256]{3,2,1,0:T(8,128)(2,1)} %all_to_all.58.refs_2_.refs_15_), channel_id=1, source_target_pairs={{1,0},{2,1},{3,2},{4,3},{5,4},{6,5},{7,6},{8,7},{9,8},{10,9},{11,1... | collective-permute-start | bytes 3145736 | tf_op jit(solution)/shard_map/ppermute | solution.py:22
  215.4 22.2 %all-to-all-start.6 = ((f32[32,1,128]{2,1,0:T(1,128)}), f32[32,1,128]{2,1,0:T(1,128)S(1)}, u32[]{:S(2)}, u32[]{:S(2)}) async-start(f32[32,1,128]{2,1,0:T(1,128)} %broadcast_in_dim.18), calls=%async_computation.6 | async-start | bytes 32768 | tf_op jit(solution)/shard_map/all_to_all | solution.py:15
  237.7 1.2 copy-start.6
  238.9 1.2 copy-start.9
  268.1 9.1 %all-to-all-start.7 = ((f32[8,1,128]{2,1,0:T(1,128)}), f32[8,1,128]{2,1,0:T(1,128)S(1)}, u32[]{:S(2)}, u32[]{:S(2)}) async-start(f32[8,1,128]{2,1,0:T(1,128)} %broadcast_in_dim.19), calls=%async_computation.7 | async-start | bytes 8192 | tf_op jit(solution)/shard_map/all_to_all | solution.py:15
  277.8 19.4 %all-to-all-start.8 = ((f32[32,1,128]{2,1,0:T(1,128)}), f32[32,1,128]{2,1,0:T(1,128)S(1)}, u32[]{:S(2)}, u32[]{:S(2)}) async-start(f32[32,1,128]{2,1,0:T(1,128)} %broadcast_in_dim.20), calls=%async_computation.8 | async-start | bytes 32768 | tf_op jit(solution)/shard_map/all_to_all | solution.py:15

commit v2 on v0

v2 whole, which is shorter than its diff:
```python
import jax
import jax.numpy as jnp
from jax import lax
from jax.experimental import pallas as pl
from jax.experimental.pallas import tpu as pltpu
from jax.sharding import PartitionSpec as P

epsilon = 1e-06
f32 = jnp.float32
bf16 = jnp.bfloat16


def to_everyone(x, axis):
    devices = lax.axis_size(axis)
    return lax.all_to_all(jnp.broadcast_to(x[None], (devices, *x.shape)), axis, 0, 0, tiled=True)


def swapped(block, first):
    pairs = [(i, i + 1) for i in range(first, lax.axis_size("sector") - 1, 2)]
    return lax.ppermute(block, "sector", pairs + [(j, i) for i, j in pairs])


def row_of(total_ref, entries):
    return jnp.sum(total_ref[...], axis=0, keepdims=True) * (1.0 / entries)


def one(row, k):
    return row[:, k : k + 1]


def first_scale(row1):
    return 1.0 / jnp.sqrt(one(row1, 6) + epsilon)


def second_weights(row1):
    inv = first_scale(row1)
    theta, a, b, aa, ab, bb, vv = (inv * inv * one(row1, k) for k in range(7))
    o = a - theta * b
    length = aa + theta * theta * bb + o * o * vv - 2.0 * theta * ab - 2.0 * o * a + 2.0 * theta * o * b
    r = 1.0 / jnp.sqrt(jnp.maximum(length, 0.0) + epsilon)
    return r * inv, -r * theta * inv, -r * o * inv


def third_weights(row1, row2):
    inv = first_scale(row1)
    theta = one(row2, 0)
    v1a = inv * one(row2, 1)
    v1b = inv * one(row2, 2)
    v2a = one(row2, 3)
    v2b = one(row2, 4)
    aa = one(row2, 5)
    ab = one(row2, 6)
    bb = one(row2, 7)
    v1v2 = inv * one(row2, 8)
    v2v2 = one(row2, 9)
    v1v1 = inv * inv * one(row1, 6)
    o1 = v1a - theta * v1b
    o2 = v2a - theta * v2b
    length = (
        aa
        - 2.0 * theta * ab
        + theta * theta * bb
        - 2.0 * o1 * o1
        - 2.0 * o2 * o2
        + o1 * o1 * v1v1
        + 2.0 * o1 * o2 * v1v2
        + o2 * o2 * v2v2
    )
    r = 1.0 / jnp.sqrt(jnp.maximum(length, 0.0) + epsilon)
    return r, -r * theta, -r * o1 * inv, -r * o2


def fold(x):
    return jnp.sum(x.reshape(x.shape[0] // 8, 8, x.shape[1]), axis=0)


def row_from(sums):
    lane = lax.broadcasted_iota(jnp.int32, (1, 128), 1)
    row = jnp.zeros((1, 128), f32)
    for k, total in enumerate(sums):
        row = row + jnp.where(lane == k, jnp.sum(total), 0.0)
    return row


def keep_of(dims_ref, s, width):
    rows = lax.broadcasted_iota(jnp.int32, (width, width), 0)
    cols = lax.broadcasted_iota(jnp.int32, (width, width), 1)
    return (rows < dims_ref[0, s]) & (cols < dims_ref[1, s])


def start_kernel(dims_ref, psi_ref, out_ref):
    blocks, width = psi_ref.shape[0], psi_ref.shape[1]
    pieces, share = out_ref.shape[0], out_ref.shape[2]

    def body(s, carry):
        cols = lax.broadcasted_iota(jnp.int32, (share, width), 1) < dims_ref[1, s]
        ids = lax.broadcasted_iota(jnp.int32, (share, width), 0)
        for p in range(pieces):
            keep = (ids < dims_ref[0, s] - p * share) & cols
            x = jnp.where(keep, psi_ref[s, pl.ds(p * share, share)].astype(f32), 0.0)
            out_ref[p, s] = x.astype(bf16)
        return carry

    lax.fori_loop(0, blocks, body, 0)


def reduce_kernel(stage, arrived_ref, psi_ref, d_ref, *refs):
    if stage > 1:
        sig1_ref, v2_ref, refs = refs[0], refs[1], refs[2:]
    mine_ref, row_ref = refs
    pieces, blocks, share, width = arrived_ref.shape

    def body(s, acc):
        sig = arrived_ref[0, s].astype(f32)
        for p in range(1, pieces):
            sig = sig + arrived_ref[p, s].astype(f32)
        mine_ref[s] = sig
        psi = psi_ref[s].astype(f32)
        rd = 1.0 / d_ref[s].astype(f32)
        a = sig * rd
        if stage == 1:
            b = psi * rd
            terms = (psi * sig, psi * a, psi * b, a * a, a * b, b * b, psi * psi)
        else:
            v2 = v2_ref[s]
            b = v2 * rd
            terms = (
                v2 * sig,
                psi * a,
                psi * b,
                v2 * a,
                v2 * b,
                a * a,
                a * b,
                b * b,
                psi * v2,
                v2 * v2,
                psi * sig,
                v2 * sig1_ref[s],
            )
        return tuple(t + fold(x) for t, x in zip(acc, terms))

    acc = lax.fori_loop(0, blocks, body, (jnp.zeros((8, width), f32),) * (7 if stage == 1 else 12))
    row_ref[...] = row_from(acc)


def update_kernel(stage, entries, *refs):
    tots, refs = refs[:stage], refs[stage:]
    psi_ref, d_ref, sig1_ref, refs = refs[0], refs[1], refs[2], refs[3:]
    if stage > 1:
        sig2_ref, v2_ref, refs = refs[0], refs[1], refs[2:]
    v_ref, vb_ref, all_ref = refs[:3]
    pieces, blocks, share, width = all_ref.shape
    rows = [row_of(t, entries) for t in tots]
    if stage == 1:
        p, q, w = (x[0, 0] for x in second_weights(*rows))
    else:
        p, q, w, y = (x[0, 0] for x in third_weights(*rows))

    def body(s, acc):
        psi = psi_ref[s].astype(f32)
        rd = 1.0 / d_ref[s].astype(f32)
        sig1 = sig1_ref[s]
        if stage == 1:
            v = (p * sig1 + q * psi) * rd + w * psi
        else:
            sig2, v2 = sig2_ref[s], v2_ref[s]
            v = (p * sig2 + q * v2) * rd + w * psi + y * v2
            acc = acc[0] + fold(v * sig1), acc[1] + fold(v * sig2)
        v_ref[s] = v
        vb = v.astype(bf16)
        vb_ref[s] = vb
        for k in range(pieces):
            all_ref[k, s] = vb
        return acc

    acc = lax.fori_loop(0, blocks, body, (jnp.zeros((8, width), f32),) * (0 if stage == 1 else 2))
    if stage > 1:
        zero = jnp.zeros((8, width), f32)
        refs[3][...] = row_from([zero, zero, zero, *acc])


def dot(a, b, ca, cb):
    return lax.dot_general(a, b, (((ca,), (cb,)), ((), ())), preferred_element_type=f32)


def product_kernel(stage, *refs):
    conn_ref, dims_ref, far_ref, own_ref, near_ref = refs[:5]
    refs = refs[5:]
    if stage == 3:
        psi_ref, v2_ref, part_ref, refs = refs[0], refs[1], refs[2], refs[3:]
    left_ref, right_ref = refs[:2]
    if stage < 3:
        out_ref, vb_ref = refs[2:]
    else:
        env_ref, row_ref, vb_ref, acc_ref = refs[2:]
    step = pl.program_id(0)
    pieces, blocks, share, width = own_ref.shape
    terms, together = left_ref.shape[:2]

    @pl.when(step == 0)
    def _():
        def body(s, carry):
            for seg, ref in enumerate((far_ref, own_ref, near_ref)):
                vb_ref[seg * blocks + s] = ref[:, s].reshape(width, width)
            return carry

        lax.fori_loop(0, blocks, body, 0)
        if stage == 3:
            acc_ref[...] = jnp.zeros_like(acc_ref)

    halves = []
    for u in range(together):
        s = step * together + u
        halves.append([dot(left_ref[t, u], vb_ref[conn_ref[t, s]], 1, 0).astype(bf16) for t in range(terms)])
    for u in range(together):
        s = step * together + u
        side = jnp.concatenate([right_ref[t, u] for t in range(terms)], axis=1)
        total = dot(jnp.concatenate(halves[u], axis=1), side, 1, 1)
        if stage < 3:
            total = jnp.where(keep_of(dims_ref, s, width), total, 0.0).astype(bf16)
            out_ref[:, u] = total.reshape(pieces, share, width)
        else:
            own_t = vb_ref[blocks + s].T
            for t in range(terms):
                env_ref[t, u] = (dot(own_t, halves[u][t], 1, 0) * width ** (-0.5)).astype(bf16)
            sums = [acc_ref[k] for k in range(3)]
            for p in range(pieces):
                part = total[p * share : (p + 1) * share]
                for k, ref in enumerate((psi_ref, v2_ref, own_ref)):
                    sums[k] += fold(ref[p, s].astype(f32) * part)
            for k in range(3):
                acc_ref[k] = sums[k]
    if stage == 3:

        @pl.when(step == pl.num_programs(0) - 1)
        def _():
            row_ref[...] = row_from([acc_ref[k] for k in range(3)]) + part_ref[...]


def product(stage, conn, dims, groups, more, left, right):
    terms, blocks, width = left.shape[:3]
    pieces, _, share, _ = groups[0].shape
    together = 2
    smem = pl.BlockSpec(memory_space=pltpu.SMEM)
    vmem = pl.BlockSpec(memory_space=pltpu.VMEM)
    env_spec = pl.BlockSpec((terms, together, width, width), lambda s: (0, s, 0, 0))
    scratch = [pltpu.VMEM((3 * blocks, width, width), bf16)]
    if stage < 3:
        out_shape = jax.ShapeDtypeStruct((pieces, blocks, share, width), bf16)
        out_specs = pl.BlockSpec((pieces, together, share, width), lambda s: (0, s, 0, 0))
    else:
        out_shape = (jax.ShapeDtypeStruct(left.shape, bf16), jax.ShapeDtypeStruct((1, 128), f32))
        out_specs = (env_spec, pl.BlockSpec((1, 128), lambda s: (0, 0)))
        scratch.append(pltpu.VMEM((3, 8, width), f32))
    return pl.pallas_call(
        lambda *refs: product_kernel(stage, *refs),
        grid=(blocks // together,),
        in_specs=[smem, smem] + [vmem] * (3 + len(more)) + [env_spec, env_spec],
        out_specs=out_specs,
        out_shape=out_shape,
        scratch_shapes=scratch,
        name=f"product_{stage}",
        compiler_params=pltpu.CompilerParams(vmem_limit_bytes=32 << 20),
    )(conn, dims, *groups, *more, left, right)


def call_small(kernel, dims, arrays, out_shape, name):
    smem = pl.BlockSpec(memory_space=pltpu.SMEM)
    vmem = pl.BlockSpec(memory_space=pltpu.VMEM)
    return pl.pallas_call(
        kernel,
        in_specs=[smem] * len(dims) + [vmem] * len(arrays),
        out_specs=jax.tree.map(lambda _: vmem, out_shape),
        out_shape=out_shape,
        name=name,
        compiler_params=pltpu.CompilerParams(vmem_limit_bytes=16 << 20),
    )(*dims, *arrays)


def last_kernel(entries, tot1, tot2, tot3, out_ref):
    r1, r2, r3 = (row_of(t, entries) for t in (tot1, tot2, tot3))
    inv = first_scale(r1)
    values = (
        (inv * inv * one(r1, 0), inv * one(r2, 10), inv * one(r3, 0)),
        (inv * one(r2, 11), one(r2, 0), one(r3, 1)),
        (inv * one(r3, 3), one(r3, 4), one(r3, 2)),
    )
    row = lax.broadcasted_iota(jnp.int32, (3, 3), 0)
    col = lax.broadcasted_iota(jnp.int32, (3, 3), 1)
    out = jnp.zeros((3, 3), f32)
    for i in range(3):
        for j in range(3):
            out = jnp.where((row == i) & (col == j), values[i][j], out)
    out_ref[...] = out


def on_device(psi_start, left_env, right_env, connect, sector_dims, precond):
    blocks, width = psi_start.shape[:2]
    devices = lax.axis_size("sector")
    pieces = lax.axis_size("term")
    share = width // pieces
    entries = float(blocks * devices * width * width)
    everyone = ("term", "sector")
    row = jax.ShapeDtypeStruct((1, 128), f32)
    cut = jax.ShapeDtypeStruct((pieces, blocks, share, width), bf16)
    part = jax.ShapeDtypeStruct((blocks, share, width), f32)
    part_b = jax.ShapeDtypeStruct((blocks, share, width), bf16)
    place = lax.axis_index("sector")
    conn = connect - (place * blocks - blocks)
    turned = (2 - conn // blocks) * blocks + conn % blocks
    conn = jnp.where(place % 2 == 1, turned, conn)
    args = (left_env, right_env)

    def far(mine):
        return to_everyone(swapped(mine, 1), "term")

    def near(block):
        return swapped(block, 0)

    def exchange(x):
        return lax.all_to_all(x, "term", 0, 0, tiled=True)

    def reduced(stage, partial, *shares):
        return call_small(
            lambda *refs: reduce_kernel(stage, *refs), [], [exchange(partial), *shares], (part, row), f"reduce_{stage}"
        )

    def updated(stage, tots, *shares):
        out = (part, part_b, cut) + ((row,) if stage > 1 else ())
        v, vb, every, *more = call_small(
            lambda *refs: update_kernel(stage, entries, *refs), [], [*tots, *shares], out, f"update_{stage}"
        )
        own = exchange(every)
        return v, (far(vb), own, near(own)), more

    psi = call_small(start_kernel, [sector_dims], [psi_start], cut, "start")
    term = lax.axis_index("term")
    psi_share = lax.dynamic_index_in_dim(psi, term, 0, keepdims=False)
    d_share = lax.dynamic_slice_in_dim(precond, term * share, share, 1)

    partial = product(1, conn, sector_dims, (far(psi_share), psi, near(psi)), (), *args)
    sig1, row1 = reduced(1, partial, psi_share, d_share)
    tot1 = to_everyone(row1[0], everyone)
    v2, groups2, _ = updated(1, (tot1,), psi_share, d_share, sig1)

    partial = product(2, conn, sector_dims, groups2, (), *args)
    sig2, row2 = reduced(2, partial, psi_share, d_share, sig1, v2)
    tot2 = to_everyone(row2[0], everyone)
    v3, groups3, (more,) = updated(2, (tot1, tot2), psi_share, d_share, sig1, sig2, v2)

    env, row3 = product(3, conn, sector_dims, groups3, (psi, groups2[1], more), *args)
    tot3 = to_everyone(row3[0], everyone)
    projected = call_small(
        lambda *refs: last_kernel(entries, *refs), [], [tot1, tot2, tot3], jax.ShapeDtypeStruct((3, 3), f32), "last"
    )
    return (projected, v3, env)


def solution(mesh):
    placed = (
        P("sector", None, None),
        P("term", "sector", None, None),
        P("term", "sector", None, None),
        P("term", "sector"),
        P(None, "sector"),
        P("sector", None, None),
    )
    return jax.shard_map(
        on_device,
        mesh=mesh,
        in_specs=placed,
        out_specs=(P(), P("sector", "term", None), P("term", "sector", None, None)),
        check_vma=False,
    )
```

time: 688 us -> 255 us (0.37)
  waiting for transfers between devices: 399 us -> 82.6 us
  other arithmetic: 49.7 us -> 0.02 us
  matrix products: 38.5 us -> 0 us
  local copies, waits for them, and re-layouts: 46.4 us -> 22.7 us
  blocking collectives: 111 us -> 90.2 us
  Pallas kernels: 0 us -> 20.5 us
  between operations: 18.1 us -> 0.91 us
  starting transfers between devices: 24.1 us -> 37.5 us
    psum x3 -> x0, waiting for transfers between devices: 352 us -> none  [on_device(): sigma = lax.psum(total, 'term')]
    all_to_all x1 -> x6, waiting for transfers between devices: 5.52 us -> 68.3 us  [the longest x3 34.2 us: to_everyone(): lax.all_to_all(jnp.broadcast_to(x[None], (devices, *x.shape)), axis, 0, 0...]
    dot_general x15 -> x0, matrix products: 38.5 us -> none  [the longest x9 27.4 us: on_device(): jnp.einsum('sik,slk->sil', half, right_env[apply_which], preferred_elemen...]
    reduce_sum x16 -> x0, other arithmetic: 33.7 us -> none  [the longest x2 10 us: on_device(): length = totals([jnp.sum(corr * corr)])[0]]
    gather x9 -> x0, local copies, waits for them, and re-layouts: 30.5 us -> none  [on_device(): source = jnp.take(extended, local_source[apply_which], axis=0)]
    ppermute x6, waiting for transfers between devices: 42.1 us -> 14.3 us  [swapped(): return lax.ppermute(block, 'sector', pairs + [(j, i) for i, j in pairs])]
    pallas_call x0 -> x9, Pallas kernels: none -> 20.5 us  [the longest x3 15.9 us: product(): pl.pallas_call(lambda *refs: product_kernel(stage, *refs), grid=(blocks /...]
    all_to_all x7 -> x4, blocking collectives: 111 us -> 90.2 us  [the longest x3 71.8 us: to_everyone(): lax.all_to_all(jnp.broadcast_to(x[None], (devices, *x.shape)), axis, 0, 0...]
  transfers between devices with their start and end apart: 10 -> 12, of which waited for: 10 -> 10; matrix products, arithmetic and copies ran while one was open for 2% -> 0% of each run, Pallas kernels for 0% -> 0%
where the time goes in v2:
time: 255 us; the launch traced here: 254 us
  blocking collectives  90.2 us (35%)
  waiting for transfers between devices  82.6 us (32%)
  starting transfers between devices  37.5 us (15%)
  local copies, waits for them, and re-layouts  22.7 us (9%)
  Pallas kernels  20.5 us (8%)
    all_to_all x3, blocking collectives, to_everyone(): lax.all_to_all(jnp.broadcast_to(x[None], (devices, *x.shape)), axis, 0, 0...  71.8 us
    all_to_all x3, waiting for transfers between devices, to_everyone(): lax.all_to_all(jnp.broadcast_to(x[None], (devices, *x.shape)), axis, 0, 0...  34.2 us
    all_to_all x3, waiting for transfers between devices, exchange(): return lax.all_to_all(x, 'term', 0, 0, tiled=True)  34.1 us
    all_to_all x1, blocking collectives, exchange(): return lax.all_to_all(x, 'term', 0, 0, tiled=True)  18.5 us
    unnamed x44, local copies, waits for them, and re-layouts  18.3 us
    pallas_call x3, Pallas kernels, product(): pl.pallas_call(lambda *refs: product_kernel(stage, *refs), grid=(blocks /...  15.9 us
    ppermute x6, waiting for transfers between devices, swapped(): return lax.ppermute(block, 'sector', pairs + [(j, i) for i, j in pairs])  14.3 us
    all_to_all x3, starting transfers between devices, to_everyone(): lax.all_to_all(jnp.broadcast_to(x[None], (devices, *x.shape)), axis, 0, 0...  13.9 us
  transfers between devices with their start and end apart: 12, of which 10 were waited for; matrix products, arithmetic and copies ran while one was open for 0% of the time, Pallas kernels for 0%

profile of v2, /device:TPU:1, one launch (start us, length us, event | category | flops | bytes accessed | tf_op | source)
XLA Modules:
  0.0 254.4 jit_solution(1078859497634405743)
XLA Ops:
  3.6 4.6 %collective-permute-start = (bf16[8,32,256]{2,1,0:T(8,128)(2,1)S(1)}, bf16[8,32,256]{2,1,0:T(8,128)(2,1)S(1)}, u32[]{:S(2)}, u32[]{:S(2)}) collective-permute-start(bf16[8,32,256]{2,1,0:T(8,128)(2,1)S(1)} %dynamic-slice_bitcast_fusion.refs_1_.refs_2_), channel_id=1, source_target_pairs={{1,2},{3,4},{5,6},{7,8},{9,10},{11,12},{13,14},{15,16},{17,18},{19... | collective-permute-start | bytes 393224 | tf_op jit(solution)/shard_map/ppermute | solution.py:20
  8.2 2.6 %collective-permute-done = bf16[8,32,256]{2,1,0:T(8,128)(2,1)S(1)} collective-permute-done((bf16[8,32,256]{2,1,0:T(8,128)(2,1)S(1)}, bf16[8,32,256]{2,1,0:T(8,128)(2,1)S(1)}, u32[]{:S(2)}, u32[]{:S(2)}) %collective-permute-start) | collective-permute-done | bytes 131104 | tf_op jit(solution)/shard_map/ppermute | solution.py:20
  11.9 5.4 %all-to-all-start = ((bf16[8,8,32,256]{3,2,1,0:T(8,128)(2,1)}), bf16[8,8,32,256]{3,2,1,0:T(8,128)(2,1)S(1)}, u32[]{:S(2)}, u32[]{:S(2)}) async-start(bf16[8,8,32,256]{3,2,1,0:T(8,128)(2,1)} %broadcast_in_dim.12), calls=%async_computation | async-start | bytes 2097152 | tf_op jit(solution)/shard_map/all_to_all | solution.py:15
  17.3 2.7 %collective-permute-done.1.refs_4_ = bf16[8,8,32,256]{3,2,1,0:T(8,128)(2,1)} collective-permute-done((bf16[8,8,32,256]{3,2,1,0:T(8,128)(2,1)S(1)}, bf16[8,8,32,256]{3,2,1,0:T(8,128)(2,1)}, u32[]{:S(2)}, u32[]{:S(2)}) %collective-permute-start.1) | collective-permute-done | bytes 1048608 | tf_op jit(solution)/shard_map/ppermute | solution.py:20
  20.1 9.0 %all-to-all-done.refs_2_ = bf16[8,8,32,256]{3,2,1,0:T(8,128)(2,1)S(1)} async-done(((bf16[8,8,32,256]{3,2,1,0:T(8,128)(2,1)}), bf16[8,8,32,256]{3,2,1,0:T(8,128)(2,1)S(1)}, u32[]{:S(2)}, u32[]{:S(2)}) %all-to-all-start) | async-done | bytes 1048608 | tf_op jit(solution)/shard_map/all_to_all | solution.py:15
  29.0 1.9 copy-done.1
  30.9 1.9 copy-done.4
  32.8 4.3 %product_1.1 = bf16[8,8,32,256]{3,2,1,0:T(8,128)(2,1)S(1)} custom-call(s32[3,8]{1,0:T(4,128)S(1)} %fusion.3.refs_0_, s32[2,8]{1,0:T(2,128)S(1)} %copy-done.18, bf16[8,8,32,256]{3,2,1,0:T(8,128)(2,1)S(1)} %all-to-all-done.refs_2_, bf16[8,8,32,256]{3,2,1,0:T(8,128)(2,1)S(1)} %start.1.refs_3_.refs_5_, bf16[8,8,32,256]{3,2,1,0:T(8,128)(2,1)} %collective-permute-done.1.refs_4_, ...), custom_call_target="tpu_custom_call" | custom-call | tf_op jit(solution)/shard_map/product_1/pallas_call | solution.py:256
  38.1 3.6 %all-to-all-start.1 = ((bf16[8,8,32,256]{3,2,1,0:T(8,128)(2,1)}), bf16[8,8,32,256]{3,2,1,0:T(8,128)(2,1)S(1)}, u32[]{:S(2)}, u32[]{:S(2)}) async-start(bf16[8,8,32,256]{3,2,1,0:T(8,128)(2,1)} %copy-done.7), calls=%async_computation.1 | async-start | bytes 2097152 | tf_op jit(solution)/shard_map/all_to_all | solution.py:322
  41.7 14.3 %all-to-all-done.1.refs_0_ = bf16[8,8,32,256]{3,2,1,0:T(8,128)(2,1)S(1)} async-done(((bf16[8,8,32,256]{3,2,1,0:T(8,128)(2,1)}), bf16[8,8,32,256]{3,2,1,0:T(8,128)(2,1)S(1)}, u32[]{:S(2)}, u32[]{:S(2)}) %all-to-all-start.1) | async-done | bytes 1048608 | tf_op jit(solution)/shard_map/all_to_all | solution.py:322
  56.6 30.4 %all_to_all.59 = f32[256,1,128]{2,1,0:T(1,128)S(1)} all-to-all(f32[256,1,128]{2,1,0:T(1,128)S(1)} %broadcast_in_dim.13), channel_id=1, replica_groups=mesh['term'=8,'sector'=32] {'term','sector'}, dimensions={0} | all-to-all | bytes 262144 | tf_op jit(solution)/shard_map/all_to_all | solution.py:15
  89.8 3.6 %all-to-all-start.4 = ((bf16[8,8,32,256]{3,2,1,0:T(8,128)(2,1)}), bf16[8,8,32,256]{3,2,1,0:T(8,128)(2,1)S(1)}, u32[]{:S(2)}, u32[]{:S(2)}) async-start(bf16[8,8,32,256]{3,2,1,0:T(8,128)(2,1)} %copy-done.15), calls=%async_computation.4 | async-start | bytes 2097152 | tf_op jit(solution)/shard_map/all_to_all | solution.py:322
  93.4 2.4 collective-permute-start.2
  95.8 4.4 %collective-permute-done.2 = bf16[8,32,256]{2,1,0:T(8,128)(2,1)} collective-permute-done((bf16[8,32,256]{2,1,0:T(8,128)(2,1)}, bf16[8,32,256]{2,1,0:T(8,128)(2,1)}, u32[]{:S(2)}, u32[]{:S(2)}) %collective-permute-start.2) | collective-permute-done | bytes 131104 | tf_op jit(solution)/shard_map/ppermute | solution.py:20
  100.2 9.9 %all-to-all-done.4.refs_3_.refs_6_ = bf16[8,8,32,256]{3,2,1,0:T(8,128)(2,1)S(1)} async-done(((bf16[8,8,32,256]{3,2,1,0:T(8,128)(2,1)}), bf16[8,8,32,256]{3,2,1,0:T(8,128)(2,1)S(1)}, u32[]{:S(2)}, u32[]{:S(2)}) %all-to-all-start.4) | async-done | bytes 1048608 | tf_op jit(solution)/shard_map/all_to_all | solution.py:322
  110.1 2.0 broadcast_in_dim.14
  112.1 4.2 %all-to-all-start.3 = ((bf16[8,8,32,256]{3,2,1,0:T(8,128)(2,1)}), bf16[8,8,32,256]{3,2,1,0:T(8,128)(2,1)}, u32[]{:S(2)}, u32[]{:S(2)}) async-start(bf16[8,8,32,256]{3,2,1,0:T(8,128)(2,1)} %broadcast_in_dim.14), calls=%async_computation.3 | async-start | bytes 2097152 | tf_op jit(solution)/shard_map/all_to_all | solution.py:15
  117.8 12.6 %all-to-all-done.3.refs_2_ = bf16[8,8,32,256]{3,2,1,0:T(8,128)(2,1)} async-done(((bf16[8,8,32,256]{3,2,1,0:T(8,128)(2,1)}), bf16[8,8,32,256]{3,2,1,0:T(8,128)(2,1)}, u32[]{:S(2)}, u32[]{:S(2)}) %all-to-all-start.3) | async-done | bytes 1048608 | tf_op jit(solution)/shard_map/all_to_all | solution.py:15
  130.4 1.9 copy-done.2
  132.3 1.9 copy-done.5
  134.2 4.6 %product_2.1 = bf16[8,8,32,256]{3,2,1,0:T(8,128)(2,1)S(1)} custom-call(s32[3,8]{1,0:T(4,128)S(1)} %fusion.3.refs_0_, s32[2,8]{1,0:T(2,128)S(1)} %copy-done.18, bf16[8,8,32,256]{3,2,1,0:T(8,128)(2,1)} %all-to-all-done.3.refs_2_, bf16[8,8,32,256]{3,2,1,0:T(8,128)(2,1)S(1)} %all-to-all-done.4.refs_3_.refs_6_, ...), custom_call_target="tpu_custom_call" | custom-call | tf_op jit(solution)/shard_map/product_2/pallas_call | solution.py:256
  138.8 18.5 %all_to_all.60.refs_0_ = bf16[8,8,32,256]{3,2,1,0:T(8,128)(2,1)S(1)} all-to-all(bf16[8,8,32,256]{3,2,1,0:T(8,128)(2,1)S(1)} %product_2.1), channel_id=1, replica_groups=mesh['term'=8,'sector'=32] {'term'}, dimensions={0} | all-to-all | bytes 2097152 | tf_op jit(solution)/shard_map/all_to_all | solution.py:322
  158.0 20.5 %all_to_all.61 = f32[256,1,128]{2,1,0:T(1,128)S(1)} all-to-all(f32[256,1,128]{2,1,0:T(1,128)S(1)} %broadcast_in_dim.15), channel_id=1, replica_groups=mesh['term'=8,'sector'=32] {'term','sector'}, dimensions={0} | all-to-all | bytes 262144 | tf_op jit(solution)/shard_map/all_to_all | solution.py:15
  181.5 4.2 %all-to-all-start.8 = ((bf16[8,8,32,256]{3,2,1,0:T(8,128)(2,1)}), bf16[8,8,32,256]{3,2,1,0:T(8,128)(2,1)}, u32[]{:S(2)}, u32[]{:S(2)}) async-start(bf16[8,8,32,256]{3,2,1,0:T(8,128)(2,1)} %copy-done.14), calls=%async_computation.8 | async-start | bytes 2097152 | tf_op jit(solution)/shard_map/all_to_all | solution.py:322
  185.8 2.4 collective-permute-start.4
  188.2 4.5 %collective-permute-done.4 = bf16[8,32,256]{2,1,0:T(8,128)(2,1)S(1)} collective-permute-done((bf16[8,32,256]{2,1,0:T(8,128)(2,1)}, bf16[8,32,256]{2,1,0:T(8,128)(2,1)S(1)}, u32[]{:S(2)}, u32[]{:S(2)}) %collective-permute-start.4) | collective-permute-done | bytes 131104 | tf_op jit(solution)/shard_map/ppermute | solution.py:20
  192.7 9.9 %all-to-all-done.8.refs_3_ = bf16[8,8,32,256]{3,2,1,0:T(8,128)(2,1)} async-done(((bf16[8,8,32,256]{3,2,1,0:T(8,128)(2,1)}), bf16[8,8,32,256]{3,2,1,0:T(8,128)(2,1)}, u32[]{:S(2)}, u32[]{:S(2)}) %all-to-all-start.8) | async-done | bytes 1048608 | tf_op jit(solution)/shard_map/all_to_all | solution.py:322
  203.6 4.2 %all-to-all-start.7 = ((bf16[8,8,32,256]{3,2,1,0:T(8,128)(2,1)}), bf16[8,8,32,256]{3,2,1,0:T(8,128)(2,1)}, u32[]{:S(2)}, u32[]{:S(2)}) async-start(bf16[8,8,32,256]{3,2,1,0:T(8,128)(2,1)} %broadcast_in_dim.16), calls=%async_computation.7 | async-start | bytes 2097152 | tf_op jit(solution)/shard_map/all_to_all | solution.py:15
  209.3 12.6 %all-to-all-done.7.refs_2_ = bf16[8,8,32,256]{3,2,1,0:T(8,128)(2,1)} async-done(((bf16[8,8,32,256]{3,2,1,0:T(8,128)(2,1)}), bf16[8,8,32,256]{3,2,1,0:T(8,128)(2,1)}, u32[]{:S(2)}, u32[]{:S(2)}) %all-to-all-start.7) | async-done | bytes 1048608 | tf_op jit(solution)/shard_map/all_to_all | solution.py:15
  222.0 1.9 copy-done.3
  225.8 7.0 %product_3.1 = (bf16[3,8,256,256]{3,2,1,0:T(8,128)(2,1)}, f32[1,128]{1,0:T(1,128)S(1)}) custom-call(s32[3,8]{1,0:T(4,128)S(1)} %fusion.3.refs_0_, s32[2,8]{1,0:T(2,128)S(1)} %copy-done.18, bf16[8,8,32,256]{3,2,1,0:T(8,128)(2,1)} %all-to-all-done.7.refs_2_, bf16[8,8,32,256]{3,2,1,0:T(8,128)(2,1)} %all-to-all-done.8.refs_3_, ...), custom_call_target="tpu_custom_call" | custom-call | tf_op jit(solution)/shard_map/product_3/pallas_call | solution.py:256
  232.8 20.8 %all_to_all.62 = f32[256,1,128]{2,1,0:T(1,128)S(1)} all-to-all(f32[256,1,128]{2,1,0:T(1,128)S(1)} %broadcast_in_dim.17), channel_id=1, replica_groups=mesh['term'=8,'sector'=32] {'term','sector'}, dimensions={0} | all-to-all | bytes 262144 | tf_op jit(solution)/shard_map/all_to_all | solution.py:15
  (58 shorter events, 18.8 us)
Async XLA Ops:
  0.6 41.0 %copy-start = (bf16[8,256,256]{2,1,0:T(8,128)(2,1)S(1)}, bf16[8,256,256]{2,1,0:T(8,128)(2,1)}, u32[]{:S(2)}) copy-start(bf16[8,256,256]{2,1,0:T(8,128)(2,1)} %param.11) | copy-start | bytes 3145732
  0.6 28.4 %copy-start.18 = (s32[2,8]{1,0:T(2,128)S(1)}, s32[2,8]{1,0:T(2,128)}, u32[]{:S(2)}) copy-start(s32[2,8]{1,0:T(2,128)} %refs_1_.5) | copy-start | bytes 196
  0.7 16.7 %copy-start.21 = (s32[3,8]{1,0:T(4,128)S(1)}, s32[3,8]{1,0:T(4,128)}, u32[]{:S(2)}) copy-start(s32[3,8]{1,0:T(4,128)} %param.9) | copy-start | bytes 292
  0.7 1.3 copy-start.16
  2.0 0.7 copy-start.17
  3.6 7.2 %collective-permute-start = (bf16[8,32,256]{2,1,0:T(8,128)(2,1)S(1)}, bf16[8,32,256]{2,1,0:T(8,128)(2,1)S(1)}, u32[]{:S(2)}, u32[]{:S(2)}) collective-permute-start(bf16[8,32,256]{2,1,0:T(8,128)(2,1)S(1)} %dynamic-slice_bitcast_fusion.refs_1_.refs_2_), channel_id=1, source_target_pairs={{1,2},{3,4},{5,6},{7,8},{9,10},{11,12},{13,14},{15,16},{17,18},{19... | collective-permute-start | bytes 393224 | tf_op jit(solution)/shard_map/ppermute | solution.py:20
  11.9 17.1 %all-to-all-start = ((bf16[8,8,32,256]{3,2,1,0:T(8,128)(2,1)}), bf16[8,8,32,256]{3,2,1,0:T(8,128)(2,1)S(1)}, u32[]{:S(2)}, u32[]{:S(2)}) async-start(bf16[8,8,32,256]{3,2,1,0:T(8,128)(2,1)} %broadcast_in_dim.12), calls=%async_computation | async-start | bytes 2097152 | tf_op jit(solution)/shard_map/all_to_all | solution.py:15
  17.3 2.8 %collective-permute-start.1 = (bf16[8,8,32,256]{3,2,1,0:T(8,128)(2,1)S(1)}, bf16[8,8,32,256]{3,2,1,0:T(8,128)(2,1)}, u32[]{:S(2)}, u32[]{:S(2)}) collective-permute-start(bf16[8,8,32,256]{3,2,1,0:T(8,128)(2,1)S(1)} %start.1.refs_3_.refs_5_), channel_id=1, source_target_pairs={{0,1},{2,3},{4,5},{6,7},{8,9},{10,11},{12,13},{14,15},{16,17},{18,... | collective-permute-start | bytes 3145736 | tf_op jit(solution)/shard_map/ppermute | solution.py:20
  29.0 1.9 copy-start.1
  30.9 1.9 copy-start.4
  37.1 1.0 copy-start.7
  38.1 18.0 %all-to-all-start.1 = ((bf16[8,8,32,256]{3,2,1,0:T(8,128)(2,1)}), bf16[8,8,32,256]{3,2,1,0:T(8,128)(2,1)S(1)}, u32[]{:S(2)}, u32[]{:S(2)}) async-start(bf16[8,8,32,256]{3,2,1,0:T(8,128)(2,1)} %copy-done.7), calls=%async_computation.1 | async-start | bytes 2097152 | tf_op jit(solution)/shard_map/all_to_all | solution.py:322
  56.5 30.5 %copy-start.8 = (f32[8,32,256]{2,1,0:T(8,128)}, f32[8,32,256]{2,1,0:T(8,128)S(1)}, u32[]{:S(2)}) copy-start(f32[8,32,256]{2,1,0:T(8,128)S(1)} %get-tuple-element.17.refs_3_.refs_4_) | copy-start | bytes 786436
  87.5 0.7 copy-start.12
  88.2 1.0 copy-start.15
  89.8 20.2 %all-to-all-start.4 = ((bf16[8,8,32,256]{3,2,1,0:T(8,128)(2,1)}), bf16[8,8,32,256]{3,2,1,0:T(8,128)(2,1)S(1)}, u32[]{:S(2)}, u32[]{:S(2)}) async-start(bf16[8,8,32,256]{3,2,1,0:T(8,128)(2,1)} %copy-done.15), calls=%async_computation.4 | async-start | bytes 2097152 | tf_op jit(solution)/shard_map/all_to_all | solution.py:322
  93.4 6.8 %collective-permute-start.2 = (bf16[8,32,256]{2,1,0:T(8,128)(2,1)}, bf16[8,32,256]{2,1,0:T(8,128)(2,1)}, u32[]{:S(2)}, u32[]{:S(2)}) collective-permute-start(bf16[8,32,256]{2,1,0:T(8,128)(2,1)} %copy-done.20), channel_id=1, source_target_pairs={{1,2},{3,4},{5,6},{7,8},{9,10},{11,12},{13,14},{15,16},{17,18},{19... | collective-permute-start | bytes 393224 | tf_op jit(solution)/shard_map/ppermute | solution.py:20
  112.1 18.3 %all-to-all-start.3 = ((bf16[8,8,32,256]{3,2,1,0:T(8,128)(2,1)}), bf16[8,8,32,256]{3,2,1,0:T(8,128)(2,1)}, u32[]{:S(2)}, u32[]{:S(2)}) async-start(bf16[8,8,32,256]{3,2,1,0:T(8,128)(2,1)} %broadcast_in_dim.14), calls=%async_computation.3 | async-start | bytes 2097152 | tf_op jit(solution)/shard_map/all_to_all | solution.py:15
  116.3 14.1 %collective-permute-start.3 = (bf16[8,8,32,256]{3,2,1,0:T(8,128)(2,1)S(1)}, bf16[8,8,32,256]{3,2,1,0:T(8,128)(2,1)}, u32[]{:S(2)}, u32[]{:S(2)}) collective-permute-start(bf16[8,8,32,256]{3,2,1,0:T(8,128)(2,1)S(1)} %all-to-all-done.4.refs_3_.refs_6_), channel_id=1, source_target_pairs={{0,1},{2,3},{4,5},{6,7},{8,9},{10,11},{12,13},{14,15},{16,17},{18,... | collective-permute-start | bytes 3145736 | tf_op jit(solution)/shard_map/ppermute | solution.py:20
  130.4 1.9 copy-start.2
  132.3 1.9 copy-start.5
  134.2 23.1 %copy-start.9 = (f32[8,32,256]{2,1,0:T(8,128)S(1)}, f32[8,32,256]{2,1,0:T(8,128)}, u32[]{:S(2)}) copy-start(f32[8,32,256]{2,1,0:T(8,128)} %copy-done.8) | copy-start | bytes 786436
  134.2 23.1 %copy-start.13 = (f32[8,32,256]{2,1,0:T(8,128)S(1)}, f32[8,32,256]{2,1,0:T(8,128)}, u32[]{:S(2)}) copy-start(f32[8,32,256]{2,1,0:T(8,128)} %copy-done.12) | copy-start | bytes 786436
  178.5 1.4 copy-start.10
  179.9 1.0 copy-start.14
  181.5 21.0 %all-to-all-start.8 = ((bf16[8,8,32,256]{3,2,1,0:T(8,128)(2,1)}), bf16[8,8,32,256]{3,2,1,0:T(8,128)(2,1)}, u32[]{:S(2)}, u32[]{:S(2)}) async-start(bf16[8,8,32,256]{3,2,1,0:T(8,128)(2,1)} %copy-done.14), calls=%async_computation.8 | async-start | bytes 2097152 | tf_op jit(solution)/shard_map/all_to_all | solution.py:322
  185.8 6.9 %collective-permute-start.4 = (bf16[8,32,256]{2,1,0:T(8,128)(2,1)}, bf16[8,32,256]{2,1,0:T(8,128)(2,1)S(1)}, u32[]{:S(2)}, u32[]{:S(2)}) collective-permute-start(bf16[8,32,256]{2,1,0:T(8,128)(2,1)} %copy-done.19), channel_id=1, source_target_pairs={{1,2},{3,4},{5,6},{7,8},{9,10},{11,12},{13,14},{15,16},{17,18},{19... | collective-permute-start | bytes 393224 | tf_op jit(solution)/shard_map/ppermute | solution.py:20
  203.6 18.3 %all-to-all-start.7 = ((bf16[8,8,32,256]{3,2,1,0:T(8,128)(2,1)}), bf16[8,8,32,256]{3,2,1,0:T(8,128)(2,1)}, u32[]{:S(2)}, u32[]{:S(2)}) async-start(bf16[8,8,32,256]{3,2,1,0:T(8,128)(2,1)} %broadcast_in_dim.16), calls=%async_computation.7 | async-start | bytes 2097152 | tf_op jit(solution)/shard_map/all_to_all | solution.py:15
  207.9 14.1 %collective-permute-start.5 = (bf16[8,8,32,256]{3,2,1,0:T(8,128)(2,1)}, bf16[8,8,32,256]{3,2,1,0:T(8,128)(2,1)}, u32[]{:S(2)}, u32[]{:S(2)}) collective-permute-start(bf16[8,8,32,256]{3,2,1,0:T(8,128)(2,1)} %all-to-all-done.8.refs_3_), channel_id=1, source_target_pairs={{0,1},{2,3},{4,5},{6,7},{8,9},{10,11},{12,13},{14,15},{16,17},{18,... | collective-permute-start | bytes 3145736 | tf_op jit(solution)/shard_map/ppermute | solution.py:20
  222.0 1.9 copy-start.3
  223.9 1.9 copy-start.6
  225.8 27.9 %copy-start.11 = (f32[256,1,128]{2,1,0:T(1,128)S(1)}, f32[256,1,128]{2,1,0:T(1,128)}, u32[]{:S(2)}) copy-start(f32[256,1,128]{2,1,0:T(1,128)} %copy-done.10) | copy-start | bytes 393220
  (2 other events, 1.3 us)

commit v3 on v2

v3 whole, which is shorter than its diff:
```python
import jax
import jax.numpy as jnp
from jax import lax
from jax.experimental import pallas as pl
from jax.experimental.pallas import tpu as pltpu
from jax.sharding import PartitionSpec as P

epsilon = 1e-06
f32 = jnp.float32
bf16 = jnp.bfloat16


def to_everyone(x, axis):
    devices = lax.axis_size(axis)
    return lax.all_to_all(jnp.broadcast_to(x[None], (devices, *x.shape)), axis, 0, 0, tiled=True)


def swapped(block, first):
    pairs = [(i, i + 1) for i in range(first, lax.axis_size("sector") - 1, 2)]
    return lax.ppermute(block, "sector", pairs + [(j, i) for i, j in pairs])


def row_of(total_ref, entries):
    return jnp.sum(total_ref[...], axis=0, keepdims=True) * (1.0 / entries)


def one(row, k):
    return row[:, k : k + 1]


def first_scale(row1):
    return 1.0 / jnp.sqrt(one(row1, 6) + epsilon)


def second_weights(row1):
    inv = first_scale(row1)
    theta, a, b, aa, ab, bb, vv = (inv * inv * one(row1, k) for k in range(7))
    o = a - theta * b
    length = aa + theta * theta * bb + o * o * vv - 2.0 * theta * ab - 2.0 * o * a + 2.0 * theta * o * b
    r = 1.0 / jnp.sqrt(jnp.maximum(length, 0.0) + epsilon)
    return r * inv, -r * theta * inv, -r * o * inv


def third_weights(row1, row2):
    inv = first_scale(row1)
    theta = one(row2, 0)
    v1a = inv * one(row2, 1)
    v1b = inv * one(row2, 2)
    v2a = one(row2, 3)
    v2b = one(row2, 4)
    aa = one(row2, 5)
    ab = one(row2, 6)
    bb = one(row2, 7)
    v1v2 = inv * one(row2, 8)
    v2v2 = one(row2, 9)
    v1v1 = inv * inv * one(row1, 6)
    o1 = v1a - theta * v1b
    o2 = v2a - theta * v2b
    length = (
        aa
        - 2.0 * theta * ab
        + theta * theta * bb
        - 2.0 * o1 * o1
        - 2.0 * o2 * o2
        + o1 * o1 * v1v1
        + 2.0 * o1 * o2 * v1v2
        + o2 * o2 * v2v2
    )
    r = 1.0 / jnp.sqrt(jnp.maximum(length, 0.0) + epsilon)
    return r, -r * theta, -r * o1 * inv, -r * o2


def fold(x):
    return jnp.sum(x.reshape(x.shape[0] // 8, 8, x.shape[1]), axis=0)


def row_from(sums):
    lane = lax.broadcasted_iota(jnp.int32, (1, 128), 1)
    row = jnp.zeros((1, 128), f32)
    for k, total in enumerate(sums):
        row = row + jnp.where(lane == k, jnp.sum(total), 0.0)
    return row


def keep_of(dims_ref, s, width):
    rows = lax.broadcasted_iota(jnp.int32, (width, width), 0)
    cols = lax.broadcasted_iota(jnp.int32, (width, width), 1)
    return (rows < dims_ref[0, s]) & (cols < dims_ref[1, s])


def masked(x, dims_ref, s, first):
    rows = lax.broadcasted_iota(jnp.int32, x.shape, 0)
    cols = lax.broadcasted_iota(jnp.int32, x.shape, 1)
    keep = (rows < dims_ref[0, s] - first) & (cols < dims_ref[1, s])
    return jnp.where(keep, x.astype(f32), 0.0).astype(bf16)


def share_kernel(dims_ref, psi_ref, d_ref, shares_ref, buf_ref, sem):
    blocks, share = buf_ref.shape[1:3]
    first = lax.axis_index("term") * share
    mine = pl.ds(pl.multiple_of(first, share), share)
    copies = [pltpu.make_async_copy(x.at[:, mine], buf_ref.at[k], sem.at[k]) for k, x in enumerate((psi_ref, d_ref))]
    for copy in copies:
        copy.start()
    for copy in copies:
        copy.wait()
    for s in range(blocks):
        buf_ref[0, s] = masked(buf_ref[0, s], dims_ref, s, first)
    copy = pltpu.make_async_copy(buf_ref, shares_ref, sem.at[2])
    copy.start()
    copy.wait()


def start_kernel(dims_ref, psi_ref, out_ref):
    pieces, blocks, share = out_ref.shape[:3]

    def body(s, carry):
        for p in range(pieces):
            out_ref[p, s] = masked(psi_ref[s, pl.ds(p * share, share)], dims_ref, s, p * share)
        return carry

    lax.fori_loop(0, blocks, body, 0)


def reduce_kernel(stage, arrived_ref, shares_ref, *refs):
    if stage > 1:
        sig1_ref, v2_ref, refs = refs[0], refs[1], refs[2:]
    mine_ref, send_ref, row_ref, sem = refs
    pieces, blocks, share, width = arrived_ref.shape

    def body(s, acc):
        sig = arrived_ref[0, s].astype(f32)
        for p in range(1, pieces):
            sig = sig + arrived_ref[p, s].astype(f32)
        mine_ref[s] = sig
        psi = shares_ref[0, s].astype(f32)
        rd = 1.0 / shares_ref[1, s].astype(f32)
        a = sig * rd
        if stage == 1:
            b = psi * rd
            terms = (psi * sig, psi * a, psi * b, a * a, a * b, b * b, psi * psi)
        else:
            v2 = v2_ref[s]
            b = v2 * rd
            terms = (
                v2 * sig,
                psi * a,
                psi * b,
                v2 * a,
                v2 * b,
                a * a,
                a * b,
                b * b,
                psi * v2,
                v2 * v2,
                psi * sig,
                v2 * sig1_ref[s],
            )
        return tuple(t + fold(x) for t, x in zip(acc, terms))

    acc = lax.fori_loop(0, blocks, body, (jnp.zeros((8, width), f32),) * (7 if stage == 1 else 12))
    copy = pltpu.make_async_copy(mine_ref, send_ref, sem)
    copy.start()
    row_ref[...] = row_from(acc)
    copy.wait()


def update_kernel(stage, entries, *refs):
    tots, refs = refs[:stage], refs[stage:]
    per = 2 if stage == 1 else 4
    groups, refs = (refs[:per], refs[per : 2 * per]), refs[2 * per :]
    v_refs, refs = refs[:2], refs[2:]
    if stage > 1:
        row_ref, refs = refs[0], refs[1:]
    all_ref, buf_ref, sem = refs
    pieces, _, blocks, share, width = all_ref.shape
    rows = [row_of(t, entries) for t in tots]
    if stage == 1:
        p, q, w = (x[0, 0] for x in second_weights(*rows))
    else:
        p, q, w, y = (x[0, 0] for x in third_weights(*rows))
    copies = []
    for g in range(2):

        def body(s, acc, g=g):
            psi = groups[g][0][0, s].astype(f32)
            rd = 1.0 / groups[g][0][1, s].astype(f32)
            sig1 = groups[g][1][s]
            if stage == 1:
                v = (p * sig1 + q * psi) * rd + w * psi
            else:
                sig2, v2 = groups[g][2][s], groups[g][3][s]
                v = (p * sig2 + q * v2) * rd + w * psi + y * v2
                acc = acc[0] + fold(v * sig1), acc[1] + fold(v * sig2)
            v_refs[g][s] = v
            buf_ref[g, s] = v.astype(bf16)
            return acc

        acc = lax.fori_loop(0, blocks, body, (jnp.zeros((8, width), f32),) * (0 if stage == 1 else 2))
        if stage > 1 and g == 0:
            zero = jnp.zeros((8, width), f32)
            row_ref[...] = row_from([zero, zero, zero, *acc])
        for k in range(pieces):
            copies.append(pltpu.make_async_copy(buf_ref.at[g], all_ref.at[k, g], sem.at[g, k]))
            copies[-1].start()
    for copy in copies:
        copy.wait()


def dot(a, b, ca, cb):
    return lax.dot_general(a, b, (((ca,), (cb,)), ((), ())), preferred_element_type=f32)


together = 2


def product_kernel(stage, *refs):
    conn_ref, dims_ref, groups, refs = refs[0], refs[1], refs[2 : 4 + (stage == 1)], refs[4 + (stage == 1) :]
    if stage == 1:
        far_ref, own_ref, near_ref = groups
    else:
        own_ref, far_ref, near_ref = groups[0].at[:, 0], groups[0].at[:, 1], groups[1]
    if stage == 3:
        psi_ref, v2_ref, part_ref, refs = refs[0], refs[1], refs[2], refs[3:]
    sources = refs[: 1 if stage == 4 else 2]
    refs = refs[len(sources) :]
    out_ref, vb_ref = refs[:2]
    sides = sources
    incoming = []
    if stage == 1:
        right_ref, in_sem = refs[2:4]
        for g in range(right_ref.shape[1] // together):
            at = pl.ds(g * together, together)
            incoming.append(pltpu.make_async_copy(sources[1].at[:, at], right_ref.at[:, at], in_sem.at[g]))
        sides = (sources[0], right_ref)
    for copy in incoming:
        copy.start()
    if stage != 3:
        buf_ref, out_sem = refs[-2:]
    pieces, blocks, share, width = own_ref.shape
    terms = sources[0].shape[0]
    steps = blocks // together
    def body(s, carry):
        for seg, ref in enumerate((far_ref, own_ref, near_ref)):
            vb_ref[seg * blocks + s] = ref[:, s].reshape(width, width)
        return carry

    lax.fori_loop(0, blocks, body, 0)
    outgoing = []
    sums = [jnp.zeros((8, width), f32)] * 3
    for g in range(steps):
        here = range(g * together, (g + 1) * together)
        halves = {
            s: [dot(sides[0][t, s], vb_ref[conn_ref[t, s]], 1, 0).astype(bf16) for t in range(terms)] for s in here
        }
        if incoming:
            incoming[g].wait()
        for s in here:
            if stage == 4:
                own_t = vb_ref[blocks + s].T
                for t in range(terms):
                    buf_ref[t, s] = (dot(own_t, halves[s][t], 1, 0) * width ** (-0.5)).astype(bf16)
                continue
            side = jnp.concatenate([sides[1][t, s] for t in range(terms)], axis=1)
            total = dot(jnp.concatenate(halves[s], axis=1), side, 1, 1)
            if stage < 3:
                total = jnp.where(keep_of(dims_ref, s, width), total, 0.0).astype(bf16)
                buf_ref[:, s] = total.reshape(pieces, share, width)
            else:
                for p in range(pieces):
                    part = total[p * share : (p + 1) * share]
                    for k, x in enumerate((psi_ref[p, s], v2_ref[p, 0, s], own_ref[p, s])):
                        sums[k] = sums[k] + fold(x.astype(f32) * part)
        if stage != 3:
            at = pl.ds(g * together, together)
            outgoing.append(pltpu.make_async_copy(buf_ref.at[:, at], out_ref.at[:, at], out_sem.at[g]))
            outgoing[-1].start()
    for copy in outgoing:
        copy.wait()
    if stage == 3:
        out_ref[...] = row_from(sums) + part_ref[...]


def product(stage, conn, dims, groups, more, *sides):
    terms, blocks, width = sides[0].shape[:3]
    pieces, share = groups[-1].shape[0], groups[-1].shape[2]
    smem = pl.BlockSpec(memory_space=pltpu.SMEM)
    vmem = pl.BlockSpec(memory_space=pltpu.VMEM)
    hbm = pl.BlockSpec(memory_space=pltpu.HBM)
    steps = blocks // together
    scratch = [pltpu.VMEM((3 * blocks, width, width), bf16)]
    if stage == 1:
        scratch += [pltpu.VMEM(sides[1].shape, bf16), pltpu.SemaphoreType.DMA((steps,))]
    if stage == 3:
        out_shape, out_specs = jax.ShapeDtypeStruct((1, 128), f32), vmem
    else:
        shape = sides[0].shape if stage == 4 else (pieces, blocks, share, width)
        out_shape, out_specs = pltpu.HBM(shape, bf16), hbm
        scratch += [pltpu.VMEM(shape, bf16), pltpu.SemaphoreType.DMA((steps,))]
    return pl.pallas_call(
        lambda *refs: product_kernel(stage, *refs),
        in_specs=[smem, smem] + [vmem] * (len(groups) + len(more) + len(sides) - (stage == 1)) + [hbm] * (stage == 1),
        out_specs=out_specs,
        out_shape=out_shape,
        scratch_shapes=scratch,
        name=f"product_{stage}",
        compiler_params=pltpu.CompilerParams(vmem_limit_bytes=12 << 20),
    )(conn, dims, *groups, *more, *sides)


def keep_kernel(here_ref, there_ref, sem):
    copies = [pltpu.make_async_copy(here_ref.at[t], there_ref.at[t], sem.at[t]) for t in range(here_ref.shape[0])]
    for copy in copies:
        copy.start()
    for copy in copies:
        copy.wait()


def kept(x):
    return pl.pallas_call(
        keep_kernel,
        in_specs=[pl.BlockSpec(memory_space=pltpu.HBM)],
        out_specs=pl.BlockSpec(memory_space=pltpu.VMEM),
        out_shape=pltpu.VMEM(x.shape, x.dtype),
        scratch_shapes=[pltpu.SemaphoreType.DMA((x.shape[0],))],
        name="keep",
        compiler_params=pltpu.CompilerParams(vmem_limit_bytes=1 << 20),
    )(pltpu.with_memory_space_constraint(x, pltpu.HBM))


def call_small(kernel, dims, arrays, out_shape, name, sent=None, scratch=()):
    smem = pl.BlockSpec(memory_space=pltpu.SMEM)
    vmem = pl.BlockSpec(memory_space=pltpu.VMEM)
    out_specs = jax.tree.map(lambda _: vmem, out_shape)
    if sent is not None:
        out_specs = tuple(pl.BlockSpec(memory_space=pltpu.HBM) if k == sent else x for k, x in enumerate(out_specs))
    return pl.pallas_call(
        kernel,
        in_specs=[smem] * len(dims) + [vmem] * len(arrays),
        out_specs=out_specs,
        out_shape=out_shape,
        scratch_shapes=scratch,
        name=name,
        compiler_params=pltpu.CompilerParams(vmem_limit_bytes=8 << 20),
    )(*dims, *arrays)


def last_kernel(entries, tot1, tot2, tot3, out_ref):
    r1, r2, r3 = (row_of(t, entries) for t in (tot1, tot2, tot3))
    inv = first_scale(r1)
    values = (
        (inv * inv * one(r1, 0), inv * one(r2, 10), inv * one(r3, 0)),
        (inv * one(r2, 11), one(r2, 0), one(r3, 1)),
        (inv * one(r3, 3), one(r3, 4), one(r3, 2)),
    )
    row = lax.broadcasted_iota(jnp.int32, (3, 3), 0)
    col = lax.broadcasted_iota(jnp.int32, (3, 3), 1)
    out = jnp.zeros((3, 3), f32)
    for i in range(3):
        for j in range(3):
            out = jnp.where((row == i) & (col == j), values[i][j], out)
    out_ref[...] = out


def on_device(psi_start, left_env, right_env, connect, sector_dims, precond):
    blocks, width = psi_start.shape[:2]
    devices = lax.axis_size("sector")
    pieces = lax.axis_size("term")
    share = width // pieces
    entries = float(blocks * devices * width * width)
    everyone = ("term", "sector")
    row = jax.ShapeDtypeStruct((1, 128), f32)
    cut = jax.ShapeDtypeStruct((pieces, blocks, share, width), bf16)
    part = jax.ShapeDtypeStruct((blocks, share, width), f32)
    place = lax.axis_index("sector")
    conn = connect - (place * blocks - blocks)
    turned = (2 - conn // blocks) * blocks + conn % blocks
    conn = jnp.where(place % 2 == 1, turned, conn)

    def exchange(x):
        return lax.all_to_all(x, "term", 0, 0, tiled=True)

    def reduced(stage, partial, *shares):
        mine, sent, sums = call_small(
            lambda *refs: reduce_kernel(stage, *refs),
            [],
            [exchange(partial), *shares],
            (part, pltpu.HBM(part.shape, f32), row),
            f"reduce_{stage}",
            1,
            [pltpu.SemaphoreType.DMA],
        )
        sums = jnp.broadcast_to(sums, (pieces * devices, 128))
        sums, sent = lax.optimization_barrier((sums, sent))
        return (mine, swapped(sent, 1)), lax.all_to_all(sums, everyone, 0, 0, tiled=True)

    def updated(stage, tots, own, far):
        out = (part, part) + ((row,) if stage > 1 else ())
        every = pltpu.HBM((pieces, 2, blocks, share, width), bf16)
        v, v_far, *more, every = call_small(
            lambda *refs: update_kernel(stage, entries, *refs),
            [],
            [*tots, *own, *far],
            (*out, every),
            f"update_{stage}",
            len(out),
            [pltpu.VMEM((2, blocks, share, width), bf16), pltpu.SemaphoreType.DMA((2, pieces))],
        )
        both = exchange(every)
        return (v, v_far), (both, swapped(both[:, 0], 0)), more

    hbm = pl.BlockSpec(memory_space=pltpu.HBM)
    shares = pl.pallas_call(
        share_kernel,
        in_specs=[pl.BlockSpec(memory_space=pltpu.SMEM), hbm, hbm],
        out_specs=hbm,
        out_shape=pltpu.HBM((2, blocks, share, width), bf16),
        scratch_shapes=[pltpu.VMEM((2, blocks, share, width), bf16), pltpu.SemaphoreType.DMA((3,))],
        name="share",
        compiler_params=pltpu.CompilerParams(vmem_limit_bytes=4 << 20),
    )(
        sector_dims,
        pltpu.with_memory_space_constraint(psi_start, pltpu.HBM),
        pltpu.with_memory_space_constraint(precond, pltpu.HBM),
    )
    psi = call_small(start_kernel, [sector_dims], [psi_start], cut, "start")
    far = swapped(shares, 1)
    left_env = kept(left_env)

    groups = (to_everyone(far[0], "term"), psi, swapped(psi, 0))
    partial = product(1, conn, sector_dims, groups, (), left_env, pltpu.with_memory_space_constraint(right_env, pltpu.HBM))
    sig1, tot1 = reduced(1, partial, shares)
    v2, groups2, _ = updated(1, (tot1,), (shares, sig1[0]), (far, sig1[1]))

    partial = product(2, conn, sector_dims, groups2, (), left_env, right_env)
    sig2, tot2 = reduced(2, partial, shares, sig1[0], v2[0])
    v3, groups3, (more,) = updated(2, (tot1, tot2), (shares, sig1[0], sig2[0], v2[0]), (far, sig1[1], sig2[1], v2[1]))

    row3 = product(3, conn, sector_dims, groups3, (psi, groups2[0], more), left_env, right_env)
    tot3 = to_everyone(row3[0], everyone)
    env = product(4, conn, sector_dims, groups3, (), left_env)
    projected = call_small(
        lambda *refs: last_kernel(entries, *refs), [], [tot1, tot2, tot3], jax.ShapeDtypeStruct((3, 3), f32), "last"
    )
    return (projected, v3[0], env)


def solution(mesh):
    placed = (
        P("sector", None, None),
        P("term", "sector", None, None),
        P("term", "sector", None, None),
        P("term", "sector"),
        P(None, "sector"),
        P("sector", None, None),
    )
    return jax.shard_map(
        on_device,
        mesh=mesh,
        in_specs=placed,
        out_specs=(P(), P("sector", "term", None), P("term", "sector", None, None)),
        check_vma=False,
    )
```

time: 255 us -> 233 us (0.914)
  waiting for transfers between devices: 82.6 us -> 23.5 us
  blocking collectives: 90.2 us -> 138 us
  local copies, waits for them, and re-layouts: 22.7 us -> 5.5 us
  Pallas kernels: 20.5 us -> 30.8 us
  starting transfers between devices: 37.5 us -> 33.2 us
    all_to_all x1 -> x4, blocking collectives: 18.5 us -> 95.1 us  [exchange(): return lax.all_to_all(x, 'term', 0, 0, tiled=True)]
    all_to_all x3 -> x0, waiting for transfers between devices: 34.1 us -> none  [exchange(): return lax.all_to_all(x, 'term', 0, 0, tiled=True)]
    all_to_all x3 -> x2, blocking collectives: 71.8 us -> 43.2 us  [reduced(): lax.all_to_all(sums, everyone, 0, 0, tiled=True)]
    all_to_all x3 -> x2, waiting for transfers between devices: 34.2 us -> 13.6 us  [to_everyone(): lax.all_to_all(jnp.broadcast_to(x[None], (devices, *x.shape)), axis, 0, 0...]
    unnamed x44 -> x24, local copies, waits for them, and re-layouts: 18.3 us -> 3.53 us
    all_to_all x3 -> x0, starting transfers between devices: 11.4 us -> none  [exchange(): return lax.all_to_all(x, 'term', 0, 0, tiled=True)]
    ppermute x6, starting transfers between devices: 12.3 us -> 22.4 us  [swapped(): return lax.ppermute(block, 'sector', pairs + [(j, i) for i, j in pairs])]
    pallas_call x3 -> x6, Pallas kernels: 15.9 us -> 21.3 us  [the longest x4 17.1 us: product(): pl.pallas_call(lambda *refs: product_kernel(stage, *refs), in_specs=[smem...]
  transfers between devices with their start and end apart: 12 -> 8, of which waited for: 10 -> 6; matrix products, arithmetic and copies ran while one was open for 0% -> 0% of each run, Pallas kernels for 0% -> 3%
where the time goes in v3:
time: 233 us; the launch traced here: 232 us
  blocking collectives  138 us (59%)
  starting transfers between devices  33.2 us (14%)
  Pallas kernels  30.8 us (13%)
  waiting for transfers between devices  23.5 us (10%)
  local copies, waits for them, and re-layouts  5.5 us (2%)
    all_to_all x4, blocking collectives, exchange(): return lax.all_to_all(x, 'term', 0, 0, tiled=True)  95.1 us
    all_to_all x2, blocking collectives, reduced(): lax.all_to_all(sums, everyone, 0, 0, tiled=True)  43.2 us
    ppermute x6, starting transfers between devices, swapped(): return lax.ppermute(block, 'sector', pairs + [(j, i) for i, j in pairs])  22.4 us
    pallas_call x4, Pallas kernels, product(): pl.pallas_call(lambda *refs: product_kernel(stage, *refs), in_specs=[smem...  17.1 us
    all_to_all x2, waiting for transfers between devices, to_everyone(): lax.all_to_all(jnp.broadcast_to(x[None], (devices, *x.shape)), axis, 0, 0...  13.6 us
    all_to_all x2, starting transfers between devices, to_everyone(): lax.all_to_all(jnp.broadcast_to(x[None], (devices, *x.shape)), axis, 0, 0...  10.8 us
    ppermute x6, waiting for transfers between devices, swapped(): return lax.ppermute(block, 'sector', pairs + [(j, i) for i, j in pairs])  9.89 us
    pallas_call x6, Pallas kernels, call_small(): pl.pallas_call(kernel, in_specs=[smem] * len(dims) + [vmem] * len(arrays)...  9.58 us
  transfers between devices with their start and end apart: 8, of which 6 were waited for; matrix products, arithmetic and copies ran while one was open for 0% of the time, Pallas kernels for 3%

profile of v3, /device:TPU:1, one launch (start us, length us, event | category | flops | bytes accessed | tf_op | source)
XLA Modules:
  0.0 232.2 jit_solution(5689795771163782510)
XLA Ops:
  1.3 2.3 share.1.refs_1_.refs_2_
  3.6 4.7 %collective-permute-start = (bf16[2,8,32,256]{3,2,1,0:T(8,128)(2,1)}, bf16[2,8,32,256]{3,2,1,0:T(8,128)(2,1)S(1)}, u32[]{:S(2)}, u32[]{:S(2)}) collective-permute-start(bf16[2,8,32,256]{3,2,1,0:T(8,128)(2,1)} %share.1.refs_1_.refs_2_), channel_id=1, source_target_pairs={{1,2},{3,4},{5,6},{7,8},{9,10},{11,12},{13,14},{15,16},{17,18},{19... | collective-permute-start | bytes 786440 | tf_op jit(solution)/shard_map/ppermute | solution.py:20
  8.4 4.3 %collective-permute-done.refs_3_.refs_6_ = bf16[2,8,32,256]{3,2,1,0:T(8,128)(2,1)S(1)} collective-permute-done((bf16[2,8,32,256]{3,2,1,0:T(8,128)(2,1)}, bf16[2,8,32,256]{3,2,1,0:T(8,128)(2,1)S(1)}, u32[]{:S(2)}, u32[]{:S(2)}) %collective-permute-start) | collective-permute-done | bytes 262176 | tf_op jit(solution)/shard_map/ppermute | solution.py:20
  12.6 1.1 broadcast_in_dim.27
  13.7 5.4 %all-to-all-start = ((bf16[8,8,32,256]{3,2,1,0:T(8,128)(2,1)}), bf16[8,8,32,256]{3,2,1,0:T(8,128)(2,1)}, u32[]{:S(2)}, u32[]{:S(2)}) async-start(bf16[8,8,32,256]{3,2,1,0:T(8,128)(2,1)} %broadcast_in_dim.27), calls=%async_computation | async-start | bytes 2097152 | tf_op jit(solution)/shard_map/all_to_all | solution.py:15
  19.1 1.9 start.1.refs_3_.refs_4_
  21.0 1.9 keep.1.refs_5_.refs_4_.refs_7_
  23.0 1.1 collective-permute-done.1.refs_4_
  24.0 6.8 %all-to-all-done.refs_2_ = bf16[8,8,32,256]{3,2,1,0:T(8,128)(2,1)} async-done(((bf16[8,8,32,256]{3,2,1,0:T(8,128)(2,1)}), bf16[8,8,32,256]{3,2,1,0:T(8,128)(2,1)}, u32[]{:S(2)}, u32[]{:S(2)}) %all-to-all-start) | async-done | bytes 1048608 | tf_op jit(solution)/shard_map/all_to_all | solution.py:15
  30.9 6.0 %product_1.1 = bf16[8,8,32,256]{3,2,1,0:T(8,128)(2,1)} custom-call(s32[3,8]{1,0:T(4,128)S(1)} %fusion.3.refs_0_, s32[2,8]{1,0:T(2,128)S(1)} %copy-done.10, bf16[8,8,32,256]{3,2,1,0:T(8,128)(2,1)} %all-to-all-done.refs_2_, bf16[8,8,32,256]{3,2,1,0:T(8,128)(2,1)} %start.1.refs_3_.refs_4_, bf16[8,8,32,256]{3,2,1,0:T(8,128)(2,1)} %collective-permute-done.1.refs_4_, ...), custom_call_target="tpu_custom_call" | custom-call | tf_op jit(solution)/shard_map/product_1/pallas_call | solution.py:300
  36.9 16.4 %all_to_all.55.refs_0_ = bf16[8,8,32,256]{3,2,1,0:T(8,128)(2,1)S(1)} all-to-all(bf16[8,8,32,256]{3,2,1,0:T(8,128)(2,1)} %product_1.1), channel_id=1, replica_groups=mesh['term'=8,'sector'=32] {'term'}, dimensions={0} | all-to-all | bytes 2097152 | tf_op jit(solution)/shard_map/all_to_all | solution.py:381
  54.4 10.6 %collective-permute-start.2 = (f32[8,32,256]{2,1,0:T(8,128)}, f32[8,32,256]{2,1,0:T(8,128)S(1)}, u32[]{:S(2)}, u32[]{:S(2)}) collective-permute-start(f32[8,32,256]{2,1,0:T(8,128)} %get-tuple-element.23), channel_id=1, source_target_pairs={{1,2},{3,4},{5,6},{7,8},{9,10},{11,12},{13,14},{15,16},{17,18},{19... | collective-permute-start | bytes 786440 | tf_op jit(solution)/shard_map/ppermute | solution.py:20
  65.0 23.6 %all_to_all.56 = f32[256,1,128]{2,1,0:T(1,128)S(1)} all-to-all(f32[256,1,128]{2,1,0:T(1,128)S(1)} %bitcast.25), channel_id=1, replica_groups=mesh['term'=8,'sector'=32] {'term','sector'}, dimensions={0} | all-to-all | bytes 262144 | tf_op jit(solution)/shard_map/all_to_all | solution.py:395
  88.6 1.8 update_1.1
  90.5 30.0 %all_to_all.57.refs_2_.refs_5_ = bf16[8,2,8,32,256]{4,3,2,1,0:T(8,128)(2,1)S(1)} all-to-all(bf16[8,2,8,32,256]{4,3,2,1,0:T(8,128)(2,1)} %get-tuple-element.24), channel_id=1, replica_groups=mesh['term'=8,'sector'=32] {'term'}, dimensions={0} | all-to-all | bytes 4194304 | tf_op jit(solution)/shard_map/all_to_all | solution.py:381
  120.6 1.7 collective-permute-start.3
  122.3 2.3 collective-permute-done.3.refs_3_
  124.6 3.4 %product_2.1 = bf16[8,8,32,256]{3,2,1,0:T(8,128)(2,1)} custom-call(s32[3,8]{1,0:T(4,128)S(1)} %fusion.3.refs_0_, s32[2,8]{1,0:T(2,128)S(1)} %copy-done.10, bf16[8,2,8,32,256]{4,3,2,1,0:T(8,128)(2,1)S(1)} %all_to_all.57.refs_2_.refs_5_, bf16[8,8,32,256]{3,2,1,0:T(8,128)(2,1)S(1)} %collective-permute-done.3.refs_3_, ...), custom_call_target="tpu_custom_call" | custom-call | tf_op jit(solution)/shard_map/product_2/pallas_call | solution.py:300
  128.0 18.9 %all_to_all.58.refs_0_ = bf16[8,8,32,256]{3,2,1,0:T(8,128)(2,1)S(1)} all-to-all(bf16[8,8,32,256]{3,2,1,0:T(8,128)(2,1)} %product_2.1), channel_id=1, replica_groups=mesh['term'=8,'sector'=32] {'term'}, dimensions={0} | all-to-all | bytes 2097152 | tf_op jit(solution)/shard_map/all_to_all | solution.py:381
  146.9 1.2 reduce_2.1
  148.1 3.4 %collective-permute-start.4 = (f32[8,32,256]{2,1,0:T(8,128)}, f32[8,32,256]{2,1,0:T(8,128)S(1)}, u32[]{:S(2)}, u32[]{:S(2)}) collective-permute-start(f32[8,32,256]{2,1,0:T(8,128)} %get-tuple-element.30), channel_id=1, source_target_pairs={{1,2},{3,4},{5,6},{7,8},{9,10},{11,12},{13,14},{15,16},{17,18},{19... | collective-permute-start | bytes 786440 | tf_op jit(solution)/shard_map/ppermute | solution.py:20
  151.5 19.6 %all_to_all.59 = f32[256,1,128]{2,1,0:T(1,128)S(1)} all-to-all(f32[256,1,128]{2,1,0:T(1,128)S(1)} %bitcast.26), channel_id=1, replica_groups=mesh['term'=8,'sector'=32] {'term','sector'}, dimensions={0} | all-to-all | bytes 262144 | tf_op jit(solution)/shard_map/all_to_all | solution.py:395
  171.1 2.8 %update_2.1 = (f32[8,32,256]{2,1,0:T(8,128)}, f32[8,32,256]{2,1,0:T(8,128)}, f32[1,128]{1,0:T(1,128)S(1)}, bf16[8,2,8,32,256]{4,3,2,1,0:T(8,128)(2,1)}) custom-call(f32[256,128]{1,0:T(8,128)S(1)} %bitcast.17, f32[256,128]{1,0:T(8,128)S(1)} %bitcast.19, bf16[2,8,32,256]{3,2,1,0:T(8,128)(2,1)S(1)} %copy-done.3, ...), custom_call_target="tpu_custom_call" | custom-call | tf_op jit(solution)/shard_map/update_2/pallas_call | solution.py:337
  174.0 29.8 %all_to_all.60.refs_2_ = bf16[8,2,8,32,256]{4,3,2,1,0:T(8,128)(2,1)S(1)} all-to-all(bf16[8,2,8,32,256]{4,3,2,1,0:T(8,128)(2,1)} %get-tuple-element.32), channel_id=1, replica_groups=mesh['term'=8,'sector'=32] {'term'}, dimensions={0} | all-to-all | bytes 4194304 | tf_op jit(solution)/shard_map/all_to_all | solution.py:381
  203.8 1.9 collective-permute-start.5
  205.7 2.3 collective-permute-done.5.refs_3_
  208.0 4.1 %product_3.1 = f32[1,128]{1,0:T(1,128)S(1)} custom-call(s32[3,8]{1,0:T(4,128)S(1)} %fusion.3.refs_0_, s32[2,8]{1,0:T(2,128)S(1)} %copy-done.10, bf16[8,2,8,32,256]{4,3,2,1,0:T(8,128)(2,1)S(1)} %all_to_all.60.refs_2_, bf16[8,8,32,256]{3,2,1,0:T(8,128)(2,1)S(1)} %collective-permute-done.5.refs_3_, bf16[8,8,32,256]{3,2,1,0:T(8,128)(2,1)} %start.1.refs_3_.refs_4_, ...), custom_call_target="tpu_custom_call" | custom-call | tf_op jit(solution)/shard_map/product_3/pallas_call | solution.py:300
  212.9 5.4 %all-to-all-start.7 = ((f32[256,1,128]{2,1,0:T(1,128)}), f32[256,1,128]{2,1,0:T(1,128)S(1)}, u32[]{:S(2)}, u32[]{:S(2)}) async-start(f32[256,1,128]{2,1,0:T(1,128)} %broadcast_in_dim.32), calls=%async_computation.7 | async-start | bytes 262144 | tf_op jit(solution)/shard_map/all_to_all | solution.py:15
  218.3 1.6 copy-done.2
  219.9 1.2 copy-done.6
  221.1 3.5 %product_4.1 = bf16[3,8,256,256]{3,2,1,0:T(8,128)(2,1)} custom-call(s32[3,8]{1,0:T(4,128)S(1)} %fusion.3.refs_0_, s32[2,8]{1,0:T(2,128)S(1)} %copy-done.10, bf16[8,2,8,32,256]{4,3,2,1,0:T(8,128)(2,1)S(1)} %copy-done.2, bf16[8,8,32,256]{3,2,1,0:T(8,128)(2,1)S(1)} %copy-done.6, bf16[3,8,256,256]{3,2,1,0:T(8,128)(2,1)S(1)} %keep.1.refs_5_.refs_4_.refs_7_), custom_call_target="tpu_custom_call" | custom-call | tf_op jit(solution)/shard_map/product_4/pallas_call | solution.py:300
  224.6 6.7 %all-to-all-done.7 = f32[256,1,128]{2,1,0:T(1,128)S(1)} async-done(((f32[256,1,128]{2,1,0:T(1,128)}), f32[256,1,128]{2,1,0:T(1,128)S(1)}, u32[]{:S(2)}, u32[]{:S(2)}) %all-to-all-start.7) | async-done | bytes 131104 | tf_op jit(solution)/shard_map/all_to_all | solution.py:15
  (34 shorter events, 3.5 us)
Async XLA Ops:
  0.6 0.7 copy-start.9
  3.6 15.5 %copy-start.4 = (bf16[8,256,256]{2,1,0:T(8,128)(2,1)S(1)}, bf16[8,256,256]{2,1,0:T(8,128)(2,1)}, u32[]{:S(2)}) copy-start(bf16[8,256,256]{2,1,0:T(8,128)(2,1)} %psi_ref.3) | copy-start | bytes 3145732
  3.6 15.5 %copy-start.10 = (s32[2,8]{1,0:T(2,128)S(1)}, s32[2,8]{1,0:T(2,128)}, u32[]{:S(2)}) copy-start(s32[2,8]{1,0:T(2,128)} %refs_1_.7) | copy-start | bytes 196
  3.6 9.0 %collective-permute-start = (bf16[2,8,32,256]{3,2,1,0:T(8,128)(2,1)}, bf16[2,8,32,256]{3,2,1,0:T(8,128)(2,1)S(1)}, u32[]{:S(2)}, u32[]{:S(2)}) collective-permute-start(bf16[2,8,32,256]{3,2,1,0:T(8,128)(2,1)} %share.1.refs_1_.refs_2_), channel_id=1, source_target_pairs={{1,2},{3,4},{5,6},{7,8},{9,10},{11,12},{13,14},{15,16},{17,18},{19... | collective-permute-start | bytes 786440 | tf_op jit(solution)/shard_map/ppermute | solution.py:20
  13.7 17.1 %all-to-all-start = ((bf16[8,8,32,256]{3,2,1,0:T(8,128)(2,1)}), bf16[8,8,32,256]{3,2,1,0:T(8,128)(2,1)}, u32[]{:S(2)}, u32[]{:S(2)}) async-start(bf16[8,8,32,256]{3,2,1,0:T(8,128)(2,1)} %broadcast_in_dim.27), calls=%async_computation | async-start | bytes 2097152 | tf_op jit(solution)/shard_map/all_to_all | solution.py:15
  21.0 3.0 %collective-permute-start.1 = (bf16[8,8,32,256]{3,2,1,0:T(8,128)(2,1)}, bf16[8,8,32,256]{3,2,1,0:T(8,128)(2,1)}, u32[]{:S(2)}, u32[]{:S(2)}) collective-permute-start(bf16[8,8,32,256]{3,2,1,0:T(8,128)(2,1)} %start.1.refs_3_.refs_4_), channel_id=1, source_target_pairs={{0,1},{2,3},{4,5},{6,7},{8,9},{10,11},{12,13},{14,15},{16,17},{18,... | collective-permute-start | bytes 3145736 | tf_op jit(solution)/shard_map/ppermute | solution.py:20
  21.0 1.9 copy-start.11
  36.9 16.4 %copy-start.3 = (bf16[2,8,32,256]{3,2,1,0:T(8,128)(2,1)S(1)}, bf16[2,8,32,256]{3,2,1,0:T(8,128)(2,1)}, u32[]{:S(2)}) copy-start(bf16[2,8,32,256]{3,2,1,0:T(8,128)(2,1)} %share.1.refs_1_.refs_2_) | copy-start | bytes 786436
  54.4 34.3 %collective-permute-start.2 = (f32[8,32,256]{2,1,0:T(8,128)}, f32[8,32,256]{2,1,0:T(8,128)S(1)}, u32[]{:S(2)}, u32[]{:S(2)}) collective-permute-start(f32[8,32,256]{2,1,0:T(8,128)} %get-tuple-element.23), channel_id=1, source_target_pairs={{1,2},{3,4},{5,6},{7,8},{9,10},{11,12},{13,14},{15,16},{17,18},{19... | collective-permute-start | bytes 786440 | tf_op jit(solution)/shard_map/ppermute | solution.py:20
  90.5 34.1 %copy-start = (bf16[3,8,256,256]{3,2,1,0:T(8,128)(2,1)S(1)}, bf16[3,8,256,256]{3,2,1,0:T(8,128)(2,1)}, u32[]{:S(2)}) copy-start(bf16[3,8,256,256]{3,2,1,0:T(8,128)(2,1)} %refs_8_.1) | copy-start | bytes 9437188
  120.6 4.0 %collective-permute-start.3 = (bf16[8,8,32,256]{3,2,1,0:T(8,128)(2,1)S(1)}, bf16[8,8,32,256]{3,2,1,0:T(8,128)(2,1)S(1)}, u32[]{:S(2)}, u32[]{:S(2)}) collective-permute-start(bf16[8,8,32,256]{3,2,1,0:T(8,128)(2,1)S(1)} %slice_bitcast_fusion.1), channel_id=1, source_target_pairs={{0,1},{2,3},{4,5},{6,7},{8,9},{10,11},{12,13},{14,15},{16,17},{18,... | collective-permute-start | bytes 3145736 | tf_op jit(solution)/shard_map/ppermute | solution.py:20
  148.1 23.0 %collective-permute-start.4 = (f32[8,32,256]{2,1,0:T(8,128)}, f32[8,32,256]{2,1,0:T(8,128)S(1)}, u32[]{:S(2)}, u32[]{:S(2)}) collective-permute-start(f32[8,32,256]{2,1,0:T(8,128)} %get-tuple-element.30), channel_id=1, source_target_pairs={{1,2},{3,4},{5,6},{7,8},{9,10},{11,12},{13,14},{15,16},{17,18},{19... | collective-permute-start | bytes 786440 | tf_op jit(solution)/shard_map/ppermute | solution.py:20
  171.1 2.9 %copy-start.7 = (f32[256,1,128]{2,1,0:T(1,128)}, f32[256,1,128]{2,1,0:T(1,128)S(1)}, u32[]{:S(2)}) copy-start(f32[256,1,128]{2,1,0:T(1,128)S(1)} %all_to_all.59) | copy-start | bytes 393220
  203.7 8.4 %copy-start.1 = (bf16[8,2,8,32,256]{4,3,2,1,0:T(8,128)(2,1)}, bf16[8,2,8,32,256]{4,3,2,1,0:T(8,128)(2,1)S(1)}, u32[]{:S(2)}) copy-start(bf16[8,2,8,32,256]{4,3,2,1,0:T(8,128)(2,1)S(1)} %all_to_all.60.refs_2_) | copy-start | bytes 6291460
  203.8 4.2 %collective-permute-start.5 = (bf16[8,8,32,256]{3,2,1,0:T(8,128)(2,1)S(1)}, bf16[8,8,32,256]{3,2,1,0:T(8,128)(2,1)S(1)}, u32[]{:S(2)}, u32[]{:S(2)}) collective-permute-start(bf16[8,8,32,256]{3,2,1,0:T(8,128)(2,1)S(1)} %slice_bitcast_fusion), channel_id=1, source_target_pairs={{0,1},{2,3},{4,5},{6,7},{8,9},{10,11},{12,13},{14,15},{16,17},{18,... | collective-permute-start | bytes 3145736 | tf_op jit(solution)/shard_map/ppermute | solution.py:20
  208.0 4.2 %copy-start.5 = (bf16[8,8,32,256]{3,2,1,0:T(8,128)(2,1)}, bf16[8,8,32,256]{3,2,1,0:T(8,128)(2,1)S(1)}, u32[]{:S(2)}) copy-start(bf16[8,8,32,256]{3,2,1,0:T(8,128)(2,1)S(1)} %collective-permute-done.5.refs_3_) | copy-start | bytes 3145732
  212.9 18.5 %all-to-all-start.7 = ((f32[256,1,128]{2,1,0:T(1,128)}), f32[256,1,128]{2,1,0:T(1,128)S(1)}, u32[]{:S(2)}, u32[]{:S(2)}) async-start(f32[256,1,128]{2,1,0:T(1,128)} %broadcast_in_dim.32), calls=%async_computation.7 | async-start | bytes 262144 | tf_op jit(solution)/shard_map/all_to_all | solution.py:15
  218.3 1.6 copy-start.2
  219.9 1.2 copy-start.6
  221.1 10.3 %copy-start.8 = (f32[256,1,128]{2,1,0:T(1,128)S(1)}, f32[256,1,128]{2,1,0:T(1,128)}, u32[]{:S(2)}) copy-start(f32[256,1,128]{2,1,0:T(1,128)} %copy-done.7) | copy-start | bytes 393220

commit v4 on v3

--- a/solution.py
+++ b/solution.py
@@ -228,11 +228,12 @@
     sides = sources
     incoming = []
     if stage == 1:
-        right_ref, in_sem = refs[2:4]
-        for g in range(right_ref.shape[1] // together):
+        sides, in_sem = refs[2:4], refs[4]
+        for g in range(sources[0].shape[1] // together):
             at = pl.ds(g * together, together)
-            incoming.append(pltpu.make_async_copy(sources[1].at[:, at], right_ref.at[:, at], in_sem.at[g]))
-        sides = (sources[0], right_ref)
+            incoming += [
+                pltpu.make_async_copy(x.at[:, at], y.at[:, at], in_sem.at[k, g]) for k, (x, y) in enumerate(zip(sources, sides))
+            ]
     for copy in incoming:
         copy.start()
     if stage != 3:
@@ -250,11 +251,11 @@
     sums = [jnp.zeros((8, width), f32)] * 3
     for g in range(steps):
         here = range(g * together, (g + 1) * together)
+        for copy in incoming[2 * g : 2 * g + 2]:
+            copy.wait()
         halves = {
             s: [dot(sides[0][t, s], vb_ref[conn_ref[t, s]], 1, 0).astype(bf16) for t in range(terms)] for s in here
         }
-        if incoming:
-            incoming[g].wait()
         for s in here:
             if stage == 4:
                 own_t = vb_ref[blocks + s].T
@@ -290,7 +291,8 @@
     steps = blocks // together
     scratch = [pltpu.VMEM((3 * blocks, width, width), bf16)]
     if stage == 1:
-        scratch += [pltpu.VMEM(sides[1].shape, bf16), pltpu.SemaphoreType.DMA((steps,))]
+        scratch += [pltpu.VMEM(x.shape, bf16) for x in sides]
+        scratch.append(pltpu.SemaphoreType.DMA((2, steps)))
     if stage == 3:
         out_shape, out_specs = jax.ShapeDtypeStruct((1, 128), f32), vmem
     else:
@@ -299,7 +301,7 @@
         scratch += [pltpu.VMEM(shape, bf16), pltpu.SemaphoreType.DMA((steps,))]
     return pl.pallas_call(
         lambda *refs: product_kernel(stage, *refs),
-        in_specs=[smem, smem] + [vmem] * (len(groups) + len(more) + len(sides) - (stage == 1)) + [hbm] * (stage == 1),
+        in_specs=[smem, smem] + [vmem] * (len(groups) + len(more)) + [hbm if stage == 1 else vmem] * len(sides),
         out_specs=out_specs,
         out_shape=out_shape,
         scratch_shapes=scratch,
@@ -425,10 +427,10 @@
     )
     psi = call_small(start_kernel, [sector_dims], [psi_start], cut, "start")
     far = swapped(shares, 1)
-    left_env = kept(left_env)
+    outside = [pltpu.with_memory_space_constraint(x, pltpu.HBM) for x in (left_env, right_env)]
 
     groups = (to_everyone(far[0], "term"), psi, swapped(psi, 0))
-    partial = product(1, conn, sector_dims, groups, (), left_env, pltpu.with_memory_space_constraint(right_env, pltpu.HBM))
+    partial = product(1, conn, sector_dims, groups, (), *outside)
     sig1, tot1 = reduced(1, partial, shares)
     v2, groups2, _ = updated(1, (tot1,), (shares, sig1[0]), (far, sig1[1]))
 

time: 233 us -> 231 us (level)
  Pallas kernels: 30.8 us -> 26 us
  waiting for transfers between devices: 23.5 us -> 25.9 us
  transfers between devices with their start and end apart: 8 -> 8, of which waited for: 6 -> 6; matrix products, arithmetic and copies ran while one was open for 0% -> 0% of each run, Pallas kernels for 3% -> 2%
where the time goes in v4:
time: 231 us; the launch traced here: 230 us
  blocking collectives  138 us (60%)
  starting transfers between devices  33.9 us (15%)
  Pallas kernels  26 us (11%)
  waiting for transfers between devices  25.9 us (11%)
  local copies, waits for them, and re-layouts  5.54 us (2%)
    all_to_all x4, blocking collectives, exchange(): return lax.all_to_all(x, 'term', 0, 0, tiled=True)  95 us
    all_to_all x2, blocking collectives, reduced(): lax.all_to_all(sums, everyone, 0, 0, tiled=True)  43.3 us
    ppermute x6, starting transfers between devices, swapped(): return lax.ppermute(block, 'sector', pairs + [(j, i) for i, j in pairs])  22.9 us
    pallas_call x4, Pallas kernels, product(): pl.pallas_call(lambda *refs: product_kernel(stage, *refs), in_specs=[smem...  15.1 us
    all_to_all x2, waiting for transfers between devices, to_everyone(): lax.all_to_all(jnp.broadcast_to(x[None], (devices, *x.shape)), axis, 0, 0...  14.4 us
    ppermute x6, waiting for transfers between devices, swapped(): return lax.ppermute(block, 'sector', pairs + [(j, i) for i, j in pairs])  11.4 us
    all_to_all x2, starting transfers between devices, to_everyone(): lax.all_to_all(jnp.broadcast_to(x[None], (devices, *x.shape)), axis, 0, 0...  10.9 us
    pallas_call x6, Pallas kernels, call_small(): pl.pallas_call(kernel, in_specs=[smem] * len(dims) + [vmem] * len(arrays)...  8.58 us
  transfers between devices with their start and end apart: 8, of which 6 were waited for; matrix products, arithmetic and copies ran while one was open for 0% of the time, Pallas kernels for 2%

profile of v4, /device:TPU:1, one launch (start us, length us, event | category | flops | bytes accessed | tf_op | source)
XLA Modules:
  0.0 230.5 jit_solution(13555649531865462434)
XLA Ops:
  1.3 2.3 share.1.refs_1_.refs_2_
  3.6 4.7 %collective-permute-start = (bf16[2,8,32,256]{3,2,1,0:T(8,128)(2,1)}, bf16[2,8,32,256]{3,2,1,0:T(8,128)(2,1)S(1)}, u32[]{:S(2)}, u32[]{:S(2)}) collective-permute-start(bf16[2,8,32,256]{3,2,1,0:T(8,128)(2,1)} %share.1.refs_1_.refs_2_), channel_id=1, source_target_pairs={{1,2},{3,4},{5,6},{7,8},{9,10},{11,12},{13,14},{15,16},{17,18},{19... | collective-permute-start | bytes 786440 | tf_op jit(solution)/shard_map/ppermute | solution.py:20
  8.4 4.3 %collective-permute-done.refs_3_.refs_6_ = bf16[2,8,32,256]{3,2,1,0:T(8,128)(2,1)S(1)} collective-permute-done((bf16[2,8,32,256]{3,2,1,0:T(8,128)(2,1)}, bf16[2,8,32,256]{3,2,1,0:T(8,128)(2,1)S(1)}, u32[]{:S(2)}, u32[]{:S(2)}) %collective-permute-start) | collective-permute-done | bytes 262176 | tf_op jit(solution)/shard_map/ppermute | solution.py:20
  12.6 1.1 broadcast_in_dim.27
  13.7 5.5 %all-to-all-start = ((bf16[8,8,32,256]{3,2,1,0:T(8,128)(2,1)}), bf16[8,8,32,256]{3,2,1,0:T(8,128)(2,1)S(1)}, u32[]{:S(2)}, u32[]{:S(2)}) async-start(bf16[8,8,32,256]{3,2,1,0:T(8,128)(2,1)} %broadcast_in_dim.27), calls=%async_computation | async-start | bytes 2097152 | tf_op jit(solution)/shard_map/all_to_all | solution.py:15
  19.3 0.9 start.1.refs_3_.refs_4_
  20.3 2.6 %collective-permute-done.1.refs_4_ = bf16[8,8,32,256]{3,2,1,0:T(8,128)(2,1)S(1)} collective-permute-done((bf16[8,8,32,256]{3,2,1,0:T(8,128)(2,1)S(1)}, bf16[8,8,32,256]{3,2,1,0:T(8,128)(2,1)S(1)}, u32[]{:S(2)}, u32[]{:S(2)}) %collective-permute-start.1) | collective-permute-done | bytes 1048608 | tf_op jit(solution)/shard_map/ppermute | solution.py:20
  22.9 7.7 %all-to-all-done.refs_2_ = bf16[8,8,32,256]{3,2,1,0:T(8,128)(2,1)S(1)} async-done(((bf16[8,8,32,256]{3,2,1,0:T(8,128)(2,1)}), bf16[8,8,32,256]{3,2,1,0:T(8,128)(2,1)S(1)}, u32[]{:S(2)}, u32[]{:S(2)}) %all-to-all-start) | async-done | bytes 1048608 | tf_op jit(solution)/shard_map/all_to_all | solution.py:15
  30.7 5.1 %product_1.1 = bf16[8,8,32,256]{3,2,1,0:T(8,128)(2,1)} custom-call(s32[3,8]{1,0:T(4,128)S(1)} %fusion.3.refs_0_, s32[2,8]{1,0:T(2,128)S(1)} %copy-done.13, bf16[8,8,32,256]{3,2,1,0:T(8,128)(2,1)S(1)} %all-to-all-done.refs_2_, bf16[8,8,32,256]{3,2,1,0:T(8,128)(2,1)S(1)} %start.1.refs_3_.refs_4_, bf16[8,8,32,256]{3,2,1,0:T(8,128)(2,1)S(1)} %collective-permute-done.1.refs_4_, ...), custom_call_target="tpu_custom_call" | custom-call | tf_op jit(solution)/shard_map/product_1/pallas_call | solution.py:302
  35.8 16.2 %all_to_all.55.refs_0_ = bf16[8,8,32,256]{3,2,1,0:T(8,128)(2,1)S(1)} all-to-all(bf16[8,8,32,256]{3,2,1,0:T(8,128)(2,1)} %product_1.1), channel_id=1, replica_groups=mesh['term'=8,'sector'=32] {'term'}, dimensions={0} | all-to-all | bytes 2097152 | tf_op jit(solution)/shard_map/all_to_all | solution.py:383
  51.9 1.0 reduce_1.1
  53.0 11.1 %collective-permute-start.2 = (f32[8,32,256]{2,1,0:T(8,128)}, f32[8,32,256]{2,1,0:T(8,128)S(1)}, u32[]{:S(2)}, u32[]{:S(2)}) collective-permute-start(f32[8,32,256]{2,1,0:T(8,128)} %get-tuple-element.23), channel_id=1, source_target_pairs={{1,2},{3,4},{5,6},{7,8},{9,10},{11,12},{13,14},{15,16},{17,18},{19... | collective-permute-start | bytes 786440 | tf_op jit(solution)/shard_map/ppermute | solution.py:20
  64.1 23.7 %all_to_all.56 = f32[256,1,128]{2,1,0:T(1,128)S(1)} all-to-all(f32[256,1,128]{2,1,0:T(1,128)S(1)} %bitcast.25), channel_id=1, replica_groups=mesh['term'=8,'sector'=32] {'term','sector'}, dimensions={0} | all-to-all | bytes 262144 | tf_op jit(solution)/shard_map/all_to_all | solution.py:397
  87.8 1.8 update_1.1
  89.6 30.2 %all_to_all.57.refs_2_.refs_5_ = bf16[8,2,8,32,256]{4,3,2,1,0:T(8,128)(2,1)S(1)} all-to-all(bf16[8,2,8,32,256]{4,3,2,1,0:T(8,128)(2,1)} %get-tuple-element.24), channel_id=1, replica_groups=mesh['term'=8,'sector'=32] {'term'}, dimensions={0} | all-to-all | bytes 4194304 | tf_op jit(solution)/shard_map/all_to_all | solution.py:383
  119.8 1.7 collective-permute-start.3
  121.6 2.3 collective-permute-done.3.refs_3_
  123.9 3.4 %product_2.1 = bf16[8,8,32,256]{3,2,1,0:T(8,128)(2,1)} custom-call(s32[3,8]{1,0:T(4,128)S(1)} %fusion.3.refs_0_, s32[2,8]{1,0:T(2,128)S(1)} %copy-done.13, bf16[8,2,8,32,256]{4,3,2,1,0:T(8,128)(2,1)S(1)} %all_to_all.57.refs_2_.refs_5_, bf16[8,8,32,256]{3,2,1,0:T(8,128)(2,1)S(1)} %collective-permute-done.3.refs_3_, bf16[3,8,256,256]{3,2,1,0:T(8,128)(2,1)S(1)} %copy-done, ...), custom_call_target="tpu_custom_call" | custom-call | tf_op jit(solution)/shard_map/product_2/pallas_call | solution.py:302
  127.3 18.9 %all_to_all.58.refs_0_ = bf16[8,8,32,256]{3,2,1,0:T(8,128)(2,1)S(1)} all-to-all(bf16[8,8,32,256]{3,2,1,0:T(8,128)(2,1)} %product_2.1), channel_id=1, replica_groups=mesh['term'=8,'sector'=32] {'term'}, dimensions={0} | all-to-all | bytes 2097152 | tf_op jit(solution)/shard_map/all_to_all | solution.py:383
  146.2 1.2 reduce_2.1
  147.4 3.4 %collective-permute-start.4 = (f32[8,32,256]{2,1,0:T(8,128)}, f32[8,32,256]{2,1,0:T(8,128)S(1)}, u32[]{:S(2)}, u32[]{:S(2)}) collective-permute-start(f32[8,32,256]{2,1,0:T(8,128)} %get-tuple-element.30), channel_id=1, source_target_pairs={{1,2},{3,4},{5,6},{7,8},{9,10},{11,12},{13,14},{15,16},{17,18},{19... | collective-permute-start | bytes 786440 | tf_op jit(solution)/shard_map/ppermute | solution.py:20
  150.8 19.6 %all_to_all.59 = f32[256,1,128]{2,1,0:T(1,128)S(1)} all-to-all(f32[256,1,128]{2,1,0:T(1,128)S(1)} %bitcast.26), channel_id=1, replica_groups=mesh['term'=8,'sector'=32] {'term','sector'}, dimensions={0} | all-to-all | bytes 262144 | tf_op jit(solution)/shard_map/all_to_all | solution.py:397
  170.4 2.9 %update_2.1 = (f32[8,32,256]{2,1,0:T(8,128)}, f32[8,32,256]{2,1,0:T(8,128)}, f32[1,128]{1,0:T(1,128)S(1)}, bf16[8,2,8,32,256]{4,3,2,1,0:T(8,128)(2,1)}) custom-call(f32[256,128]{1,0:T(8,128)S(1)} %bitcast.17, f32[256,128]{1,0:T(8,128)S(1)} %bitcast.19, bf16[2,8,32,256]{3,2,1,0:T(8,128)(2,1)S(1)} %copy-done.6, ...), custom_call_target="tpu_custom_call" | custom-call | tf_op jit(solution)/shard_map/update_2/pallas_call | solution.py:339
  173.3 29.8 %all_to_all.60.refs_2_ = bf16[8,2,8,32,256]{4,3,2,1,0:T(8,128)(2,1)S(1)} all-to-all(bf16[8,2,8,32,256]{4,3,2,1,0:T(8,128)(2,1)} %get-tuple-element.32), channel_id=1, replica_groups=mesh['term'=8,'sector'=32] {'term'}, dimensions={0} | all-to-all | bytes 4194304 | tf_op jit(solution)/shard_map/all_to_all | solution.py:383
  203.1 1.9 collective-permute-start.5
  205.0 2.3 collective-permute-done.5.refs_3_
  207.3 3.1 %product_3.1 = f32[1,128]{1,0:T(1,128)S(1)} custom-call(s32[3,8]{1,0:T(4,128)S(1)} %fusion.3.refs_0_, s32[2,8]{1,0:T(2,128)S(1)} %copy-done.13, bf16[8,2,8,32,256]{4,3,2,1,0:T(8,128)(2,1)S(1)} %all_to_all.60.refs_2_, bf16[8,8,32,256]{3,2,1,0:T(8,128)(2,1)S(1)} %collective-permute-done.5.refs_3_, bf16[8,8,32,256]{3,2,1,0:T(8,128)(2,1)S(1)} %copy-done.5, ...), custom_call_target="tpu_custom_call" | custom-call | tf_op jit(solution)/shard_map/product_3/pallas_call | solution.py:302
  211.2 5.4 %all-to-all-start.7 = ((f32[256,1,128]{2,1,0:T(1,128)}), f32[256,1,128]{2,1,0:T(1,128)S(1)}, u32[]{:S(2)}, u32[]{:S(2)}) async-start(f32[256,1,128]{2,1,0:T(1,128)} %broadcast_in_dim.32), calls=%async_computation.7 | async-start | bytes 262144 | tf_op jit(solution)/shard_map/all_to_all | solution.py:15
  216.6 1.6 copy-done.3
  218.2 1.2 copy-done.9
  219.4 3.5 %product_4.1 = bf16[3,8,256,256]{3,2,1,0:T(8,128)(2,1)} custom-call(s32[3,8]{1,0:T(4,128)S(1)} %fusion.3.refs_0_, s32[2,8]{1,0:T(2,128)S(1)} %copy-done.13, bf16[8,2,8,32,256]{4,3,2,1,0:T(8,128)(2,1)S(1)} %copy-done.3, bf16[8,8,32,256]{3,2,1,0:T(8,128)(2,1)S(1)} %copy-done.9, bf16[3,8,256,256]{3,2,1,0:T(8,128)(2,1)S(1)} %copy-done), custom_call_target="tpu_custom_call" | custom-call | tf_op jit(solution)/shard_map/product_4/pallas_call | solution.py:302
  223.0 6.7 %all-to-all-done.7 = f32[256,1,128]{2,1,0:T(1,128)S(1)} async-done(((f32[256,1,128]{2,1,0:T(1,128)}), f32[256,1,128]{2,1,0:T(1,128)S(1)}, u32[]{:S(2)}, u32[]{:S(2)}) %all-to-all-start.7) | async-done | bytes 131104 | tf_op jit(solution)/shard_map/all_to_all | solution.py:15
  (39 shorter events, 2.6 us)
Async XLA Ops:
  0.6 0.7 copy-start.12
  3.6 15.6 %copy-start.7 = (bf16[8,256,256]{2,1,0:T(8,128)(2,1)S(1)}, bf16[8,256,256]{2,1,0:T(8,128)(2,1)}, u32[]{:S(2)}) copy-start(bf16[8,256,256]{2,1,0:T(8,128)(2,1)} %psi_ref.3) | copy-start | bytes 3145732
  3.6 15.6 %copy-start.13 = (s32[2,8]{1,0:T(2,128)S(1)}, s32[2,8]{1,0:T(2,128)}, u32[]{:S(2)}) copy-start(s32[2,8]{1,0:T(2,128)} %refs_1_.7) | copy-start | bytes 196
  3.6 9.0 %collective-permute-start = (bf16[2,8,32,256]{3,2,1,0:T(8,128)(2,1)}, bf16[2,8,32,256]{3,2,1,0:T(8,128)(2,1)S(1)}, u32[]{:S(2)}, u32[]{:S(2)}) collective-permute-start(bf16[2,8,32,256]{3,2,1,0:T(8,128)(2,1)} %share.1.refs_1_.refs_2_), channel_id=1, source_target_pairs={{1,2},{3,4},{5,6},{7,8},{9,10},{11,12},{13,14},{15,16},{17,18},{19... | collective-permute-start | bytes 786440 | tf_op jit(solution)/shard_map/ppermute | solution.py:20
  13.7 6.5 %copy-start.14 = (s32[3,8]{1,0:T(4,128)S(1)}, s32[3,8]{1,0:T(4,128)}, u32[]{:S(2)}) copy-start(s32[3,8]{1,0:T(4,128)} %param.9) | copy-start | bytes 292
  13.7 16.9 %all-to-all-start = ((bf16[8,8,32,256]{3,2,1,0:T(8,128)(2,1)}), bf16[8,8,32,256]{3,2,1,0:T(8,128)(2,1)S(1)}, u32[]{:S(2)}, u32[]{:S(2)}) async-start(bf16[8,8,32,256]{3,2,1,0:T(8,128)(2,1)} %broadcast_in_dim.27), calls=%async_computation | async-start | bytes 2097152 | tf_op jit(solution)/shard_map/all_to_all | solution.py:15
  20.2 15.6 %copy-start.4 = (bf16[8,8,32,256]{3,2,1,0:T(8,128)(2,1)}, bf16[8,8,32,256]{3,2,1,0:T(8,128)(2,1)S(1)}, u32[]{:S(2)}) copy-start(bf16[8,8,32,256]{3,2,1,0:T(8,128)(2,1)S(1)} %start.1.refs_3_.refs_4_) | copy-start | bytes 3145732
  20.2 2.7 %collective-permute-start.1 = (bf16[8,8,32,256]{3,2,1,0:T(8,128)(2,1)S(1)}, bf16[8,8,32,256]{3,2,1,0:T(8,128)(2,1)S(1)}, u32[]{:S(2)}, u32[]{:S(2)}) collective-permute-start(bf16[8,8,32,256]{3,2,1,0:T(8,128)(2,1)S(1)} %start.1.refs_3_.refs_4_), channel_id=1, source_target_pairs={{0,1},{2,3},{4,5},{6,7},{8,9},{10,11},{12,13},{14,15},{16,17},{18,... | collective-permute-start | bytes 3145736 | tf_op jit(solution)/shard_map/ppermute | solution.py:20
  35.8 16.2 %copy-start.6 = (bf16[2,8,32,256]{3,2,1,0:T(8,128)(2,1)S(1)}, bf16[2,8,32,256]{3,2,1,0:T(8,128)(2,1)}, u32[]{:S(2)}) copy-start(bf16[2,8,32,256]{3,2,1,0:T(8,128)(2,1)} %share.1.refs_1_.refs_2_) | copy-start | bytes 786436
  53.0 34.8 %collective-permute-start.2 = (f32[8,32,256]{2,1,0:T(8,128)}, f32[8,32,256]{2,1,0:T(8,128)S(1)}, u32[]{:S(2)}, u32[]{:S(2)}) collective-permute-start(f32[8,32,256]{2,1,0:T(8,128)} %get-tuple-element.23), channel_id=1, source_target_pairs={{1,2},{3,4},{5,6},{7,8},{9,10},{11,12},{13,14},{15,16},{17,18},{19... | collective-permute-start | bytes 786440 | tf_op jit(solution)/shard_map/ppermute | solution.py:20
  89.6 34.3 %copy-start = (bf16[3,8,256,256]{3,2,1,0:T(8,128)(2,1)S(1)}, bf16[3,8,256,256]{3,2,1,0:T(8,128)(2,1)}, u32[]{:S(2)}) copy-start(bf16[3,8,256,256]{3,2,1,0:T(8,128)(2,1)} %refs_4_.3) | copy-start | bytes 9437188
  89.6 34.3 %copy-start.1 = (bf16[3,8,256,256]{3,2,1,0:T(8,128)(2,1)S(1)}, bf16[3,8,256,256]{3,2,1,0:T(8,128)(2,1)}, u32[]{:S(2)}) copy-start(bf16[3,8,256,256]{3,2,1,0:T(8,128)(2,1)} %refs_8_.1) | copy-start | bytes 9437188
  119.8 4.0 %collective-permute-start.3 = (bf16[8,8,32,256]{3,2,1,0:T(8,128)(2,1)S(1)}, bf16[8,8,32,256]{3,2,1,0:T(8,128)(2,1)S(1)}, u32[]{:S(2)}, u32[]{:S(2)}) collective-permute-start(bf16[8,8,32,256]{3,2,1,0:T(8,128)(2,1)S(1)} %slice_bitcast_fusion.1), channel_id=1, source_target_pairs={{0,1},{2,3},{4,5},{6,7},{8,9},{10,11},{12,13},{14,15},{16,17},{18,... | collective-permute-start | bytes 3145736 | tf_op jit(solution)/shard_map/ppermute | solution.py:20
  147.4 23.0 %collective-permute-start.4 = (f32[8,32,256]{2,1,0:T(8,128)}, f32[8,32,256]{2,1,0:T(8,128)S(1)}, u32[]{:S(2)}, u32[]{:S(2)}) collective-permute-start(f32[8,32,256]{2,1,0:T(8,128)} %get-tuple-element.30), channel_id=1, source_target_pairs={{1,2},{3,4},{5,6},{7,8},{9,10},{11,12},{13,14},{15,16},{17,18},{19... | collective-permute-start | bytes 786440 | tf_op jit(solution)/shard_map/ppermute | solution.py:20
  170.4 2.9 %copy-start.10 = (f32[256,1,128]{2,1,0:T(1,128)}, f32[256,1,128]{2,1,0:T(1,128)S(1)}, u32[]{:S(2)}) copy-start(f32[256,1,128]{2,1,0:T(1,128)S(1)} %all_to_all.59) | copy-start | bytes 393220
  203.0 7.4 %copy-start.2 = (bf16[8,2,8,32,256]{4,3,2,1,0:T(8,128)(2,1)}, bf16[8,2,8,32,256]{4,3,2,1,0:T(8,128)(2,1)S(1)}, u32[]{:S(2)}) copy-start(bf16[8,2,8,32,256]{4,3,2,1,0:T(8,128)(2,1)S(1)} %all_to_all.60.refs_2_) | copy-start | bytes 6291460
  203.0 4.3 %copy-start.5 = (bf16[8,8,32,256]{3,2,1,0:T(8,128)(2,1)S(1)}, bf16[8,8,32,256]{3,2,1,0:T(8,128)(2,1)}, u32[]{:S(2)}) copy-start(bf16[8,8,32,256]{3,2,1,0:T(8,128)(2,1)} %copy-done.4) | copy-start | bytes 3145732
  203.1 4.2 %collective-permute-start.5 = (bf16[8,8,32,256]{3,2,1,0:T(8,128)(2,1)S(1)}, bf16[8,8,32,256]{3,2,1,0:T(8,128)(2,1)S(1)}, u32[]{:S(2)}, u32[]{:S(2)}) collective-permute-start(bf16[8,8,32,256]{3,2,1,0:T(8,128)(2,1)S(1)} %slice_bitcast_fusion), channel_id=1, source_target_pairs={{0,1},{2,3},{4,5},{6,7},{8,9},{10,11},{12,13},{14,15},{16,17},{18,... | collective-permute-start | bytes 3145736 | tf_op jit(solution)/shard_map/ppermute | solution.py:20
  207.3 3.1 %copy-start.8 = (bf16[8,8,32,256]{3,2,1,0:T(8,128)(2,1)}, bf16[8,8,32,256]{3,2,1,0:T(8,128)(2,1)S(1)}, u32[]{:S(2)}) copy-start(bf16[8,8,32,256]{3,2,1,0:T(8,128)(2,1)S(1)} %collective-permute-done.5.refs_3_) | copy-start | bytes 3145732
  211.2 18.5 %all-to-all-start.7 = ((f32[256,1,128]{2,1,0:T(1,128)}), f32[256,1,128]{2,1,0:T(1,128)S(1)}, u32[]{:S(2)}, u32[]{:S(2)}) async-start(f32[256,1,128]{2,1,0:T(1,128)} %broadcast_in_dim.32), calls=%async_computation.7 | async-start | bytes 262144 | tf_op jit(solution)/shard_map/all_to_all | solution.py:15
  216.6 1.6 copy-start.3
  218.2 1.2 copy-start.9
  219.4 10.2 %copy-start.11 = (f32[256,1,128]{2,1,0:T(1,128)S(1)}, f32[256,1,128]{2,1,0:T(1,128)}, u32[]{:S(2)}) copy-start(f32[256,1,128]{2,1,0:T(1,128)} %copy-done.10) | copy-start | bytes 393220

commit v5 on v4

--- a/solution.py
+++ b/solution.py
@@ -169,7 +169,7 @@
     tots, refs = refs[:stage], refs[stage:]
     per = 2 if stage == 1 else 4
     groups, refs = (refs[:per], refs[per : 2 * per]), refs[2 * per :]
-    v_refs, refs = refs[:2], refs[2:]
+    v_refs, refs = refs[: 3 - stage], refs[3 - stage :]
     if stage > 1:
         row_ref, refs = refs[0], refs[1:]
     all_ref, buf_ref, sem = refs
@@ -192,7 +192,8 @@
                 sig2, v2 = groups[g][2][s], groups[g][3][s]
                 v = (p * sig2 + q * v2) * rd + w * psi + y * v2
                 acc = acc[0] + fold(v * sig1), acc[1] + fold(v * sig2)
-            v_refs[g][s] = v
+            if g < len(v_refs):
+                v_refs[g][s] = v
             buf_ref[g, s] = v.astype(bf16)
             return acc
 
@@ -397,9 +398,9 @@
         return (mine, swapped(sent, 1)), lax.all_to_all(sums, everyone, 0, 0, tiled=True)
 
     def updated(stage, tots, own, far):
-        out = (part, part) + ((row,) if stage > 1 else ())
+        out = (part, part) if stage == 1 else (part, row)
         every = pltpu.HBM((pieces, 2, blocks, share, width), bf16)
-        v, v_far, *more, every = call_small(
+        v, other, every = call_small(
             lambda *refs: update_kernel(stage, entries, *refs),
             [],
             [*tots, *own, *far],
@@ -409,7 +410,7 @@
             [pltpu.VMEM((2, blocks, share, width), bf16), pltpu.SemaphoreType.DMA((2, pieces))],
         )
         both = exchange(every)
-        return (v, v_far), (both, swapped(both[:, 0], 0)), more
+        return v, other, (both, swapped(both[:, 0], 0))
 
     hbm = pl.BlockSpec(memory_space=pltpu.HBM)
     shares = pl.pallas_call(
@@ -432,11 +433,11 @@
     groups = (to_everyone(far[0], "term"), psi, swapped(psi, 0))
     partial = product(1, conn, sector_dims, groups, (), *outside)
     sig1, tot1 = reduced(1, partial, shares)
-    v2, groups2, _ = updated(1, (tot1,), (shares, sig1[0]), (far, sig1[1]))
+    v2, v2_far, groups2 = updated(1, (tot1,), (shares, sig1[0]), (far, sig1[1]))
 
     partial = product(2, conn, sector_dims, groups2, (), left_env, right_env)
-    sig2, tot2 = reduced(2, partial, shares, sig1[0], v2[0])
-    v3, groups3, (more,) = updated(2, (tot1, tot2), (shares, sig1[0], sig2[0], v2[0]), (far, sig1[1], sig2[1], v2[1]))
+    sig2, tot2 = reduced(2, partial, shares, sig1[0], v2)
+    v3, more, groups3 = updated(2, (tot1, tot2), (shares, sig1[0], sig2[0], v2), (far, sig1[1], sig2[1], v2_far))
 
     row3 = product(3, conn, sector_dims, groups3, (psi, groups2[0], more), left_env, right_env)
     tot3 = to_everyone(row3[0], everyone)
@@ -444,7 +445,7 @@
     projected = call_small(
         lambda *refs: last_kernel(entries, *refs), [], [tot1, tot2, tot3], jax.ShapeDtypeStruct((3, 3), f32), "last"
     )
-    return (projected, v3[0], env)
+    return (projected, v3, env)
 
 
 def solution(mesh):

time: 231 us -> 231 us (level)
  no operation moved by 1% of the time
where the time goes in v5:
time: 231 us; the launch traced here: 230 us
  blocking collectives  138 us (60%)
  starting transfers between devices  33.9 us (15%)
  Pallas kernels  25.9 us (11%)
  waiting for transfers between devices  25.9 us (11%)
  local copies, waits for them, and re-layouts  5.54 us (2%)
    all_to_all x4, blocking collectives, exchange(): return lax.all_to_all(x, 'term', 0, 0, tiled=True)  95 us
    all_to_all x2, blocking collectives, reduced(): lax.all_to_all(sums, everyone, 0, 0, tiled=True)  43.3 us
    ppermute x6, starting transfers between devices, swapped(): return lax.ppermute(block, 'sector', pairs + [(j, i) for i, j in pairs])  22.9 us
    pallas_call x4, Pallas kernels, product(): pl.pallas_call(lambda *refs: product_kernel(stage, *refs), in_specs=[smem...  15.1 us
    all_to_all x2, waiting for transfers between devices, to_everyone(): lax.all_to_all(jnp.broadcast_to(x[None], (devices, *x.shape)), axis, 0, 0...  14.4 us
    ppermute x6, waiting for transfers between devices, swapped(): return lax.ppermute(block, 'sector', pairs + [(j, i) for i, j in pairs])  11.4 us
    all_to_all x2, starting transfers between devices, to_everyone(): lax.all_to_all(jnp.broadcast_to(x[None], (devices, *x.shape)), axis, 0, 0...  10.9 us
    pallas_call x6, Pallas kernels, call_small(): pl.pallas_call(kernel, in_specs=[smem] * len(dims) + [vmem] * len(arrays)...  8.49 us
  transfers between devices with their start and end apart: 8, of which 6 were waited for; matrix products, arithmetic and copies ran while one was open for 0% of the time, Pallas kernels for 2%

profile of v5, /device:TPU:1, one launch (start us, length us, event | category | flops | bytes accessed | tf_op | source)
XLA Modules:
  0.0 230.4 jit_solution(1201375825941571501)
XLA Ops:
  1.3 2.3 share.1.refs_1_.refs_2_
  3.6 4.7 %collective-permute-start = (bf16[2,8,32,256]{3,2,1,0:T(8,128)(2,1)}, bf16[2,8,32,256]{3,2,1,0:T(8,128)(2,1)S(1)}, u32[]{:S(2)}, u32[]{:S(2)}) collective-permute-start(bf16[2,8,32,256]{3,2,1,0:T(8,128)(2,1)} %share.1.refs_1_.refs_2_), channel_id=1, source_target_pairs={{1,2},{3,4},{5,6},{7,8},{9,10},{11,12},{13,14},{15,16},{17,18},{19... | collective-permute-start | bytes 786440 | tf_op jit(solution)/shard_map/ppermute | solution.py:20
  8.4 4.3 %collective-permute-done.refs_3_.refs_6_ = bf16[2,8,32,256]{3,2,1,0:T(8,128)(2,1)S(1)} collective-permute-done((bf16[2,8,32,256]{3,2,1,0:T(8,128)(2,1)}, bf16[2,8,32,256]{3,2,1,0:T(8,128)(2,1)S(1)}, u32[]{:S(2)}, u32[]{:S(2)}) %collective-permute-start) | collective-permute-done | bytes 262176 | tf_op jit(solution)/shard_map/ppermute | solution.py:20
  12.6 1.1 broadcast_in_dim.27
  13.7 5.5 %all-to-all-start = ((bf16[8,8,32,256]{3,2,1,0:T(8,128)(2,1)}), bf16[8,8,32,256]{3,2,1,0:T(8,128)(2,1)S(1)}, u32[]{:S(2)}, u32[]{:S(2)}) async-start(bf16[8,8,32,256]{3,2,1,0:T(8,128)(2,1)} %broadcast_in_dim.27), calls=%async_computation | async-start | bytes 2097152 | tf_op jit(solution)/shard_map/all_to_all | solution.py:15
  19.3 0.9 start.1.refs_3_.refs_4_
  20.3 2.6 %collective-permute-done.1.refs_4_ = bf16[8,8,32,256]{3,2,1,0:T(8,128)(2,1)S(1)} collective-permute-done((bf16[8,8,32,256]{3,2,1,0:T(8,128)(2,1)S(1)}, bf16[8,8,32,256]{3,2,1,0:T(8,128)(2,1)S(1)}, u32[]{:S(2)}, u32[]{:S(2)}) %collective-permute-start.1) | collective-permute-done | bytes 1048608 | tf_op jit(solution)/shard_map/ppermute | solution.py:20
  22.9 7.7 %all-to-all-done.refs_2_ = bf16[8,8,32,256]{3,2,1,0:T(8,128)(2,1)S(1)} async-done(((bf16[8,8,32,256]{3,2,1,0:T(8,128)(2,1)}), bf16[8,8,32,256]{3,2,1,0:T(8,128)(2,1)S(1)}, u32[]{:S(2)}, u32[]{:S(2)}) %all-to-all-start) | async-done | bytes 1048608 | tf_op jit(solution)/shard_map/all_to_all | solution.py:15
  30.7 5.1 %product_1.1 = bf16[8,8,32,256]{3,2,1,0:T(8,128)(2,1)} custom-call(s32[3,8]{1,0:T(4,128)S(1)} %fusion.3.refs_0_, s32[2,8]{1,0:T(2,128)S(1)} %copy-done.13, bf16[8,8,32,256]{3,2,1,0:T(8,128)(2,1)S(1)} %all-to-all-done.refs_2_, bf16[8,8,32,256]{3,2,1,0:T(8,128)(2,1)S(1)} %start.1.refs_3_.refs_4_, bf16[8,8,32,256]{3,2,1,0:T(8,128)(2,1)S(1)} %collective-permute-done.1.refs_4_, ...), custom_call_target="tpu_custom_call" | custom-call | tf_op jit(solution)/shard_map/product_1/pallas_call | solution.py:303
  35.8 16.2 %all_to_all.55.refs_0_ = bf16[8,8,32,256]{3,2,1,0:T(8,128)(2,1)S(1)} all-to-all(bf16[8,8,32,256]{3,2,1,0:T(8,128)(2,1)} %product_1.1), channel_id=1, replica_groups=mesh['term'=8,'sector'=32] {'term'}, dimensions={0} | all-to-all | bytes 2097152 | tf_op jit(solution)/shard_map/all_to_all | solution.py:384
  51.9 1.0 reduce_1.1
  53.0 11.1 %collective-permute-start.2 = (f32[8,32,256]{2,1,0:T(8,128)}, f32[8,32,256]{2,1,0:T(8,128)S(1)}, u32[]{:S(2)}, u32[]{:S(2)}) collective-permute-start(f32[8,32,256]{2,1,0:T(8,128)} %get-tuple-element.23), channel_id=1, source_target_pairs={{1,2},{3,4},{5,6},{7,8},{9,10},{11,12},{13,14},{15,16},{17,18},{19... | collective-permute-start | bytes 786440 | tf_op jit(solution)/shard_map/ppermute | solution.py:20
  64.1 23.7 %all_to_all.56 = f32[256,1,128]{2,1,0:T(1,128)S(1)} all-to-all(f32[256,1,128]{2,1,0:T(1,128)S(1)} %bitcast.25), channel_id=1, replica_groups=mesh['term'=8,'sector'=32] {'term','sector'}, dimensions={0} | all-to-all | bytes 262144 | tf_op jit(solution)/shard_map/all_to_all | solution.py:398
  87.8 1.8 update_1.1
  89.6 30.2 %all_to_all.57.refs_2_.refs_5_ = bf16[8,2,8,32,256]{4,3,2,1,0:T(8,128)(2,1)S(1)} all-to-all(bf16[8,2,8,32,256]{4,3,2,1,0:T(8,128)(2,1)} %get-tuple-element.24), channel_id=1, replica_groups=mesh['term'=8,'sector'=32] {'term'}, dimensions={0} | all-to-all | bytes 4194304 | tf_op jit(solution)/shard_map/all_to_all | solution.py:384
  119.8 1.7 collective-permute-start.3
  121.6 2.3 collective-permute-done.3.refs_3_
  123.9 3.4 %product_2.1 = bf16[8,8,32,256]{3,2,1,0:T(8,128)(2,1)} custom-call(s32[3,8]{1,0:T(4,128)S(1)} %fusion.3.refs_0_, s32[2,8]{1,0:T(2,128)S(1)} %copy-done.13, bf16[8,2,8,32,256]{4,3,2,1,0:T(8,128)(2,1)S(1)} %all_to_all.57.refs_2_.refs_5_, bf16[8,8,32,256]{3,2,1,0:T(8,128)(2,1)S(1)} %collective-permute-done.3.refs_3_, bf16[3,8,256,256]{3,2,1,0:T(8,128)(2,1)S(1)} %copy-done, ...), custom_call_target="tpu_custom_call" | custom-call | tf_op jit(solution)/shard_map/product_2/pallas_call | solution.py:303
  127.3 18.9 %all_to_all.58.refs_0_ = bf16[8,8,32,256]{3,2,1,0:T(8,128)(2,1)S(1)} all-to-all(bf16[8,8,32,256]{3,2,1,0:T(8,128)(2,1)} %product_2.1), channel_id=1, replica_groups=mesh['term'=8,'sector'=32] {'term'}, dimensions={0} | all-to-all | bytes 2097152 | tf_op jit(solution)/shard_map/all_to_all | solution.py:384
  146.2 1.2 reduce_2.1
  147.4 3.4 %collective-permute-start.4 = (f32[8,32,256]{2,1,0:T(8,128)}, f32[8,32,256]{2,1,0:T(8,128)S(1)}, u32[]{:S(2)}, u32[]{:S(2)}) collective-permute-start(f32[8,32,256]{2,1,0:T(8,128)} %get-tuple-element.30), channel_id=1, source_target_pairs={{1,2},{3,4},{5,6},{7,8},{9,10},{11,12},{13,14},{15,16},{17,18},{19... | collective-permute-start | bytes 786440 | tf_op jit(solution)/shard_map/ppermute | solution.py:20
  150.8 19.6 %all_to_all.59 = f32[256,1,128]{2,1,0:T(1,128)S(1)} all-to-all(f32[256,1,128]{2,1,0:T(1,128)S(1)} %bitcast.26), channel_id=1, replica_groups=mesh['term'=8,'sector'=32] {'term','sector'}, dimensions={0} | all-to-all | bytes 262144 | tf_op jit(solution)/shard_map/all_to_all | solution.py:398
  170.4 2.8 %update_2.1 = (f32[8,32,256]{2,1,0:T(8,128)}, f32[1,128]{1,0:T(1,128)S(1)}, bf16[8,2,8,32,256]{4,3,2,1,0:T(8,128)(2,1)}) custom-call(f32[256,128]{1,0:T(8,128)S(1)} %bitcast.17, f32[256,128]{1,0:T(8,128)S(1)} %bitcast.19, bf16[2,8,32,256]{3,2,1,0:T(8,128)(2,1)S(1)} %copy-done.6, f32[8,32,256]{2,1,0:T(8,128)S(1)} %get-tuple-element.22.refs_2_.refs_3_, ...), custom_call_target="tpu_custom_call" | custom-call | tf_op jit(solution)/shard_map/update_2/pallas_call | solution.py:340
  173.2 29.8 %all_to_all.60.refs_2_ = bf16[8,2,8,32,256]{4,3,2,1,0:T(8,128)(2,1)S(1)} all-to-all(bf16[8,2,8,32,256]{4,3,2,1,0:T(8,128)(2,1)} %get-tuple-element.32), channel_id=1, replica_groups=mesh['term'=8,'sector'=32] {'term'}, dimensions={0} | all-to-all | bytes 4194304 | tf_op jit(solution)/shard_map/all_to_all | solution.py:384
  203.0 1.9 collective-permute-start.5
  204.9 2.3 collective-permute-done.5.refs_3_
  207.2 3.1 %product_3.1 = f32[1,128]{1,0:T(1,128)S(1)} custom-call(s32[3,8]{1,0:T(4,128)S(1)} %fusion.3.refs_0_, s32[2,8]{1,0:T(2,128)S(1)} %copy-done.13, bf16[8,2,8,32,256]{4,3,2,1,0:T(8,128)(2,1)S(1)} %all_to_all.60.refs_2_, bf16[8,8,32,256]{3,2,1,0:T(8,128)(2,1)S(1)} %collective-permute-done.5.refs_3_, bf16[8,8,32,256]{3,2,1,0:T(8,128)(2,1)S(1)} %copy-done.5, ...), custom_call_target="tpu_custom_call" | custom-call | tf_op jit(solution)/shard_map/product_3/pallas_call | solution.py:303
  211.1 5.4 %all-to-all-start.7 = ((f32[256,1,128]{2,1,0:T(1,128)}), f32[256,1,128]{2,1,0:T(1,128)S(1)}, u32[]{:S(2)}, u32[]{:S(2)}) async-start(f32[256,1,128]{2,1,0:T(1,128)} %broadcast_in_dim.32), calls=%async_computation.7 | async-start | bytes 262144 | tf_op jit(solution)/shard_map/all_to_all | solution.py:15
  216.5 1.6 copy-done.3
  218.1 1.2 copy-done.9
  219.3 3.5 %product_4.1 = bf16[3,8,256,256]{3,2,1,0:T(8,128)(2,1)} custom-call(s32[3,8]{1,0:T(4,128)S(1)} %fusion.3.refs_0_, s32[2,8]{1,0:T(2,128)S(1)} %copy-done.13, bf16[8,2,8,32,256]{4,3,2,1,0:T(8,128)(2,1)S(1)} %copy-done.3, bf16[8,8,32,256]{3,2,1,0:T(8,128)(2,1)S(1)} %copy-done.9, bf16[3,8,256,256]{3,2,1,0:T(8,128)(2,1)S(1)} %copy-done), custom_call_target="tpu_custom_call" | custom-call | tf_op jit(solution)/shard_map/product_4/pallas_call | solution.py:303
  222.9 6.7 %all-to-all-done.7 = f32[256,1,128]{2,1,0:T(1,128)S(1)} async-done(((f32[256,1,128]{2,1,0:T(1,128)}), f32[256,1,128]{2,1,0:T(1,128)S(1)}, u32[]{:S(2)}, u32[]{:S(2)}) %all-to-all-start.7) | async-done | bytes 131104 | tf_op jit(solution)/shard_map/all_to_all | solution.py:15
  (39 shorter events, 2.6 us)
Async XLA Ops:
  0.6 0.7 copy-start.12
  3.6 15.6 %copy-start.7 = (bf16[8,256,256]{2,1,0:T(8,128)(2,1)S(1)}, bf16[8,256,256]{2,1,0:T(8,128)(2,1)}, u32[]{:S(2)}) copy-start(bf16[8,256,256]{2,1,0:T(8,128)(2,1)} %psi_ref.3) | copy-start | bytes 3145732
  3.6 15.6 %copy-start.13 = (s32[2,8]{1,0:T(2,128)S(1)}, s32[2,8]{1,0:T(2,128)}, u32[]{:S(2)}) copy-start(s32[2,8]{1,0:T(2,128)} %refs_1_.7) | copy-start | bytes 196
  3.6 9.0 %collective-permute-start = (bf16[2,8,32,256]{3,2,1,0:T(8,128)(2,1)}, bf16[2,8,32,256]{3,2,1,0:T(8,128)(2,1)S(1)}, u32[]{:S(2)}, u32[]{:S(2)}) collective-permute-start(bf16[2,8,32,256]{3,2,1,0:T(8,128)(2,1)} %share.1.refs_1_.refs_2_), channel_id=1, source_target_pairs={{1,2},{3,4},{5,6},{7,8},{9,10},{11,12},{13,14},{15,16},{17,18},{19... | collective-permute-start | bytes 786440 | tf_op jit(solution)/shard_map/ppermute | solution.py:20
  13.7 6.5 %copy-start.14 = (s32[3,8]{1,0:T(4,128)S(1)}, s32[3,8]{1,0:T(4,128)}, u32[]{:S(2)}) copy-start(s32[3,8]{1,0:T(4,128)} %param.9) | copy-start | bytes 292
  13.7 16.9 %all-to-all-start = ((bf16[8,8,32,256]{3,2,1,0:T(8,128)(2,1)}), bf16[8,8,32,256]{3,2,1,0:T(8,128)(2,1)S(1)}, u32[]{:S(2)}, u32[]{:S(2)}) async-start(bf16[8,8,32,256]{3,2,1,0:T(8,128)(2,1)} %broadcast_in_dim.27), calls=%async_computation | async-start | bytes 2097152 | tf_op jit(solution)/shard_map/all_to_all | solution.py:15
  20.2 15.6 %copy-start.4 = (bf16[8,8,32,256]{3,2,1,0:T(8,128)(2,1)}, bf16[8,8,32,256]{3,2,1,0:T(8,128)(2,1)S(1)}, u32[]{:S(2)}) copy-start(bf16[8,8,32,256]{3,2,1,0:T(8,128)(2,1)S(1)} %start.1.refs_3_.refs_4_) | copy-start | bytes 3145732
  20.2 2.7 %collective-permute-start.1 = (bf16[8,8,32,256]{3,2,1,0:T(8,128)(2,1)S(1)}, bf16[8,8,32,256]{3,2,1,0:T(8,128)(2,1)S(1)}, u32[]{:S(2)}, u32[]{:S(2)}) collective-permute-start(bf16[8,8,32,256]{3,2,1,0:T(8,128)(2,1)S(1)} %start.1.refs_3_.refs_4_), channel_id=1, source_target_pairs={{0,1},{2,3},{4,5},{6,7},{8,9},{10,11},{12,13},{14,15},{16,17},{18,... | collective-permute-start | bytes 3145736 | tf_op jit(solution)/shard_map/ppermute | solution.py:20
  35.8 16.2 %copy-start.6 = (bf16[2,8,32,256]{3,2,1,0:T(8,128)(2,1)S(1)}, bf16[2,8,32,256]{3,2,1,0:T(8,128)(2,1)}, u32[]{:S(2)}) copy-start(bf16[2,8,32,256]{3,2,1,0:T(8,128)(2,1)} %share.1.refs_1_.refs_2_) | copy-start | bytes 786436
  53.0 34.8 %collective-permute-start.2 = (f32[8,32,256]{2,1,0:T(8,128)}, f32[8,32,256]{2,1,0:T(8,128)S(1)}, u32[]{:S(2)}, u32[]{:S(2)}) collective-permute-start(f32[8,32,256]{2,1,0:T(8,128)} %get-tuple-element.23), channel_id=1, source_target_pairs={{1,2},{3,4},{5,6},{7,8},{9,10},{11,12},{13,14},{15,16},{17,18},{19... | collective-permute-start | bytes 786440 | tf_op jit(solution)/shard_map/ppermute | solution.py:20
  89.6 34.3 %copy-start = (bf16[3,8,256,256]{3,2,1,0:T(8,128)(2,1)S(1)}, bf16[3,8,256,256]{3,2,1,0:T(8,128)(2,1)}, u32[]{:S(2)}) copy-start(bf16[3,8,256,256]{3,2,1,0:T(8,128)(2,1)} %refs_4_.3) | copy-start | bytes 9437188
  89.6 34.3 %copy-start.1 = (bf16[3,8,256,256]{3,2,1,0:T(8,128)(2,1)S(1)}, bf16[3,8,256,256]{3,2,1,0:T(8,128)(2,1)}, u32[]{:S(2)}) copy-start(bf16[3,8,256,256]{3,2,1,0:T(8,128)(2,1)} %refs_8_.1) | copy-start | bytes 9437188
  119.8 4.0 %collective-permute-start.3 = (bf16[8,8,32,256]{3,2,1,0:T(8,128)(2,1)S(1)}, bf16[8,8,32,256]{3,2,1,0:T(8,128)(2,1)S(1)}, u32[]{:S(2)}, u32[]{:S(2)}) collective-permute-start(bf16[8,8,32,256]{3,2,1,0:T(8,128)(2,1)S(1)} %slice_bitcast_fusion.1), channel_id=1, source_target_pairs={{0,1},{2,3},{4,5},{6,7},{8,9},{10,11},{12,13},{14,15},{16,17},{18,... | collective-permute-start | bytes 3145736 | tf_op jit(solution)/shard_map/ppermute | solution.py:20
  147.4 23.0 %collective-permute-start.4 = (f32[8,32,256]{2,1,0:T(8,128)}, f32[8,32,256]{2,1,0:T(8,128)S(1)}, u32[]{:S(2)}, u32[]{:S(2)}) collective-permute-start(f32[8,32,256]{2,1,0:T(8,128)} %get-tuple-element.30), channel_id=1, source_target_pairs={{1,2},{3,4},{5,6},{7,8},{9,10},{11,12},{13,14},{15,16},{17,18},{19... | collective-permute-start | bytes 786440 | tf_op jit(solution)/shard_map/ppermute | solution.py:20
  170.4 2.8 %copy-start.10 = (f32[256,1,128]{2,1,0:T(1,128)}, f32[256,1,128]{2,1,0:T(1,128)S(1)}, u32[]{:S(2)}) copy-start(f32[256,1,128]{2,1,0:T(1,128)S(1)} %all_to_all.59) | copy-start | bytes 393220
  202.9 7.4 %copy-start.2 = (bf16[8,2,8,32,256]{4,3,2,1,0:T(8,128)(2,1)}, bf16[8,2,8,32,256]{4,3,2,1,0:T(8,128)(2,1)S(1)}, u32[]{:S(2)}) copy-start(bf16[8,2,8,32,256]{4,3,2,1,0:T(8,128)(2,1)S(1)} %all_to_all.60.refs_2_) | copy-start | bytes 6291460
  202.9 4.3 %copy-start.5 = (bf16[8,8,32,256]{3,2,1,0:T(8,128)(2,1)S(1)}, bf16[8,8,32,256]{3,2,1,0:T(8,128)(2,1)}, u32[]{:S(2)}) copy-start(bf16[8,8,32,256]{3,2,1,0:T(8,128)(2,1)} %copy-done.4) | copy-start | bytes 3145732
  203.0 4.2 %collective-permute-start.5 = (bf16[8,8,32,256]{3,2,1,0:T(8,128)(2,1)S(1)}, bf16[8,8,32,256]{3,2,1,0:T(8,128)(2,1)S(1)}, u32[]{:S(2)}, u32[]{:S(2)}) collective-permute-start(bf16[8,8,32,256]{3,2,1,0:T(8,128)(2,1)S(1)} %slice_bitcast_fusion), channel_id=1, source_target_pairs={{0,1},{2,3},{4,5},{6,7},{8,9},{10,11},{12,13},{14,15},{16,17},{18,... | collective-permute-start | bytes 3145736 | tf_op jit(solution)/shard_map/ppermute | solution.py:20
  207.2 3.1 %copy-start.8 = (bf16[8,8,32,256]{3,2,1,0:T(8,128)(2,1)}, bf16[8,8,32,256]{3,2,1,0:T(8,128)(2,1)S(1)}, u32[]{:S(2)}) copy-start(bf16[8,8,32,256]{3,2,1,0:T(8,128)(2,1)S(1)} %collective-permute-done.5.refs_3_) | copy-start | bytes 3145732
  211.1 18.5 %all-to-all-start.7 = ((f32[256,1,128]{2,1,0:T(1,128)}), f32[256,1,128]{2,1,0:T(1,128)S(1)}, u32[]{:S(2)}, u32[]{:S(2)}) async-start(f32[256,1,128]{2,1,0:T(1,128)} %broadcast_in_dim.32), calls=%async_computation.7 | async-start | bytes 262144 | tf_op jit(solution)/shard_map/all_to_all | solution.py:15
  216.5 1.6 copy-start.3
  218.1 1.2 copy-start.9
  219.3 10.2 %copy-start.11 = (f32[256,1,128]{2,1,0:T(1,128)S(1)}, f32[256,1,128]{2,1,0:T(1,128)}, u32[]{:S(2)}) copy-start(f32[256,1,128]{2,1,0:T(1,128)} %copy-done.10) | copy-start | bytes 393220
